TPU v7x, 32 devices: a whole 2x2x4 slice. The times are simulated.
32 devices in a mesh: lon: 16 (over z, x, core), lat: 2 (over y).
Axes of the slice: x: 2, y: 2, z: 4, core: 2. Of those that a mesh axis runs over, the one named last changes fastest.
Arguments:
- fields: bfloat16 [64, 1792, 256], P('lat', 'lon'), may hold values from -6 to 6
- cotangent: bfloat16 [64, 1792, 256], P('lat', 'lon'), may hold values from -6 to 6
- kernel: float32 [31, 256], replicated, may hold values from -1 to 1
- up_weight: bfloat16 [256, 1024], replicated, may hold values from -0.375 to 0.375
- down_weight: bfloat16 [1024, 256], replicated, may hold values from -0.1875 to 0.1875
Outputs:
- output: bfloat16 [64, 1792, 256], P('lat', 'lon')
- field_grad: bfloat16 [64, 1792, 256], P('lat', 'lon')
- kernel_grad: float32 [31, 256], replicated
- up_grad: float32 [256, 1024], replicated
- down_grad: float32 [1024, 256], replicated
All inputs are finite; a program needn't handle non-finite values.
Results may differ from a plain program's by a relative error of at most 0.0055.
Values may be sent and summed in bfloat16 or wider, within the bound.
No kernel may reach another device: no remote copies, remote signals or barrier semaphores. Data moves between devices by JAX's collectives and lax.ppermute only.
A program may use at most 128 MiB of HBM per device.

v0:
```python
import math

import jax
import jax.numpy as jnp
from jax import lax
from jax.sharding import PartitionSpec as P

KERNEL_SPACING = 4


def passed_along(value, axis, by):
    count = lax.axis_size(axis)
    return lax.ppermute(value, axis, [(i, (i + by) % count) for i in range(count)])


def gelu_tanh(values):
    return jax.nn.gelu(values, approximate=True)


def per_device(fields, cotangent, kernel, up_weight, down_weight):
    rows, column_list, channels = fields.shape
    taps = kernel.shape[0]
    taps_half_span = taps // 2
    border_extent = KERNEL_SPACING * taps_half_span
    blocks_out = -(-border_extent // column_list)
    sides = []
    for direction in (1, -1):
        current = fields
        current = passed_along(current, "lon", direction)
        passed = [current]
        sides.append(passed)
    whole = jnp.concatenate(sides[0][::-1] + [fields] + sides[1], axis=1)
    first = blocks_out * column_list - border_extent
    wrapped_input = whole[:, first : first + column_list + 2 * border_extent]
    conv = jnp.zeros((rows, column_list, channels), jnp.float32)
    for index_of_tap in range(taps):
        tap_window = wrapped_input[
            :, KERNEL_SPACING * index_of_tap : KERNEL_SPACING * index_of_tap + column_list
        ].astype(jnp.float32)
        conv = conv + kernel[index_of_tap] * tap_window
    conv = conv.reshape(rows * column_list, channels)
    center = jnp.mean(conv, axis=-1, keepdims=True)
    deviation = conv - center
    spread = jnp.mean(deviation * deviation, axis=-1, keepdims=True)
    inv_scale = lax.rsqrt(spread + 1e-06)
    normed = deviation * inv_scale
    normed_low = normed.astype(jnp.bfloat16)
    hidden = jnp.dot(normed_low, up_weight, preferred_element_type=jnp.float32)
    activated, pullback = jax.vjp(gelu_tanh, hidden)
    activated_low = activated.astype(jnp.bfloat16)
    flat_in = fields.reshape(rows * column_list, channels)
    flat_cot = cotangent.reshape(rows * column_list, channels)
    output = (
        flat_in.astype(jnp.float32)
        + jnp.dot(activated_low, down_weight, preferred_element_type=jnp.float32)
    ).astype(jnp.bfloat16)
    output = output.reshape(rows, column_list, channels)
    contract_last = (((1,), (1,)), ((), ()))
    contract_first = (((0,), (0,)), ((), ()))
    upstream = lax.dot_general(
        flat_cot, down_weight, contract_last, preferred_element_type=jnp.float32
    )
    hidden_grad = pullback(upstream)[0].astype(jnp.bfloat16)
    normed_grad = lax.dot_general(
        hidden_grad, up_weight, contract_last, preferred_element_type=jnp.float32
    )
    mean_grad = jnp.mean(normed_grad, axis=-1, keepdims=True)
    mean_cross = jnp.mean(normed_grad * normed, axis=-1, keepdims=True)
    conv_grad = (inv_scale * (normed_grad - mean_grad - normed * mean_cross)).reshape(
        rows, column_list, channels
    )
    layout = [(1, max(0, column_list - border_extent), column_list)]
    layout = layout + [(-1, 0, min(column_list, column_list + border_extent - column_list))]
    pieces = [
        passed_along(conv_grad[:, lower:upper].astype(jnp.bfloat16), "lon", moved).astype(
            jnp.float32
        )
        for moved, lower, upper in layout
    ]
    grad_padded = jnp.concatenate(pieces[:blocks_out] + [conv_grad] + pieces[blocks_out:], axis=1)
    conv_back = jnp.zeros((rows, column_list, channels), jnp.float32)
    for index_of_tap in range(taps):
        window_start = KERNEL_SPACING * (2 * taps_half_span - index_of_tap)
        conv_back = (
            conv_back
            + kernel[index_of_tap] * grad_padded[:, window_start : window_start + column_list]
        )
    field_grad = (cotangent.astype(jnp.float32) + conv_back).astype(jnp.bfloat16)
    kernel_terms = jnp.stack(
        [
            jnp.sum(
                wrapped_input[
                    :, KERNEL_SPACING * index_of_tap : KERNEL_SPACING * index_of_tap + column_list
                ].astype(jnp.float32)
                * conv_grad,
                axis=(0, 1),
            )
            for index_of_tap in range(taps)
        ]
    )
    grad_up = lax.dot_general(
        normed_low, hidden_grad, contract_first, preferred_element_type=jnp.float32
    )
    grad_down = lax.dot_general(
        activated_low, flat_cot, contract_first, preferred_element_type=jnp.float32
    )
    summed = lax.psum((kernel_terms, grad_up, grad_down), ("lon", "lat"))
    factor = 1.0 / math.sqrt(rows * column_list * lax.axis_size("lon") * lax.axis_size("lat"))
    return (output, field_grad, summed[0] * factor, summed[1] * factor, summed[2] * factor)


def solution(mesh):
    placed = (P("lat", "lon", None), P("lat", "lon", None), P(), P(), P())
    return jax.shard_map(
        per_device,
        mesh=mesh,
        in_specs=placed,
        out_specs=(P("lat", "lon", None), P("lat", "lon", None), P(), P(), P()),
        check_vma=False,
    )
```

profile of v0, /device:TPU:0, one launch (start us, length us, event | category | flops | bytes accessed | tf_op | source)
XLA Modules:
  0.0 282.3 jit_solution(12317122125374097740)
XLA Ops:
  7.2 0.0 copy-start
  7.2 0.0 copy-start.8
  7.2 0.0 all-reduce.3.cloned.1.call-start
  7.2 0.5 collective-permute-start
  7.7 5.0 %collective-permute-start.1 = (bf16[32,112,256]{2,1,0:T(8,128)(2,1)}, bf16[32,112,256]{2,1,0:T(8,128)(2,1)S(1)}, u32[]{:S(2)}, u32[]{:S(2)}) collective-permute-start(bf16[32,112,256]{2,1,0:T(8,128)(2,1)} %param.5), channel_id=1, source_target_pairs={{0,30},{2,0},{4,2},{6,4},{8,6},{10,8},{12,10},{14,12},{16,14},{18,... | collective-permute-start | bytes 5505032 | tf_op jit(solution)/shard_map/ppermute | solution.py:13
  12.8 1.0 fusion.165
  13.7 1.0 fusion.164
  14.8 19.2 %collective-permute-done = bf16[32,112,256]{2,1,0:T(8,128)(2,1)S(1)} collective-permute-done((bf16[32,112,256]{2,1,0:T(8,128)(2,1)}, bf16[32,112,256]{2,1,0:T(8,128)(2,1)S(1)}, u32[]{:S(2)}, u32[]{:S(2)}) %collective-permute-start) | collective-permute-done | bytes 1835040 | tf_op jit(solution)/shard_map/ppermute | solution.py:13
  33.9 0.2 constant_dynamic-update-slice_fusion.1
  34.2 0.0 copy-done.8
  34.2 0.3 constant_dynamic-update-slice_fusion
  34.5 0.0 copy-start.3
  34.5 0.0 collective-permute-done.1
  34.5 0.2 constant_dynamic-update-slice_fusion.2
  34.7 0.0 copy-start.1
  34.8 16.6 %fusion.161 = (f32[32,112]{1,0:T(8,128)S(1)}, f32[32,112,256]{2,1,0:T(8,128)}) fusion(bf16[32,224,256]{2,1,0:T(8,128)(2,1)S(1)} %constant_dynamic-update-slice_fusion.2, f32[256]{0:T(256)S(1)} %bitcast.116, f32[256]{0:T(256)S(1)} %bitcast.118, f32[256]{0:T(256)S(1)} %bitcast.122, f32[256]{0:T(256)S(1)} %bitcast.124, f32[256]{0:T(256)S(1)} %bitcast.126, ...), kind=kLoop, calls=%fused_computation.300 | loop fusion | flops 85324288 | bytes 60601344 | tf_op jit(solution)/shard_map/reduce_sum | solution.py:42
  51.3 0.0 copy-done.3
  51.3 0.0 copy-done.1
  51.4 0.1 div.15
  51.4 2.7 multiply_reduce_fusion.2
  54.2 0.1 rsqrt.12
  54.3 3.4 %fusion.159 = bf16[3584,256]{1,0:T(8,128)(2,1)S(1)} fusion(f32[32,112,256]{2,1,0:T(8,128)} %get-tuple-element.41, f32[3584]{0:T(1024)S(1)} %rsqrt.12, f32[3584]{0:T(1024)S(1)} %div.15), kind=kLoop, calls=%fused_computation.287 | loop fusion | flops 2752512 | bytes 5533696 | tf_op jit(solution)/shard_map/convert_element_type | solution.py:47
  57.7 0.0 copy-done
  57.7 0.0 copy-start.11
  57.7 7.9 %multiply_convert_fusion = (bf16[3584,1024]{1,0:T(8,128)(2,1)S(1)}, f32[3584,1024]{1,0:T(8,128)}) fusion(bf16[3584,256]{1,0:T(8,128)(2,1)S(1)} %fusion.159, bf16[256,1024]{1,0:T(8,128)(2,1)S(1)} %copy-done), kind=kOutput, calls=%fused_computation.65 | convolution fusion | flops 1912078336 | bytes 24379392 | tf_op jit(solution)/shard_map/dot_general | solution.py:48
  65.6 0.0 copy-start.9
  65.6 0.0 copy-done.11
  65.6 0.0 copy-start.7
  65.6 15.9 %fusion.6 = bf16[3584,1024]{1,0:T(8,128)(2,1)S(1)} fusion(f32[3584,1024]{1,0:T(8,128)} %get-tuple-element.78, bf16[3584,256]{1,0:T(8,128)(2,1)} %bitcast.94, bf16[1024,256]{1,0:T(8,128)(2,1)S(1)} %copy-done.11), kind=kOutput, calls=%fused_computation.64 | convolution fusion | flops 1952448512 | bytes 24379392 | tf_op jit(solution)/shard_map/dot_general | solution.py:60
  81.5 0.0 copy-done.7
  81.5 2.5 fusion.160
  84.0 0.0 copy-start.4
  84.0 2.7 subtract_multiply_fusion
  86.7 0.0 copy-start.5
  86.7 0.0 copy-done.4
  86.7 0.0 copy-start.2
  86.7 9.4 %fusion.47 = (f32[256]{0:T(256)}, f32[256]{0:T(256)}, f32[256]{0:T(256)}, f32[256]{0:T(256)}, f32[256]{0:T(256)}, /*index=5*/f32[256]{0:T(256)}, f32[256]{0:T(25...) fusion(f32[32,112,256]{2,1,0:T(8,128)S(1)} %bitcast.89, ...), kind=kLoop, calls=%fused_computation.167 | loop fusion | flops 41283840 | bytes 31210496 | tf_op jit(solution)/shard_map/reduce_sum | solution.py:91
  96.1 0.0 copy-done.2
  96.1 9.5 %fusion.67 = (f32[256]{0:T(256)S(1)}, f32[256]{0:T(256)S(1)}, f32[256]{0:T(256)S(1)}, f32[256]{0:T(256)S(1)}, f32[256]{0:T(256)S(1)}, /*index=5*/f32[256]{0:T(25...) fusion(f32[32,112,256]{2,1,0:T(8,128)S(1)} %bitcast.90, ...), kind=kLoop, calls=%fused_computation.187 | loop fusion | flops 44036096 | bytes 33046528 | tf_op jit(solution)/shard_map/reduce_sum | solution.py:91
  105.7 0.0 copy-done.5
  105.7 0.0 copy-start.10
  105.7 2.0 copy.14
  107.6 0.0 copy-done.9
  107.6 0.0 copy-done.10
  107.6 3.1 %fusion.167 = f32[1024,256]{1,0:T(8,128)} fusion(bf16[3584,1024]{1,0:T(8,128)(2,1)S(1)} %get-tuple-element.77, bf16[3584,256]{1,0:T(8,128)(2,1)S(1)} %bitcast.95), kind=kOutput, calls=%fused_computation.305 | convolution fusion | flops 1879048192 | bytes 10223616 | tf_op jit(solution)/shard_map/dot_general | solution.py:104
  110.7 1.5 fusion.163
  112.2 3.9 %collective-permute-start.2 = (bf16[32,60,256]{2,0,1:T(8,128)(2,1)}, bf16[32,60,256]{2,0,1:T(8,128)(2,1)S(1)}, u32[]{:S(2)}, u32[]{:S(2)}) collective-permute-start(bf16[32,60,256]{2,0,1:T(8,128)(2,1)} %get-tuple-element.42), channel_id=1, source_target_pairs={{0,30},{2,0},{4,2},{6,4},{8,6},{10,8},{12,10},{14,12},{16,14},{18,... | collective-permute-start | bytes 2949128 | tf_op jit(solution)/shard_map/ppermute | solution.py:13
  116.1 14.4 %collective-permute-start.3 = (bf16[32,60,256]{2,0,1:T(8,128)(2,1)}, bf16[32,60,256]{2,0,1:T(8,128)(2,1)}, u32[]{:S(2)}, u32[]{:S(2)}) collective-permute-start(bf16[32,60,256]{2,0,1:T(8,128)(2,1)} %get-tuple-element.43), channel_id=1, source_target_pairs={{0,2},{2,4},{4,6},{6,8},{8,10},{10,12},{12,14},{14,16},{16,18},{18... | collective-permute-start | bytes 2949128 | tf_op jit(solution)/shard_map/ppermute | solution.py:13
  130.6 3.0 %fusion.166 = f32[256,1024]{1,0:T(8,128)} fusion(bf16[3584,256]{1,0:T(8,128)(2,1)S(1)} %fusion.159, bf16[3584,1024]{1,0:T(8,128)(2,1)S(1)} %fusion.6), kind=kOutput, calls=%fused_computation.304 | convolution fusion | flops 1879048192 | bytes 10223616 | tf_op jit(solution)/shard_map/dot_general | solution.py:101
  133.6 0.0 all-reduce.3.cloned.1.call-update
  133.6 2.8 %stack.127 = f32[31,256]{1,0:T(8,128)S(1)} concatenate(f32[1,256]{1,0:T(1,128)} %bitcast.188, f32[1,256]{1,0:T(1,128)} %bitcast.187, f32[1,256]{1,0:T(1,128)} %bitcast.186, f32[1,256]{1,0:T(1,128)} %bitcast.185, f32[1,256]{1,0:T(1,128)} %bitcast.184, f32[1,256]{1,0:T(1,128)} %bitcast.183, f32[1,256]{1,0:T(1,128)} %bitcast.182, f32[1,256]{1,0:T(1,128)} %bitcast.181, ...), dimensions={0} | concatenate | bytes 63488 | tf_op jit(solution)/shard_map/stack | solution.py:89
  136.5 56.0 %psum.21 = f32[31,256]{1,0:T(8,128)S(1)} all-reduce(f32[31,256]{1,0:T(8,128)S(1)} %stack.127), channel_id=1, replica_groups=mesh['lon'=16,'lat'=2] {'lon','lat'}, use_global_device_ids=true, to_apply=%region_35.0 | all-reduce | flops 7936 | bytes 63488 | tf_op jit(solution)/shard_map/psum | solution.py:107
  192.5 0.6 broadcast_multiply_fusion.2
  193.1 6.5 %fusion.7 = bf16[3584,256]{1,0:T(8,128)(2,1)} fusion(bf16[3584,1024]{1,0:T(8,128)(2,1)} %copy-done.9, bf16[1024,256]{1,0:T(8,128)(2,1)} %param.9, bf16[3584,256]{1,0:T(8,128)(2,1)S(1)} %bitcast.93), kind=kOutput, calls=%fused_computation.67 | convolution fusion | flops 1881800704 | bytes 11534336 | tf_op jit(solution)/shard_map/dot_general | solution.py:55
  199.6 0.0 copy-start.6
  199.6 0.0 collective-permute-done.3
  199.6 1.9 copy.12
  201.5 0.0 collective-permute-done.2
  201.5 0.6 copy.11
  202.1 0.0 copy-done.6
  202.1 22.8 %fusion.73 = bf16[32,112,256]{2,1,0:T(8,128)(2,1)} fusion(f32[32,112,256]{2,1,0:T(8,128)S(1)} %bitcast.92, f32[32,60,256]{2,1,0:T(8,128)S(1)} %copy.12, f32[32,60,256]{2,1,0:T(8,128)S(1)} %copy.11, bf16[32,112,256]{2,1,0:T(8,128)(2,1)} %param.6, f32[256]{0:T(256)S(1)} %bitcast.117, f32[256]{0:T(256)S(1)} %bitcast.119, f32[256]{0:T(256)S(1)} %bitcast.123, ...), kind=kLoop, calls=%fused_computation.193 | loop fusion | flops 86245376 | bytes 11303936 | tf_op jit(solution)/shard_map/convert_element_type | solution.py:88
  224.9 45.9 %all-reduce.3.cloned.1.call-done = (f32[256,1024]{1,0:T(8,128)}, f32[1024,256]{1,0:T(8,128)}) async-done(((f32[256,1024]{1,0:T(8,128)}, f32[1024,256]{1,0:T(8,128)}), (f32[256,1024]{1,0:T(8,128)}, f32[1024,256]{1,0:T(8,128)})) %all-reduce.3.cloned.1.call-update) | async-done | bytes 2097168 | tf_op jit(solution)/shard_map/psum | solution.py:107
  270.8 2.3 broadcast_multiply_fusion.1
  273.2 2.3 broadcast_multiply_fusion
  (3 shorter events, 0.0 us)
Async XLA Ops:
  7.2 50.5 %copy-start = (bf16[256,1024]{1,0:T(8,128)(2,1)S(1)}, bf16[256,1024]{1,0:T(8,128)(2,1)}, u32[]{:S(2)}) copy-start(bf16[256,1024]{1,0:T(8,128)(2,1)} %param.8) | copy-start | bytes 1572868
  7.2 27.0 %copy-start.8 = (bf16[32,112,256]{2,1,0:T(8,128)(2,1)S(1)}, bf16[32,112,256]{2,1,0:T(8,128)(2,1)}, u32[]{:S(2)}) copy-start(bf16[32,112,256]{2,1,0:T(8,128)(2,1)} %param.5) | copy-start | bytes 5505028
  7.2 263.6 %all-reduce.3.cloned.1.call-start = ((), (), s32[]{:S(2)}) async-start(), calls=%async_computation | async-start | bytes 4194304 | tf_op jit(solution)/shard_map/psum | solution.py:107
  7.2 26.7 %collective-permute-start = (bf16[32,112,256]{2,1,0:T(8,128)(2,1)}, bf16[32,112,256]{2,1,0:T(8,128)(2,1)S(1)}, u32[]{:S(2)}, u32[]{:S(2)}) collective-permute-start(bf16[32,112,256]{2,1,0:T(8,128)(2,1)} %param.5), channel_id=1, source_target_pairs={{0,2},{2,4},{4,6},{6,8},{8,10},{10,12},{12,14},{14,16},{16,18},{18... | collective-permute-start | bytes 5505032 | tf_op jit(solution)/shard_map/ppermute | solution.py:13
  7.7 26.8 %collective-permute-start.1 = (bf16[32,112,256]{2,1,0:T(8,128)(2,1)}, bf16[32,112,256]{2,1,0:T(8,128)(2,1)S(1)}, u32[]{:S(2)}, u32[]{:S(2)}) collective-permute-start(bf16[32,112,256]{2,1,0:T(8,128)(2,1)} %param.5), channel_id=1, source_target_pairs={{0,30},{2,0},{4,2},{6,4},{8,6},{10,8},{12,10},{14,12},{16,14},{18,... | collective-permute-start | bytes 5505032 | tf_op jit(solution)/shard_map/ppermute | solution.py:13
  34.5 16.9 %copy-start.3 = (bf16[32,224,256]{2,1,0:T(8,128)(2,1)}, bf16[32,224,256]{2,1,0:T(8,128)(2,1)S(1)}, u32[]{:S(2)}) copy-start(bf16[32,224,256]{2,1,0:T(8,128)(2,1)S(1)} %get-tuple-element.44) | copy-start | bytes 11010052
  34.7 16.6 %copy-start.1 = (bf16[32,224,256]{2,1,0:T(8,128)(2,1)}, bf16[32,224,256]{2,1,0:T(8,128)(2,1)S(1)}, u32[]{:S(2)}) copy-start(bf16[32,224,256]{2,1,0:T(8,128)(2,1)S(1)} %constant_dynamic-update-slice_fusion.2) | copy-start | bytes 11010052
  57.7 7.9 %copy-start.11 = (bf16[1024,256]{1,0:T(8,128)(2,1)S(1)}, bf16[1024,256]{1,0:T(8,128)(2,1)}, u32[]{:S(2)}) copy-start(bf16[1024,256]{1,0:T(8,128)(2,1)} %param.9) | copy-start | bytes 1572868
  65.6 42.0 %copy-start.9 = (bf16[3584,1024]{1,0:T(8,128)(2,1)}, bf16[3584,1024]{1,0:T(8,128)(2,1)S(1)}, u32[]{:S(2)}) copy-start(bf16[3584,1024]{1,0:T(8,128)(2,1)S(1)} %get-tuple-element.77) | copy-start | bytes 22020100
  65.6 15.9 %copy-start.7 = (f32[32,112,256]{2,1,0:T(8,128)S(1)}, f32[32,112,256]{2,1,0:T(8,128)}, u32[]{:S(2)}) copy-start(f32[32,112,256]{2,1,0:T(8,128)} %get-tuple-element.41) | copy-start | bytes 11010052
  84.0 2.7 copy-start.4
  86.7 19.0 %copy-start.5 = (f32[3584,256]{1,0:T(8,128)}, f32[3584,256]{1,0:T(8,128)S(1)}, u32[]{:S(2)}) copy-start(f32[3584,256]{1,0:T(8,128)S(1)} %subtract_multiply_fusion) | copy-start | bytes 11010052
  86.7 9.4 %copy-start.2 = (bf16[32,224,256]{2,1,0:T(8,128)(2,1)S(1)}, bf16[32,224,256]{2,1,0:T(8,128)(2,1)}, u32[]{:S(2)}) copy-start(bf16[32,224,256]{2,1,0:T(8,128)(2,1)} %copy-done.1) | copy-start | bytes 11010052
  105.7 2.0 copy-start.10
  112.2 89.3 %collective-permute-start.2 = (bf16[32,60,256]{2,0,1:T(8,128)(2,1)}, bf16[32,60,256]{2,0,1:T(8,128)(2,1)S(1)}, u32[]{:S(2)}, u32[]{:S(2)}) collective-permute-start(bf16[32,60,256]{2,0,1:T(8,128)(2,1)} %get-tuple-element.42), channel_id=1, source_target_pairs={{0,30},{2,0},{4,2},{6,4},{8,6},{10,8},{12,10},{14,12},{16,14},{18,... | collective-permute-start | bytes 2949128 | tf_op jit(solution)/shard_map/ppermute | solution.py:13
  116.1 83.5 %collective-permute-start.3 = (bf16[32,60,256]{2,0,1:T(8,128)(2,1)}, bf16[32,60,256]{2,0,1:T(8,128)(2,1)}, u32[]{:S(2)}, u32[]{:S(2)}) collective-permute-start(bf16[32,60,256]{2,0,1:T(8,128)(2,1)} %get-tuple-element.43), channel_id=1, source_target_pairs={{0,2},{2,4},{4,6},{6,8},{8,10},{10,12},{12,14},{14,16},{16,18},{18... | collective-permute-start | bytes 2949128 | tf_op jit(solution)/shard_map/ppermute | solution.py:13
  199.6 2.5 copy-start.6
Sparse Core Ops, SparseCore 0:
  133.7 137.0 all-reduce.2
where the time goes:
time: 283 us; the launch traced here: 282 us
  other arithmetic  72.4 us (26%)
  waiting for transfers between devices  65.1 us (23%)
  blocking collectives  56 us (20%)
  matrix products  38.9 us (14%)
  starting transfers between devices  23.9 us (8%)
  between operations  14.3 us (5%)
  local copies, waits for them, and re-layouts  11.7 us (4%)
    psum x1, blocking collectives, per_device(): summed = lax.psum((kernel_terms, grad_up, grad_down), ('lon', 'lat'))  56 us
    psum x1, waiting for transfers between devices, per_device(): summed = lax.psum((kernel_terms, grad_up, grad_down), ('lon', 'lat'))  45.9 us
    ppermute x4, starting transfers between devices, passed_along(): lax.ppermute(value, axis, [(i, (i + by) % count) for i in range(count)])  23.9 us
    convert_element_type x1, other arithmetic, per_device(): (cotangent.astype(jnp.float32) + conv_back).astype(jnp.bfloat16)  22.8 us
    ppermute x4, waiting for transfers between devices, passed_along(): lax.ppermute(value, axis, [(i, (i + by) % count) for i in range(count)])  19.2 us
    reduce_sum x2, other arithmetic, per_device(): jnp.sum(wrapped_input[:, KERNEL_SPACING * index_of_tap:KERNEL_SPACING * i...  18.9 us
    reduce_sum x1, other arithmetic, per_device(): center = jnp.mean(conv, axis=-1, keepdims=True)  16.6 us
    dot_general x1, matrix products, per_device(): lax.dot_general(flat_cot, down_weight, contract_last, preferred_element_t...  15.9 us
  transfers between devices with their start and end apart: 5, of which 2 were waited for; matrix products, arithmetic and copies ran while one was open for 14% of the time, Pallas kernels for 0%

commit v1 on v0

v1 whole, which is shorter than its diff:
```python
import functools
import math

import jax
import jax.numpy as jnp
from jax import lax
from jax.experimental import pallas as pl
from jax.experimental.pallas import tpu as pltpu
from jax.sharding import PartitionSpec as P

KERNEL_SPACING = 4
AXES = ("lon", "lat")
F32 = jnp.float32
BF16 = jnp.bfloat16
GELU_A = math.sqrt(2.0 / math.pi)
GELU_B = GELU_A * 0.044715


def xor_permute(value, mask):
    nlon, nlat = lax.axis_size("lon"), lax.axis_size("lat")
    lat_mask, lon_mask = mask
    pairs = [
        (lon * nlat + lat, (lon ^ lon_mask) * nlat + (lat ^ lat_mask))
        for lon in range(nlon)
        for lat in range(nlat)
    ]
    return lax.ppermute(value, AXES, pairs)


def passed_along(value, by):
    count = lax.axis_size("lon")
    return lax.ppermute(value, "lon", [(i, (i + by) % count) for i in range(count)])


def groups():
    nlon, nlat = lax.axis_size("lon"), lax.axis_size("lat")
    lon, lat = lax.axis_index("lon"), lax.axis_index("lat")
    core = (2, lon % 2, [(0, s) for s in range(2)])
    plane = (2 * nlat, lat * 2 + (lon // 2) % 2, [(s >> 1, (s & 1) * 2) for s in range(2 * nlat)])
    depth = (nlon // 4, lon // 4, [(0, s * 4) for s in range(nlon // 4)])
    return core, plane, depth


def scatter_stage(value, group):
    size, own, masks = group
    parts = value.reshape(size, value.shape[0] // size, value.shape[1])
    sends = [
        lax.dynamic_index_in_dim(parts, own ^ s, 0, keepdims=False).astype(BF16)
        for s in range(1, size)
    ]
    total = lax.dynamic_index_in_dim(parts, own, 0, keepdims=False)
    for s in range(1, size):
        total = total + xor_permute(sends[s - 1], masks[s]).astype(F32)
    return total


def gather_stage(value, extra, group):
    size, own, masks = group
    rows = value.shape[0]
    packed = jnp.concatenate([value, extra.astype(BF16)], axis=0)
    got = [value]
    for s in range(1, size):
        part = xor_permute(packed, masks[s])
        got.append(part[:rows])
        extra = extra + part[rows:].astype(F32)
    whole = jnp.zeros((size,) + value.shape, value.dtype)
    for s in range(size):
        whole = lax.dynamic_update_index_in_dim(whole, got[s], own ^ s, 0)
    return whole.reshape(size * rows, value.shape[1]), extra


def stage_row(s0, s4, left, middle, right):
    edge, cols = left.shape[0], middle.shape[0]
    left, middle, right = left.astype(F32), middle.astype(F32), right.astype(F32)
    s0[pl.ds(0, edge), :] = left
    s0[pl.ds(edge, cols), :] = middle
    s0[pl.ds(edge + cols, edge), :] = right
    s4[pl.ds(0, edge - 4), :] = left[4:]
    s4[pl.ds(edge - 4, cols), :] = middle
    s4[pl.ds(edge - 4 + cols, edge), :] = right


def spread_taps(kb, kernel_ref, taps, flip):
    for t in range(taps):
        row = kernel_ref[pl.ds(taps - 1 - t if flip else t, 1), :]
        kb[t] = jnp.broadcast_to(row, kb.shape[1:])


def conv_lane(s0, s4, kb, lane, cols, taps):
    blocks = cols // 8
    lanes = pl.ds(lane * 128, 128)
    acc = [None] * blocks
    weights = [kb[t, :, lanes] for t in range(taps)]
    for i in range(blocks + taps // 2):
        for half, ref in ((0, s0), (1, s4)):
            uses = [(j, 2 * (i - j) + half) for j in range(blocks) if 0 <= 2 * (i - j) + half < taps]
            if not uses:
                continue
            x = ref[pl.ds(8 * i, 8), lanes]
            for j, t in uses:
                term = weights[t] * x
                acc[j] = term if acc[j] is None else acc[j] + term
    return acc


def forward_kernel(
    fields_ref, left_ref, right_ref, cot_ref, kernel_ref, up_ref, upt_ref, down_ref, downt_ref,
    out_ref, grad_ref, edge_left_ref, edge_right_ref, gup_ref, gdown_ref,
    s0, s4, kb, conv_s, normed_s, gdt_s,
):
    step = pl.program_id(0)
    rows, cols, channels = fields_ref.shape
    edge = left_ref.shape[1]
    taps = kernel_ref.shape[0]
    hidden_size = up_ref.shape[1]
    cells = rows * cols
    width = 256

    @pl.when(step == 0)
    def _():
        spread_taps(kb, kernel_ref, taps, False)
        gup_ref[...] = jnp.zeros_like(gup_ref)
        gdt_s[...] = jnp.zeros_like(gdt_s)

    def one_row(r, carry):
        stage_row(s0, s4, left_ref[r], fields_ref[r], right_ref[r])
        for lane in range(channels // 128):
            acc = conv_lane(s0, s4, kb, lane, cols, taps)
            for j, value in enumerate(acc):
                conv_s[r, pl.ds(8 * j, 8), pl.ds(lane * 128, 128)] = value
        return carry

    lax.fori_loop(0, rows, one_row, 0)

    conv = conv_s[...].reshape(cells, channels)
    center = jnp.mean(conv, axis=-1, keepdims=True)
    deviation = conv - center
    spread = jnp.mean(deviation * deviation, axis=-1, keepdims=True)
    inv_scale = lax.rsqrt(spread + 1e-06)
    normed = deviation * inv_scale
    normed_s[...] = normed
    low = normed.astype(BF16)
    cot = cot_ref[...].reshape(cells, channels)
    first = (((0,), (0,)), ((), ()))
    out = fields_ref[...].reshape(cells, channels).astype(F32)
    normed_grad = None
    for j in range(hidden_size // width):
        part = pl.ds(j * width, width)
        h = jnp.dot(low, up_ref[:, part], preferred_element_type=F32)
        u = jnp.dot(cot, downt_ref[:, part], preferred_element_type=F32)
        sq = h * h
        t = jnp.tanh(h * (GELU_A + GELU_B * sq))
        half = 0.5 * h
        act = (half + half * t).astype(BF16)
        slope = (0.5 + 0.5 * t) + half * (1.0 - t * t) * (GELU_A + (3.0 * GELU_B) * sq)
        hg = (u * slope).astype(BF16)
        out = out + jnp.dot(act, down_ref[part, :], preferred_element_type=F32)
        term = jnp.dot(hg, upt_ref[part, :], preferred_element_type=F32)
        normed_grad = term if normed_grad is None else normed_grad + term
        gup_ref[j] += lax.dot_general(low, hg, first, preferred_element_type=F32)
        gdt_s[:, part] += lax.dot_general(cot, act, first, preferred_element_type=F32)
    out_ref[...] = out.astype(BF16).reshape(rows, cols, channels)
    normed = normed_s[...]
    mean_grad = jnp.mean(normed_grad, axis=-1, keepdims=True)
    mean_cross = jnp.mean(normed_grad * normed, axis=-1, keepdims=True)
    grad = inv_scale * (normed_grad - mean_grad - normed * mean_cross)
    grad_ref[...] = grad.reshape(rows, cols, channels)
    edge_left_ref[...] = grad_ref[:, pl.ds(0, edge), :].astype(BF16)
    edge_right_ref[...] = grad_ref[:, pl.ds(cols - edge, edge), :].astype(BF16)

    @pl.when(step == pl.num_programs(0) - 1)
    def _():
        for j in range(hidden_size // width):
            part = pl.ds(j * width, width)
            gdown_ref[part, :] = gdt_s[:, part].T


def forward(fields, left, right, cot, kernel, up, down, block):
    rows, cols, channels = fields.shape
    edge, taps, hid = left.shape[1], kernel.shape[0], up.shape[1]
    by_row = lambda n: pl.BlockSpec((block, n, channels), lambda i: (i, 0, 0))
    whole = lambda *shape: pl.BlockSpec(shape, lambda i: (0,) * len(shape))
    padded = cols + 2 * edge
    cells = rows * cols
    return pl.pallas_call(
        forward_kernel,
        grid=(rows // block,),
        in_specs=[
            by_row(cols), by_row(edge), by_row(edge), by_row(cols), whole(taps, channels),
            whole(channels, hid), whole(hid, channels), whole(hid, channels), whole(channels, hid),
        ],
        out_specs=[
            by_row(cols), by_row(cols), by_row(edge), by_row(edge),
            whole(hid // 256, channels, 256), whole(hid, channels),
        ],
        out_shape=[
            jax.ShapeDtypeStruct((rows, cols, channels), BF16),
            jax.ShapeDtypeStruct((rows, cols, channels), F32),
            jax.ShapeDtypeStruct((rows, edge, channels), BF16),
            jax.ShapeDtypeStruct((rows, edge, channels), BF16),
            jax.ShapeDtypeStruct((hid // 256, channels, 256), F32),
            jax.ShapeDtypeStruct((hid, channels), F32),
        ],
        scratch_shapes=[
            pltpu.VMEM((padded, channels), F32),
            pltpu.VMEM((padded, channels), F32),
            pltpu.VMEM((taps, 8, channels), F32),
            pltpu.VMEM((block, cols, channels), F32),
            pltpu.VMEM((block * cols, channels), F32),
            pltpu.VMEM((channels, hid), F32),
        ],
        compiler_params=pltpu.CompilerParams(
            dimension_semantics=("arbitrary",), vmem_limit_bytes=50 * 2**20
        ),
        cost_estimate=pl.CostEstimate(
            flops=12 * cells * channels * hid, transcendentals=cells * hid,
            bytes_accessed=cells * channels * 12,
        ),
        name="forward",
    )(fields, left, right, cot, kernel, up, up.T, down, down.T)


def kernel_grad_kernel(fields_ref, left_ref, right_ref, grad_ref, out_ref, s0, s4, sums):
    step = pl.program_id(0)
    rows, cols, channels = fields_ref.shape
    taps = out_ref.shape[0] - 1
    blocks = cols // 8

    @pl.when(step == 0)
    def _():
        sums[...] = jnp.zeros_like(sums)

    def one_row(r, carry):
        stage_row(s0, s4, left_ref[r], fields_ref[r], right_ref[r])
        for lane in range(channels // 128):
            lanes = pl.ds(lane * 128, 128)
            grads = [grad_ref[r, pl.ds(8 * j, 8), lanes] for j in range(blocks)]
            acc = [None] * taps
            for i in range(blocks + taps // 2):
                for half, ref in ((0, s0), (1, s4)):
                    uses = [
                        (j, 2 * (i - j) + half)
                        for j in range(blocks)
                        if 0 <= 2 * (i - j) + half < taps
                    ]
                    if not uses:
                        continue
                    x = ref[pl.ds(8 * i, 8), lanes]
                    for j, t in uses:
                        term = grads[j] * x
                        acc[t] = term if acc[t] is None else acc[t] + term
            for t in range(taps):
                sums[t, :, lanes] += acc[t]
        return carry

    lax.fori_loop(0, rows, one_row, 0)

    @pl.when(step == pl.num_programs(0) - 1)
    def _():
        for t in range(taps):
            out_ref[pl.ds(t, 1), :] = jnp.sum(sums[t], axis=0, keepdims=True)
        out_ref[pl.ds(taps, 1), :] = jnp.zeros((1, channels), F32)


def kernel_grad(fields, left, right, grad, taps, block):
    rows, cols, channels = fields.shape
    edge = left.shape[1]
    by_row = lambda n: pl.BlockSpec((block, n, channels), lambda i: (i, 0, 0))
    return pl.pallas_call(
        kernel_grad_kernel,
        grid=(rows // block,),
        in_specs=[by_row(cols), by_row(edge), by_row(edge), by_row(cols)],
        out_specs=pl.BlockSpec((taps + 1, channels), lambda i: (0, 0)),
        out_shape=jax.ShapeDtypeStruct((taps + 1, channels), F32),
        scratch_shapes=[
            pltpu.VMEM((cols + 2 * edge, channels), F32),
            pltpu.VMEM((cols + 2 * edge, channels), F32),
            pltpu.VMEM((taps, 8, channels), F32),
        ],
        compiler_params=pltpu.CompilerParams(
            dimension_semantics=("arbitrary",), vmem_limit_bytes=32 * 2**20
        ),
        cost_estimate=pl.CostEstimate(
            flops=2 * taps * rows * cols * channels, transcendentals=0,
            bytes_accessed=rows * cols * channels * 8,
        ),
        name="kernel_grad",
    )(fields, left, right, grad)


def backward_kernel(grad_ref, left_ref, right_ref, cot_ref, kernel_ref, out_ref, s0, s4, kb):
    rows, cols, channels = grad_ref.shape
    taps = kernel_ref.shape[0]

    @pl.when(pl.program_id(0) == 0)
    def _():
        spread_taps(kb, kernel_ref, taps, True)

    def one_row(r, carry):
        stage_row(s0, s4, left_ref[r], grad_ref[r], right_ref[r])
        for lane in range(channels // 128):
            acc = conv_lane(s0, s4, kb, lane, cols, taps)
            lanes = pl.ds(lane * 128, 128)
            back = jnp.concatenate(acc, axis=0) + cot_ref[r, :, lanes].astype(F32)
            out_ref[r, :, lanes] = back.astype(BF16)
        return carry

    lax.fori_loop(0, rows, one_row, 0)


def backward(grad, left, right, cot, kernel, block):
    rows, cols, channels = grad.shape
    edge, taps = left.shape[1], kernel.shape[0]
    by_row = lambda n: pl.BlockSpec((block, n, channels), lambda i: (i, 0, 0))
    return pl.pallas_call(
        backward_kernel,
        grid=(rows // block,),
        in_specs=[
            by_row(cols), by_row(edge), by_row(edge), by_row(cols),
            pl.BlockSpec((taps, channels), lambda i: (0, 0)),
        ],
        out_specs=by_row(cols),
        out_shape=jax.ShapeDtypeStruct((rows, cols, channels), BF16),
        scratch_shapes=[
            pltpu.VMEM((cols + 2 * edge, channels), F32),
            pltpu.VMEM((cols + 2 * edge, channels), F32),
            pltpu.VMEM((taps, 8, channels), F32),
        ],
        compiler_params=pltpu.CompilerParams(
            dimension_semantics=("arbitrary",), vmem_limit_bytes=32 * 2**20
        ),
        cost_estimate=pl.CostEstimate(
            flops=2 * taps * rows * cols * channels, transcendentals=0,
            bytes_accessed=rows * cols * channels * 10,
        ),
        name="backward",
    )(grad, left, right, cot, kernel)


def per_device(fields, cotangent, kernel, up_weight, down_weight):
    rows, cols, channels = fields.shape
    taps, hid = kernel.shape[0], up_weight.shape[1]
    edge = KERNEL_SPACING * (taps // 2)
    left = passed_along(fields[:, cols - edge :], 1)
    right = passed_along(fields[:, :edge], -1)
    output, grad, edge_left, edge_right, gup, gdown = forward(
        fields, left, right, cotangent, kernel, up_weight, down_weight, 4
    )
    core, plane, depth = groups()
    weights = jnp.concatenate([gup.reshape(hid, channels), gdown], axis=0)
    part = scatter_stage(weights, core)
    grad_left = passed_along(edge_right, 1)
    grad_right = passed_along(edge_left, -1)
    part = scatter_stage(part, plane)
    kgrad = kernel_grad(fields, left, right, grad, taps, 8)
    part = scatter_stage(part, depth).astype(BF16)
    field_grad = backward(grad, grad_left, grad_right, cotangent, kernel, 8)
    part, kgrad = gather_stage(part, kgrad, depth)
    part, kgrad = gather_stage(part, kgrad, plane)
    part, kgrad = gather_stage(part, kgrad, core)
    factor = 1.0 / math.sqrt(rows * cols * lax.axis_size("lon") * lax.axis_size("lat"))
    scaled = part.astype(F32) * factor
    up_grad = scaled[:hid].reshape(hid // 256, channels, 256).transpose(1, 0, 2).reshape(channels, hid)
    return (output, field_grad, kgrad[:taps] * factor, up_grad, scaled[hid:])


def solution(mesh):
    placed = (P("lat", "lon", None), P("lat", "lon", None), P(), P(), P())
    return jax.shard_map(
        per_device,
        mesh=mesh,
        in_specs=placed,
        out_specs=(P("lat", "lon", None), P("lat", "lon", None), P(), P(), P()),
        check_vma=False,
    )
```

time: 283 us -> 158 us (0.56)
  other arithmetic: 72.4 us -> 5.55 us
  blocking collectives: 56 us -> 0 us
  Pallas kernels: 0 us -> 50.7 us
  matrix products: 38.9 us -> 0 us
  waiting for transfers between devices: 65.1 us -> 45.2 us
  between operations: 14.3 us -> 1.02 us
  local copies, waits for them, and re-layouts: 11.7 us -> 22.3 us
  starting transfers between devices: 23.9 us -> 33 us
    psum x1 -> x0, blocking collectives: 56 us -> none  [per_device(): summed = lax.psum((kernel_terms, grad_up, grad_down), ('lon', 'lat'))]
    pallas_call x0 -> x3, Pallas kernels: none -> 50.7 us  [the longest x1 32.5 us: forward(): pl.pallas_call(forward_kernel, grid=(rows // block,), in_specs=[by_row(co...]
    psum x1 -> x0, waiting for transfers between devices: 45.9 us -> none  [per_device(): summed = lax.psum((kernel_terms, grad_up, grad_down), ('lon', 'lat'))]
    dot_general x6 -> x0, matrix products: 38.9 us -> none  [the longest x1 15.9 us: per_device(): lax.dot_general(flat_cot, down_weight, contract_last, preferred_element_t...]
    reduce_sum x4 -> x0, other arithmetic: 38.2 us -> none  [the longest x2 18.9 us: per_device(): jnp.sum(wrapped_input[:, KERNEL_SPACING * index_of_tap:KERNEL_SPACING * i...]
    convert_element_type x2 -> x3, other arithmetic: 26.2 us -> 0.04 us  [gather_stage(): packed = jnp.concatenate([value, extra.astype(BF16)], axis=0)]
    ppermute x4 -> x18, waiting for transfers between devices: 19.2 us -> 45.2 us  [the longest x14 35.2 us: xor_permute(): return lax.ppermute(value, AXES, pairs)]
    ppermute x4 -> x18, starting transfers between devices: 23.9 us -> 33 us  [the longest x14 22.8 us: xor_permute(): return lax.ppermute(value, AXES, pairs)]
  transfers between devices with their start and end apart: 5 -> 18, of which waited for: 2 -> 9; matrix products, arithmetic and copies ran while one was open for 14% -> 4% of each run, Pallas kernels for 0% -> 12%
where the time goes in v1:
time: 158 us
  Pallas kernels  50.7 us (32%)
  waiting for transfers between devices  45.2 us (29%)
  starting transfers between devices  33 us (21%)
  local copies, waits for them, and re-layouts  22.3 us (14%)
  other arithmetic  5.55 us (4%)
    ppermute x14, waiting for transfers between devices, xor_permute(): return lax.ppermute(value, AXES, pairs)  35.2 us
    pallas_call x1, Pallas kernels, forward(): pl.pallas_call(forward_kernel, grid=(rows // block,), in_specs=[by_row(co...  32.5 us
    ppermute x14, starting transfers between devices, xor_permute(): return lax.ppermute(value, AXES, pairs)  22.8 us
    ppermute x4, starting transfers between devices, passed_along(): lax.ppermute(value, 'lon', [(i, (i + by) % count) for i in range(count)])  10.2 us
    ppermute x4, waiting for transfers between devices, passed_along(): lax.ppermute(value, 'lon', [(i, (i + by) % count) for i in range(count)])  10 us
    pallas_call x1, Pallas kernels, backward(): pl.pallas_call(backward_kernel, grid=(rows // block,), in_specs=[by_row(c...  9.48 us
    unnamed x32, local copies, waits for them, and re-layouts  9.38 us
    pallas_call x1, Pallas kernels, kernel_grad(): pl.pallas_call(kernel_grad_kernel, grid=(rows // block,), in_specs=[by_ro...  8.7 us
  transfers between devices with their start and end apart: 18, of which 9 were waited for; matrix products, arithmetic and copies ran while one was open for 4% of the time, Pallas kernels for 12%

profile of v1, /device:TPU:0, one launch (start us, length us, event | category | flops | bytes accessed | tf_op | source)
XLA Modules:
  0.0 157.8 jit_solution(5161425109120398591)
XLA Ops:
  0.6 2.1 %fusion.23 = (bf16[32,60,256]{2,1,0:T(8,128)(2,1)S(1)}, bf16[32,60,256]{2,1,0:T(8,128)(2,1)S(1)}) fusion(bf16[32,112,256]{2,1,0:T(8,128)(2,1)} %fields_ref.3), kind=kLoop, calls=%fused_computation.51 | loop fusion | bytes 3932160 | tf_op jit(solution)/shard_map/slice | solution.py:345
  2.7 0.0 copy-start.8
  2.7 0.0 copy-start.9
  2.7 0.5 copy.26
  3.3 0.5 collective-permute-start
  3.8 1.5 copy.27
  5.3 5.0 %collective-permute-start.1 = (bf16[32,60,256]{2,0,1:T(8,128)(2,1)}, bf16[32,60,256]{2,0,1:T(8,128)(2,1)}, u32[]{:S(2)}, u32[]{:S(2)}) collective-permute-start(bf16[32,60,256]{2,0,1:T(8,128)(2,1)} %copy.27), channel_id=1, source_target_pairs={{0,30},{2,0},{4,2},{6,4},{8,6},{10,8},{12,10},{14,12},{16,14},{18,... | collective-permute-start | bytes 2949128 | tf_op jit(solution)/shard_map/ppermute | solution.py:32
  10.3 0.2 copy.15
  10.5 0.2 copy.16
  10.7 0.0 copy-start.10
  10.7 10.0 %collective-permute-done = bf16[32,60,256]{2,0,1:T(8,128)(2,1)} collective-permute-done((bf16[32,60,256]{2,0,1:T(8,128)(2,1)S(1)}, bf16[32,60,256]{2,0,1:T(8,128)(2,1)}, u32[]{:S(2)}, u32[]{:S(2)}) %collective-permute-start) | collective-permute-done | bytes 983072 | tf_op jit(solution)/shard_map/ppermute | solution.py:32
  20.8 2.7 %copy.17.left_ref = bf16[32,60,256]{2,1,0:T(8,128)(2,1)} copy(bf16[32,60,256]{2,0,1:T(8,128)(2,1)} %collective-permute-done) | data formatting | bytes 1966080 | tf_op jit(solution)/shard_map/ppermute | solution.py:32
  23.5 2.7 %copy.18.right_ref = bf16[32,60,256]{2,1,0:T(8,128)(2,1)} copy(bf16[32,60,256]{2,0,1:T(8,128)(2,1)} %collective-permute-done.1) | data formatting | bytes 1966080 | tf_op jit(solution)/shard_map/ppermute | solution.py:32
  26.2 32.5 %forward.1 = (bf16[32,112,256]{2,1,0:T(8,128)(2,1)}, f32[32,112,256]{2,1,0:T(8,128)}, bf16[32,60,256]{2,1,0:T(8,128)(2,1)S(1)}, bf16[32,60,256]{2,1,0:T(8,128)(2...) custom-call(bf16[32,112,256]{2,1,0:T(8,128)(2,1)} %fields_ref.3, bf16[32,60,256]{2,1,0:T(8,128)(2,1)} %copy.17.left_ref, ...), custom_call_target="tpu_custom_call" | custom-call | flops 11274289152 | bytes 11010048 | tf_op jit(solution)/shard_map/forward/pallas_call | solution.py:185
  58.7 2.1 %pad_maximum_fusion = f32[2048,256]{1,0:T(8,128)S(1)} fusion(f32[1024,256]{1,0:T(8,128)} %get-tuple-element.16, f32[1024,256]{1,0:T(8,128)} %bitcast.94), kind=kLoop, calls=%fused_computation | loop fusion | flops 524288 | bytes 4194304 | tf_op jit(solution)/shard_map/concatenate | solution.py:350
  60.8 1.3 copy-done.11
  62.1 0.1 fusion
  62.1 7.6 %collective-permute-start.4 = (bf16[1024,256]{1,0:T(8,128)(2,1)S(1)}, bf16[1024,256]{1,0:T(8,128)(2,1)}, u32[]{:S(2)}, u32[]{:S(2)}) collective-permute-start(bf16[1024,256]{1,0:T(8,128)(2,1)S(1)} %fusion), channel_id=1, source_target_pairs={{0,2},{1,3},{2,0},{3,1},{4,6},{5,7},{6,4},{7,5},{8,10},{9,11},{10,... | collective-permute-start | bytes 1572872 | tf_op jit(solution)/shard_map/ppermute | solution.py:27
  69.7 1.7 %collective-permute-done.4 = bf16[1024,256]{1,0:T(8,128)(2,1)} collective-permute-done((bf16[1024,256]{1,0:T(8,128)(2,1)S(1)}, bf16[1024,256]{1,0:T(8,128)(2,1)}, u32[]{:S(2)}, u32[]{:S(2)}) %collective-permute-start.4) | collective-permute-done | bytes 524320 | tf_op jit(solution)/shard_map/ppermute | solution.py:27
  71.4 1.5 bitcast_add_fusion
  72.9 1.0 copy-done.12
  73.9 0.7 fusion.4
  74.6 3.5 %collective-permute-start.7 = (bf16[256,256]{1,0:T(8,128)(2,1)}, bf16[256,256]{1,0:T(8,128)(2,1)S(1)}, u32[]{:S(2)}, u32[]{:S(2)}) collective-permute-start(bf16[256,256]{1,0:T(8,128)(2,1)} %get-tuple-element.26), channel_id=1, source_target_pairs={{0,5},{1,4},{2,7},{3,6},{4,1},{5,0},{6,3},{7,2},{8,13},{9,12},{10,... | collective-permute-start | bytes 393224 | tf_op jit(solution)/shard_map/ppermute | solution.py:27
  78.1 0.5 collective-permute-start.6
  78.6 0.1 collective-permute-start.5
  78.6 3.7 %collective-permute-done.7 = bf16[256,256]{1,0:T(8,128)(2,1)S(1)} collective-permute-done((bf16[256,256]{1,0:T(8,128)(2,1)}, bf16[256,256]{1,0:T(8,128)(2,1)S(1)}, u32[]{:S(2)}, u32[]{:S(2)}) %collective-permute-start.7) | collective-permute-done | bytes 131104 | tf_op jit(solution)/shard_map/ppermute | solution.py:27
  82.4 2.5 %collective-permute-done.6 = bf16[256,256]{1,0:T(8,128)(2,1)S(1)} collective-permute-done((bf16[256,256]{1,0:T(8,128)(2,1)S(1)}, bf16[256,256]{1,0:T(8,128)(2,1)S(1)}, u32[]{:S(2)}, u32[]{:S(2)}) %collective-permute-start.6) | collective-permute-done | bytes 131104 | tf_op jit(solution)/shard_map/ppermute | solution.py:27
  84.9 0.1 collective-permute-done.5
  85.0 1.1 fusion.3
  86.1 3.6 %collective-permute-start.10 = (bf16[64,256]{1,0:T(8,128)(2,1)S(1)}, bf16[64,256]{1,0:T(8,128)(2,1)S(1)}, u32[]{:S(2)}, u32[]{:S(2)}) collective-permute-start(bf16[64,256]{1,0:T(8,128)(2,1)S(1)} %get-tuple-element.29), channel_id=1, source_target_pairs={{0,24},{1,25},{2,26},{3,27},{4,28},{5,29},{6,30},{7,31},{8,16},{9,... | collective-permute-start | bytes 98312 | tf_op jit(solution)/shard_map/ppermute | solution.py:27
  89.7 0.0 collective-permute-start.9
  89.7 0.8 collective-permute-start.8
  90.5 2.0 %copy-done = f32[32,112,256]{2,1,0:T(8,128)S(1)} copy-done((f32[32,112,256]{2,1,0:T(8,128)S(1)}, f32[32,112,256]{2,1,0:T(8,128)}, u32[]{:S(2)}) %copy-start) | copy-done | bytes 3670040
  92.6 1.2 copy-done.4
  93.8 8.7 %kernel_grad.1 = f32[32,256]{1,0:T(8,128)S(1)} custom-call(bf16[32,112,256]{2,1,0:T(8,128)(2,1)S(1)} %copy-done.2, bf16[32,60,256]{2,1,0:T(8,128)(2,1)S(1)} %copy-done.3, bf16[32,60,256]{2,1,0:T(8,128)(2,1)S(1)} %copy-done.4, f32[32,112,256]{2,1,0:T(8,128)S(1)} %copy-done), custom_call_target="tpu_custom_call" | custom-call | flops 56885248 | bytes 7340032 | tf_op jit(solution)/shard_map/kernel_grad/pallas_call | solution.py:269
  102.5 0.0 collective-permute-done.10
  102.5 0.0 collective-permute-done.9
  102.6 1.3 collective-permute-start.11
  103.9 2.4 %collective-permute-start.13 = (bf16[96,256]{1,0:T(8,128)(2,1)S(1)}, bf16[96,256]{1,0:T(8,128)(2,1)S(1)}, u32[]{:S(2)}, u32[]{:S(2)}) collective-permute-start(bf16[96,256]{1,0:T(8,128)(2,1)S(1)} %pad_maximum_fusion.3), channel_id=1, source_target_pairs={{0,24},{1,25},{2,26},{3,27},{4,28},{5,29},{6,30},{7,31},{8,16},{9,... | collective-permute-start | bytes 147464 | tf_op jit(solution)/shard_map/ppermute | solution.py:27
  106.3 0.5 collective-permute-start.12
  106.8 0.0 collective-permute-done.11
  106.8 3.3 %collective-permute-done.13 = bf16[96,256]{1,0:T(8,128)(2,1)S(1)} collective-permute-done((bf16[96,256]{1,0:T(8,128)(2,1)S(1)}, bf16[96,256]{1,0:T(8,128)(2,1)S(1)}, u32[]{:S(2)}, u32[]{:S(2)}) %collective-permute-start.13) | collective-permute-done | bytes 49184 | tf_op jit(solution)/shard_map/ppermute | solution.py:27
  110.1 1.3 collective-permute-done.12
  111.4 2.0 %collective-permute-start.14 = (bf16[288,256]{1,0:T(8,128)(2,1)S(1)}, bf16[288,256]{1,0:T(8,128)(2,1)S(1)}, u32[]{:S(2)}, u32[]{:S(2)}) collective-permute-start(bf16[288,256]{1,0:T(8,128)(2,1)S(1)} %pad_maximum_fusion.2), channel_id=1, source_target_pairs={{0,4},{1,5},{2,6},{3,7},{4,0},{5,1},{6,2},{7,3},{8,12},{9,13},{10,... | collective-permute-start | bytes 442376 | tf_op jit(solution)/shard_map/ppermute | solution.py:27
  113.3 0.5 copy.19
  113.9 0.1 collective-permute-start.2
  114.0 0.5 copy.20
  114.5 4.7 %collective-permute-start.3 = (bf16[32,60,256]{2,0,1:T(8,128)(2,1)S(1)}, bf16[32,60,256]{2,0,1:T(8,128)(2,1)S(1)}, u32[]{:S(2)}, u32[]{:S(2)}) collective-permute-start(bf16[32,60,256]{2,0,1:T(8,128)(2,1)S(1)} %copy.20), channel_id=1, source_target_pairs={{0,30},{2,0},{4,2},{6,4},{8,6},{10,8},{12,10},{14,12},{16,14},{18,... | collective-permute-start | bytes 2949128 | tf_op jit(solution)/shard_map/ppermute | solution.py:32
  119.2 0.0 collective-permute-start.16
  119.2 0.5 collective-permute-start.15
  119.8 4.5 %collective-permute-done.15 = bf16[288,256]{1,0:T(8,128)(2,1)S(1)} collective-permute-done((bf16[288,256]{1,0:T(8,128)(2,1)S(1)}, bf16[288,256]{1,0:T(8,128)(2,1)S(1)}, u32[]{:S(2)}, u32[]{:S(2)}) %collective-permute-start.15) | collective-permute-done | bytes 147488 | tf_op jit(solution)/shard_map/ppermute | solution.py:27
  124.3 18.1 %collective-permute-done.16 = bf16[288,256]{1,0:T(8,128)(2,1)S(1)} collective-permute-done((bf16[288,256]{1,0:T(8,128)(2,1)S(1)}, bf16[288,256]{1,0:T(8,128)(2,1)S(1)}, u32[]{:S(2)}, u32[]{:S(2)}) %collective-permute-start.16) | collective-permute-done | bytes 147488 | tf_op jit(solution)/shard_map/ppermute | solution.py:27
  142.6 0.1 collective-permute-start.17
  142.6 0.0 copy-start.5
  142.7 0.1 broadcast_in_dim.52
  142.8 0.5 copy.21.left_ref
  143.4 0.5 copy.22.right_ref
  143.9 0.2 copy-done.5
  144.1 1.1 copy-done.1
  145.3 9.5 %backward.1 = bf16[32,112,256]{2,1,0:T(8,128)(2,1)} custom-call(f32[32,112,256]{2,1,0:T(8,128)S(1)} %copy-done.1, bf16[32,60,256]{2,1,0:T(8,128)(2,1)S(1)} %copy.21.left_ref, bf16[32,60,256]{2,1,0:T(8,128)(2,1)S(1)} %copy.22.right_ref, bf16[32,112,256]{2,1,0:T(8,128)(2,1)S(1)} %copy-done.5, f32[31,256]{1,0:T(8,128)S(1)} %copy-done.10), custom_call_target="tpu_custom_call" | custom-call | flops 56885248 | bytes 9175040 | tf_op jit(solution)/shard_map/backward/pallas_call | solution.py:315
  154.8 0.2 convert_multiply_fusion
  155.0 1.1 slice_bitcast_fusion
  156.1 1.1 copy.28
  157.2 0.6 fusion.16
  (44 shorter events, 0.4 us)
Async XLA Ops:
  2.7 7.6 %copy-start.8 = (bf16[256,1024]{1,0:T(8,128)(2,1)S(1)}, bf16[256,1024]{1,0:T(8,128)(2,1)}, u32[]{:S(2)}) copy-start(bf16[256,1024]{1,0:T(8,128)(2,1)} %up_ref.1) | copy-start | bytes 1572868
  2.7 7.8 %copy-start.9 = (bf16[1024,256]{1,0:T(8,128)(2,1)S(1)}, bf16[1024,256]{1,0:T(8,128)(2,1)}, u32[]{:S(2)}) copy-start(bf16[1024,256]{1,0:T(8,128)(2,1)} %down_ref.1) | copy-start | bytes 1572868
  3.3 17.5 %collective-permute-start = (bf16[32,60,256]{2,0,1:T(8,128)(2,1)S(1)}, bf16[32,60,256]{2,0,1:T(8,128)(2,1)}, u32[]{:S(2)}, u32[]{:S(2)}) collective-permute-start(bf16[32,60,256]{2,0,1:T(8,128)(2,1)S(1)} %copy.26), channel_id=1, source_target_pairs={{0,2},{2,4},{4,6},{6,8},{8,10},{10,12},{12,14},{14,16},{16,18},{18... | collective-permute-start | bytes 2949128 | tf_op jit(solution)/shard_map/ppermute | solution.py:32
  5.3 18.2 %collective-permute-start.1 = (bf16[32,60,256]{2,0,1:T(8,128)(2,1)}, bf16[32,60,256]{2,0,1:T(8,128)(2,1)}, u32[]{:S(2)}, u32[]{:S(2)}) collective-permute-start(bf16[32,60,256]{2,0,1:T(8,128)(2,1)} %copy.27), channel_id=1, source_target_pairs={{0,30},{2,0},{4,2},{6,4},{8,6},{10,8},{12,10},{14,12},{16,14},{18,... | collective-permute-start | bytes 2949128 | tf_op jit(solution)/shard_map/ppermute | solution.py:32
  10.7 15.5 %copy-start.10 = (f32[31,256]{1,0:T(8,128)S(1)}, f32[31,256]{1,0:T(8,128)}, u32[]{:S(2)}) copy-start(f32[31,256]{1,0:T(8,128)} %kernel_ref.3) | copy-start | bytes 95236
  58.7 2.1 %copy-start.6 = (bf16[32,60,256]{2,1,0:T(8,128)(2,1)}, bf16[32,60,256]{2,1,0:T(8,128)(2,1)S(1)}, u32[]{:S(2)}) copy-start(bf16[32,60,256]{2,1,0:T(8,128)(2,1)S(1)} %get-tuple-element.14) | copy-start | bytes 2949124
  60.8 1.3 copy-start.11
  62.1 9.3 %collective-permute-start.4 = (bf16[1024,256]{1,0:T(8,128)(2,1)S(1)}, bf16[1024,256]{1,0:T(8,128)(2,1)}, u32[]{:S(2)}, u32[]{:S(2)}) collective-permute-start(bf16[1024,256]{1,0:T(8,128)(2,1)S(1)} %fusion), channel_id=1, source_target_pairs={{0,2},{1,3},{2,0},{3,1},{4,6},{5,7},{6,4},{7,5},{8,10},{9,11},{10,... | collective-permute-start | bytes 1572872 | tf_op jit(solution)/shard_map/ppermute | solution.py:27
  69.7 20.8 %copy-start.2 = (bf16[32,112,256]{2,1,0:T(8,128)(2,1)S(1)}, bf16[32,112,256]{2,1,0:T(8,128)(2,1)}, u32[]{:S(2)}) copy-start(bf16[32,112,256]{2,1,0:T(8,128)(2,1)} %fields_ref.3) | copy-start | bytes 5505028
  69.7 20.8 %copy-start.3 = (bf16[32,60,256]{2,1,0:T(8,128)(2,1)S(1)}, bf16[32,60,256]{2,1,0:T(8,128)(2,1)}, u32[]{:S(2)}) copy-start(bf16[32,60,256]{2,1,0:T(8,128)(2,1)} %copy.17.left_ref) | copy-start | bytes 2949124
  72.9 1.0 copy-start.12
  74.6 7.8 %collective-permute-start.7 = (bf16[256,256]{1,0:T(8,128)(2,1)}, bf16[256,256]{1,0:T(8,128)(2,1)S(1)}, u32[]{:S(2)}, u32[]{:S(2)}) collective-permute-start(bf16[256,256]{1,0:T(8,128)(2,1)} %get-tuple-element.26), channel_id=1, source_target_pairs={{0,5},{1,4},{2,7},{3,6},{4,1},{5,0},{6,3},{7,2},{8,13},{9,12},{10,... | collective-permute-start | bytes 393224 | tf_op jit(solution)/shard_map/ppermute | solution.py:27
  78.1 6.8 %collective-permute-start.6 = (bf16[256,256]{1,0:T(8,128)(2,1)S(1)}, bf16[256,256]{1,0:T(8,128)(2,1)S(1)}, u32[]{:S(2)}, u32[]{:S(2)}) collective-permute-start(bf16[256,256]{1,0:T(8,128)(2,1)S(1)} %get-tuple-element.27), channel_id=1, source_target_pairs={{0,1},{1,0},{2,3},{3,2},{4,5},{5,4},{6,7},{7,6},{8,9},{9,8},{10,11... | collective-permute-start | bytes 393224 | tf_op jit(solution)/shard_map/ppermute | solution.py:27
  78.6 6.4 %collective-permute-start.5 = (bf16[256,256]{1,0:T(8,128)(2,1)S(1)}, bf16[256,256]{1,0:T(8,128)(2,1)}, u32[]{:S(2)}, u32[]{:S(2)}) collective-permute-start(bf16[256,256]{1,0:T(8,128)(2,1)S(1)} %get-tuple-element.25), channel_id=1, source_target_pairs={{0,4},{1,5},{2,6},{3,7},{4,0},{5,1},{6,2},{7,3},{8,12},{9,13},{10,... | collective-permute-start | bytes 393224 | tf_op jit(solution)/shard_map/ppermute | solution.py:27
  86.1 16.5 %collective-permute-start.10 = (bf16[64,256]{1,0:T(8,128)(2,1)S(1)}, bf16[64,256]{1,0:T(8,128)(2,1)S(1)}, u32[]{:S(2)}, u32[]{:S(2)}) collective-permute-start(bf16[64,256]{1,0:T(8,128)(2,1)S(1)} %get-tuple-element.29), channel_id=1, source_target_pairs={{0,24},{1,25},{2,26},{3,27},{4,28},{5,29},{6,30},{7,31},{8,16},{9,... | collective-permute-start | bytes 98312 | tf_op jit(solution)/shard_map/ppermute | solution.py:27
  89.7 12.9 %collective-permute-start.9 = (bf16[64,256]{1,0:T(8,128)(2,1)S(1)}, bf16[64,256]{1,0:T(8,128)(2,1)S(1)}, u32[]{:S(2)}, u32[]{:S(2)}) collective-permute-start(bf16[64,256]{1,0:T(8,128)(2,1)S(1)} %get-tuple-element.30), channel_id=1, source_target_pairs={{0,16},{1,17},{2,18},{3,19},{4,20},{5,21},{6,22},{7,23},{8,24},{9,... | collective-permute-start | bytes 98312 | tf_op jit(solution)/shard_map/ppermute | solution.py:27
  89.7 12.9 %collective-permute-start.8 = (bf16[64,256]{1,0:T(8,128)(2,1)S(1)}, bf16[64,256]{1,0:T(8,128)(2,1)S(1)}, u32[]{:S(2)}, u32[]{:S(2)}) collective-permute-start(bf16[64,256]{1,0:T(8,128)(2,1)S(1)} %get-tuple-element.28), channel_id=1, source_target_pairs={{0,8},{1,9},{2,10},{3,11},{4,12},{5,13},{6,14},{7,15},{8,0},{9,1},... | collective-permute-start | bytes 98312 | tf_op jit(solution)/shard_map/ppermute | solution.py:27
  90.5 2.0 %copy-start = (f32[32,112,256]{2,1,0:T(8,128)S(1)}, f32[32,112,256]{2,1,0:T(8,128)}, u32[]{:S(2)}) copy-start(f32[32,112,256]{2,1,0:T(8,128)} %get-tuple-element.12.grad_ref) | copy-start | bytes 11010052
  92.6 1.2 copy-start.4
  93.8 19.6 %copy-start.13 = (bf16[32,60,256]{2,1,0:T(8,128)(2,1)S(1)}, bf16[32,60,256]{2,1,0:T(8,128)(2,1)}, u32[]{:S(2)}) copy-start(bf16[32,60,256]{2,1,0:T(8,128)(2,1)} %get-tuple-element.13) | copy-start | bytes 2949124
  102.5 11.5 %copy-start.7 = (bf16[32,60,256]{2,1,0:T(8,128)(2,1)S(1)}, bf16[32,60,256]{2,1,0:T(8,128)(2,1)}, u32[]{:S(2)}) copy-start(bf16[32,60,256]{2,1,0:T(8,128)(2,1)} %copy-done.6) | copy-start | bytes 2949124
  102.6 4.2 %collective-permute-start.11 = (bf16[96,256]{1,0:T(8,128)(2,1)S(1)}, bf16[96,256]{1,0:T(8,128)(2,1)S(1)}, u32[]{:S(2)}, u32[]{:S(2)}) collective-permute-start(bf16[96,256]{1,0:T(8,128)(2,1)S(1)} %pad_maximum_fusion.3), channel_id=1, source_target_pairs={{0,8},{1,9},{2,10},{3,11},{4,12},{5,13},{6,14},{7,15},{8,0},{9,1},... | collective-permute-start | bytes 147464 | tf_op jit(solution)/shard_map/ppermute | solution.py:27
  103.9 6.2 %collective-permute-start.13 = (bf16[96,256]{1,0:T(8,128)(2,1)S(1)}, bf16[96,256]{1,0:T(8,128)(2,1)S(1)}, u32[]{:S(2)}, u32[]{:S(2)}) collective-permute-start(bf16[96,256]{1,0:T(8,128)(2,1)S(1)} %pad_maximum_fusion.3), channel_id=1, source_target_pairs={{0,24},{1,25},{2,26},{3,27},{4,28},{5,29},{6,30},{7,31},{8,16},{9,... | collective-permute-start | bytes 147464 | tf_op jit(solution)/shard_map/ppermute | solution.py:27
  106.3 5.0 %collective-permute-start.12 = (bf16[96,256]{1,0:T(8,128)(2,1)S(1)}, bf16[96,256]{1,0:T(8,128)(2,1)S(1)}, u32[]{:S(2)}, u32[]{:S(2)}) collective-permute-start(bf16[96,256]{1,0:T(8,128)(2,1)S(1)} %pad_maximum_fusion.3), channel_id=1, source_target_pairs={{0,16},{1,17},{2,18},{3,19},{4,20},{5,21},{6,22},{7,23},{8,24},{9,... | collective-permute-start | bytes 147464 | tf_op jit(solution)/shard_map/ppermute | solution.py:27
  111.4 8.4 %collective-permute-start.14 = (bf16[288,256]{1,0:T(8,128)(2,1)S(1)}, bf16[288,256]{1,0:T(8,128)(2,1)S(1)}, u32[]{:S(2)}, u32[]{:S(2)}) collective-permute-start(bf16[288,256]{1,0:T(8,128)(2,1)S(1)} %pad_maximum_fusion.2), channel_id=1, source_target_pairs={{0,4},{1,5},{2,6},{3,7},{4,0},{5,1},{6,2},{7,3},{8,12},{9,13},{10,... | collective-permute-start | bytes 442376 | tf_op jit(solution)/shard_map/ppermute | solution.py:27
  113.9 28.9 %collective-permute-start.2 = (bf16[32,60,256]{2,0,1:T(8,128)(2,1)S(1)}, bf16[32,60,256]{2,0,1:T(8,128)(2,1)S(1)}, u32[]{:S(2)}, u32[]{:S(2)}) collective-permute-start(bf16[32,60,256]{2,0,1:T(8,128)(2,1)S(1)} %copy.19), channel_id=1, source_target_pairs={{0,2},{2,4},{4,6},{6,8},{8,10},{10,12},{12,14},{14,16},{16,18},{18... | collective-permute-start | bytes 2949128 | tf_op jit(solution)/shard_map/ppermute | solution.py:32
  114.5 28.8 %collective-permute-start.3 = (bf16[32,60,256]{2,0,1:T(8,128)(2,1)S(1)}, bf16[32,60,256]{2,0,1:T(8,128)(2,1)S(1)}, u32[]{:S(2)}, u32[]{:S(2)}) collective-permute-start(bf16[32,60,256]{2,0,1:T(8,128)(2,1)S(1)} %copy.20), channel_id=1, source_target_pairs={{0,30},{2,0},{4,2},{6,4},{8,6},{10,8},{12,10},{14,12},{16,14},{18,... | collective-permute-start | bytes 2949128 | tf_op jit(solution)/shard_map/ppermute | solution.py:32
  119.2 23.3 %collective-permute-start.16 = (bf16[288,256]{1,0:T(8,128)(2,1)S(1)}, bf16[288,256]{1,0:T(8,128)(2,1)S(1)}, u32[]{:S(2)}, u32[]{:S(2)}) collective-permute-start(bf16[288,256]{1,0:T(8,128)(2,1)S(1)} %pad_maximum_fusion.2), channel_id=1, source_target_pairs={{0,5},{1,4},{2,7},{3,6},{4,1},{5,0},{6,3},{7,2},{8,13},{9,12},{10,... | collective-permute-start | bytes 442376 | tf_op jit(solution)/shard_map/ppermute | solution.py:27
  119.2 5.1 %collective-permute-start.15 = (bf16[288,256]{1,0:T(8,128)(2,1)S(1)}, bf16[288,256]{1,0:T(8,128)(2,1)S(1)}, u32[]{:S(2)}, u32[]{:S(2)}) collective-permute-start(bf16[288,256]{1,0:T(8,128)(2,1)S(1)} %pad_maximum_fusion.2), channel_id=1, source_target_pairs={{0,1},{1,0},{2,3},{3,2},{4,5},{5,4},{6,7},{7,6},{8,9},{9,8},{10,11... | collective-permute-start | bytes 442376 | tf_op jit(solution)/shard_map/ppermute | solution.py:27
  142.6 12.2 %collective-permute-start.17 = (bf16[1056,256]{1,0:T(8,128)(2,1)S(1)}, bf16[1056,256]{1,0:T(8,128)(2,1)S(1)}, u32[]{:S(2)}, u32[]{:S(2)}) collective-permute-start(bf16[1056,256]{1,0:T(8,128)(2,1)S(1)} %pad_maximum_fusion.1), channel_id=1, source_target_pairs={{0,2},{1,3},{2,0},{3,1},{4,6},{5,7},{6,4},{7,5},{8,10},{9,11},{10,... | collective-permute-start | bytes 1622024 | tf_op jit(solution)/shard_map/ppermute | solution.py:27
  142.6 1.5 copy-start.5
  142.8 2.5 %copy-start.1 = (f32[32,112,256]{2,1,0:T(8,128)S(1)}, f32[32,112,256]{2,1,0:T(8,128)}, u32[]{:S(2)}) copy-start(f32[32,112,256]{2,1,0:T(8,128)} %get-tuple-element.12.grad_ref) | copy-start | bytes 11010052

commit v2 on v0

v2 whole, which is shorter than its diff:
```python
import functools
import math

import jax
import jax.numpy as jnp
from jax import lax
from jax.experimental import pallas as pl
from jax.experimental.pallas import tpu as pltpu
from jax.sharding import PartitionSpec as P

KERNEL_SPACING = 4
BLOCK = 4
AXES = ("lon", "lat")
F32 = jnp.float32
BF16 = jnp.bfloat16
GELU_A = math.sqrt(2.0 / math.pi)
GELU_B = GELU_A * 0.044715


def xor_permute(value, mask):
    nlon, nlat = lax.axis_size("lon"), lax.axis_size("lat")
    lat_mask, lon_mask = mask
    pairs = [
        (lon * nlat + lat, (lon ^ lon_mask) * nlat + (lat ^ lat_mask))
        for lon in range(nlon)
        for lat in range(nlat)
    ]
    return lax.ppermute(value, AXES, pairs)


def passed_along(value, by):
    count = lax.axis_size("lon")
    return lax.ppermute(value, "lon", [(i, (i + by) % count) for i in range(count)])


def groups():
    nlon, nlat = lax.axis_size("lon"), lax.axis_size("lat")
    lon, lat = lax.axis_index("lon").astype(jnp.uint32), lax.axis_index("lat").astype(jnp.uint32)
    core = (lon & 1, [(0, s) for s in range(2)])
    plane = (lat * 2 + ((lon >> 1) & 1), [(s >> 1, (s & 1) * 2) for s in range(2 * nlat)])
    depth = (lon >> 2, [(0, s * 4) for s in range(nlon // 4)])
    return [([own ^ jnp.uint32(s) for s in range(len(masks))], masks) for own, masks in (core, plane, depth)]


def piece(parts, place):
    zero = jnp.uint32(0)
    return lax.dynamic_slice(parts, (place, zero, zero), (1,) + parts.shape[1:])[0]


def scatter_stage(value, group):
    places, _ = group
    size = len(places)
    parts = value.reshape(size, value.shape[0] // size, value.shape[1])
    return [piece(parts, p).astype(BF16) for p in places[1:]], piece(parts, places[0])


def scatter_finish(sends, total, group):
    _, masks = group
    for send, mask in zip(sends, masks[1:]):
        total = total + xor_permute(send, mask).astype(F32)
    return total


def gather_finish(packed, extra, group):
    places, masks = group
    size = len(places)
    rows = packed.shape[0] - extra.shape[0]
    got = [packed[:rows]]
    for s in range(1, size):
        part = xor_permute(packed, masks[s])
        got.append(part[:rows])
        extra = extra + part[rows:].astype(F32)
    whole = jnp.zeros((size, rows, packed.shape[1]), packed.dtype)
    zero = jnp.uint32(0)
    for part, place in zip(got, places):
        whole = lax.dynamic_update_slice(whole, part[None], (place, zero, zero))
    return whole.reshape(size * rows, packed.shape[1]), extra


def pack(value, extra):
    return jnp.concatenate([value, extra.astype(BF16)], axis=0)


def lane_groups(channels):
    return range(channels // 128)


def stage_row(s0, s4, left, middle, right):
    edge, cols = left.shape[0], middle.shape[0]
    left, middle, right = left.astype(F32), middle.astype(F32), right.astype(F32)
    s0[pl.ds(0, edge), :] = left
    s0[pl.ds(edge, cols), :] = middle
    s0[pl.ds(edge + cols, edge), :] = right
    s4[pl.ds(0, edge - 4), :] = left[4:]
    s4[pl.ds(edge - 4, cols), :] = middle
    s4[pl.ds(edge - 4 + cols, edge - 4), :] = right[: edge - 4]


def spread_taps(kb, kernel_ref, flip):
    taps = kernel_ref.shape[0]
    for t in range(taps):
        row = kernel_ref[pl.ds(taps - 1 - t if flip else t, 1), :]
        kb[t] = jnp.broadcast_to(row, kb.shape[1:])


def tap_uses(blocks, taps, edge):
    lead = (edge - KERNEL_SPACING * (taps // 2)) // 4
    result = []
    for i in range(blocks + 2 * edge // 8):
        for half in (0, 1):
            uses = []
            for j in range(blocks):
                t = 2 * (i - j) + half - lead
                if 0 <= t < taps:
                    uses.append((j, t))
            if uses:
                result.append((i, half, uses))
    return result


def add_to(acc, at, term):
    acc[at] = term if acc[at] is None else acc[at] + term


def conv_lane(s0, s4, kb, lane, cols, taps, edge):
    lanes = pl.ds(lane * 128, 128)
    acc = [None] * (cols // 8)
    weights = [kb[t, :, lanes] for t in range(taps)]
    for i, half, uses in tap_uses(cols // 8, taps, edge):
        x = (s4 if half else s0)[pl.ds(8 * i, 8), lanes]
        for j, t in uses:
            add_to(acc, j, weights[t] * x)
    return acc


def row_spec(block, n, width):
    return pl.BlockSpec((block, n, width), lambda i: (i, 0, 0))


def whole_spec(*shape):
    return pl.BlockSpec(shape, lambda i: (0,) * len(shape))


def resident():
    return pl.BlockSpec(memory_space=pltpu.VMEM)


def resident_shape(*shape):
    return pltpu.VMEM(shape, F32)


def params(mib):
    return pltpu.CompilerParams(dimension_semantics=("arbitrary",), vmem_limit_bytes=mib * 2**20)


def inner_kernel(fields_ref, kernel_ref, up_hbm, down_hbm, out_ref, upt_ref, downt_ref, s0, s4, kb, up_ref, down_ref, sems):
    rows, cols, channels = fields_ref.shape
    taps = kernel_ref.shape[0]

    spread_taps(kb, kernel_ref, False)
    s4[...] = jnp.zeros_like(s4)
    copies = [
        pltpu.make_async_copy(up_hbm, up_ref, sems.at[0]),
        pltpu.make_async_copy(down_hbm, down_ref, sems.at[1]),
    ]
    for copy in copies:
        copy.start()

    def one_row(r, carry):
        middle = fields_ref[r].astype(F32)
        s0[...] = middle
        s4[pl.ds(4, cols), :] = middle
        for lane in lane_groups(channels):
            lanes = pl.ds(lane * 128, 128)
            weights = [kb[t, :, lanes] for t in range(taps)]
            acc = [None] * (cols // 8)
            for i in range(cols // 8 + 1):
                for half, ref in ((0, s0), (1, s4)):
                    if half == 0 and i == cols // 8:
                        continue
                    x = ref[pl.ds(8 * i, 8), lanes]
                    for j in range(cols // 8):
                        t = 2 * (i - j) - half + taps // 2
                        if 0 <= t < taps:
                            add_to(acc, j, weights[t] * x)
            for j, value in enumerate(acc):
                out_ref[r, pl.ds(8 * j, 8), lanes] = value
        return carry

    lax.fori_loop(0, rows, one_row, 0)

    for copy in copies:
        copy.wait()
    for j in range(up_ref.shape[1] // 256):
        part = pl.ds(256 * j, 256)
        upt_ref[part, :] = up_ref[:, part].T
        downt_ref[:, part] = down_ref[part, :].T


def inner(fields, kernel, up, down):
    rows, cols, channels = fields.shape
    taps = kernel.shape[0]
    return pl.pallas_call(
        inner_kernel,
        in_specs=[resident()] * 2 + [pl.BlockSpec(memory_space=pltpu.HBM)] * 2,
        out_specs=[resident()] * 3,
        out_shape=[resident_shape(rows, cols, channels), pltpu.VMEM(down.shape, BF16), pltpu.VMEM(up.shape, BF16)],
        scratch_shapes=[
            pltpu.VMEM((cols, channels), F32),
            pltpu.VMEM((cols + 8, channels), F32),
            pltpu.VMEM((taps, 8, channels), F32),
            pltpu.VMEM(up.shape, BF16),
            pltpu.VMEM(down.shape, BF16),
            pltpu.SemaphoreType.DMA((2,)),
        ],
        compiler_params=pltpu.CompilerParams(vmem_limit_bytes=8 * 2**20),
        cost_estimate=pl.CostEstimate(
            flops=260 * taps * rows * cols * channels, transcendentals=0,
            bytes_accessed=rows * cols * channels * 6,
        ),
        name="inner",
    )(fields, kernel, up, down)


def forward_kernel(
    first, last, start, core_ref, inner_ref, left_ref, right_ref, fields_ref, cot_ref, kernel_ref,
    up_ref, upt_ref, down_ref, downt_ref, *refs,
):
    given, refs = ((), refs) if first else (refs[:4], refs[4:])
    (out_ref, grad_ref, gup_ref, gdt_ref, edge_left_ref, edge_right_ref), refs = refs[:6], refs[6:]
    edges, kb, conv_s, normed_s, act_s, hg_s = refs[:6]
    gup_s, gdt_s = refs[6:] if last else (gup_ref, gdt_ref)
    step = pl.program_id(0)
    rows, edge, _ = left_ref.shape
    _, cols, channels = inner_ref.shape
    base_row = start + step * rows
    here = pl.ds(base_row, rows)
    taps = kernel_ref.shape[0]
    hid = up_ref.shape[1]
    cells = rows * cols
    blocks, reach = cols // 8, taps // 2
    width = 256

    @pl.when(step == 0)
    def _():
        spread_taps(kb, kernel_ref, False)
        gup_s[...] = jnp.zeros_like(gup_s) if first else given[2][...]
        gdt_s[...] = jnp.zeros_like(gdt_s) if first else given[3][...]
        edges[...] = jnp.zeros_like(edges)

    def one_row(r, carry):
        left, right = left_ref[r].astype(F32), right_ref[r].astype(F32)
        edges[0] = left
        edges[1, pl.ds(0, edge - 4), :] = left[4:]
        edges[2] = right
        edges[3, pl.ds(4, edge - 4), :] = right[: edge - 4]
        for lane in lane_groups(channels):
            lanes = pl.ds(lane * 128, 128)
            weights = [kb[t, :, lanes] for t in range(taps)]
            acc = [None] * blocks
            for which in range(4):
                for i in range(edge // 8):
                    column = (-edge, 4 - edge, cols, cols - 4)[which] + 8 * i
                    x = None
                    for j in range(blocks):
                        t = (column - 8 * j) // 4 + reach
                        if 0 <= t < taps:
                            if x is None:
                                x = edges[which, pl.ds(8 * i, 8), lanes]
                            add_to(acc, j, weights[t] * x)
            for j, value in enumerate(acc):
                base = inner_ref[base_row + r, pl.ds(8 * j, 8), lanes]
                conv_s[r, pl.ds(8 * j, 8), lanes] = base if value is None else base + value
        return carry

    lax.fori_loop(0, rows, one_row, 0)

    conv = conv_s[...].reshape(cells, channels)
    center = jnp.mean(conv, axis=-1, keepdims=True)
    deviation = conv - center
    spread = jnp.mean(deviation * deviation, axis=-1, keepdims=True)
    inv_scale = lax.rsqrt(spread + 1e-06)
    normed = deviation * inv_scale
    normed_s[...] = normed
    low = normed.astype(BF16)
    cot = cot_ref[...].reshape(cells, channels)
    over_cells = (((0,), (0,)), ((), ()))
    for j in range(hid // width):
        part = pl.ds(j * width, width)
        h = jnp.dot(low, up_ref[:, part], preferred_element_type=F32)
        u = jnp.dot(cot, downt_ref[:, part], preferred_element_type=F32)
        sq = h * h
        t = jnp.tanh(h * (GELU_A + GELU_B * sq))
        half = 0.5 * h
        act_s[:, part] = (half + half * t).astype(BF16)
        slope = (0.5 + 0.5 * t) + half * (1.0 - t * t) * (GELU_A + (3.0 * GELU_B) * sq)
        hg_s[:, part] = (u * slope).astype(BF16)
    out = jnp.dot(act_s[...], down_ref[...], preferred_element_type=F32)
    out = out + fields_ref[here].reshape(cells, channels).astype(F32)
    normed_grad = jnp.dot(hg_s[...], upt_ref[...], preferred_element_type=F32)
    for j in range(hid // width):
        part = pl.ds(j * width, width)
        gup_s[j] += lax.dot_general(low, hg_s[:, part], over_cells, preferred_element_type=F32)
        gdt_s[:, part] += lax.dot_general(cot, act_s[:, part], over_cells, preferred_element_type=F32)
    out_ref[...] = out.astype(BF16).reshape(rows, cols, channels)
    normed = normed_s[...]
    mean_grad = jnp.mean(normed_grad, axis=-1, keepdims=True)
    mean_cross = jnp.mean(normed_grad * normed, axis=-1, keepdims=True)
    grad = inv_scale * (normed_grad - mean_grad - normed * mean_cross)
    grad_ref[here] = grad.reshape(rows, cols, channels)
    edge_left_ref[...] = grad_ref[here, pl.ds(0, edge), :].astype(BF16)
    edge_right_ref[...] = grad_ref[here, pl.ds(cols - edge, edge), :].astype(BF16)

    if last:
        mine_ref, theirs_ref = gup_ref, gdt_ref
        ending = step == pl.num_programs(0) - 1

        @pl.when(ending & (core_ref[0] == 0))
        def _():
            for j in range(hid // width):
                part = pl.ds(j * width, width)
                mine_ref[part, :] = gup_s[j]
                theirs_ref[part, :] = gdt_s[:, part].T.astype(BF16)

        @pl.when(ending & (core_ref[0] == 1))
        def _():
            for j in range(hid // width):
                part = pl.ds(j * width, width)
                theirs_ref[part, :] = gup_s[j].astype(BF16)
                mine_ref[part, :] = gdt_s[:, part].T


def forward(core, conv_inner, left, right, fields, cot, kernel, up, up_t, down, down_t, carried, start, last):
    rows, cols, channels = cot.shape
    count, edge, _ = left.shape
    taps, hid = kernel.shape[0], up.shape[1]
    cells = count * cols
    block = BLOCK
    own = functools.partial(row_spec, block)
    at = lambda n: pl.BlockSpec((block, n, channels), lambda i: (i + start // block, 0, 0))
    anywhere = pl.BlockSpec(memory_space=pl.ANY)
    sums = [(hid // 256, channels, 256), (channels, hid)]
    ends = [((hid, channels), F32), ((hid, channels), BF16)] if last else [(s, F32) for s in sums]
    fixed = [
        pl.BlockSpec(memory_space=pltpu.SMEM),
        resident(), own(edge, channels), own(edge, channels), resident(), at(cols), resident(),
        resident(), resident(), resident(), resident(),
    ]
    return pl.pallas_call(
        functools.partial(forward_kernel, not carried, last, start),
        grid=(count // block,),
        in_specs=fixed + ([anywhere, resident(), resident(), resident()] if carried else []),
        out_specs=[at(cols)] + [resident()] * 3 + [own(edge, channels)] * 2,
        out_shape=[
            jax.ShapeDtypeStruct((rows, cols, channels), BF16),
            resident_shape(rows, cols, channels),
        ]
        + [pltpu.VMEM(s, d) for s, d in ends]
        + [jax.ShapeDtypeStruct((count, edge, channels), BF16)] * 2,
        input_output_aliases={11: 0, 12: 1} if carried else {},
        scratch_shapes=[
            pltpu.VMEM((4, edge, channels), F32),
            pltpu.VMEM((taps, 8, channels), F32),
            pltpu.VMEM((block, cols, channels), F32),
            pltpu.VMEM((block * cols, channels), F32),
            pltpu.VMEM((block * cols, hid), BF16),
            pltpu.VMEM((block * cols, hid), BF16),
        ]
        + ([pltpu.VMEM(s, F32) for s in sums] if last else []),
        compiler_params=params(20),
        cost_estimate=pl.CostEstimate(
            flops=28 * cells * channels * hid, transcendentals=cells * hid,
            bytes_accessed=cells * channels * 12,
        ),
        name="forward",
    )(core, conv_inner, left, right, fields, cot, kernel, up, up_t, down, down_t, *carried)


def kernel_grad_kernel(start, fields_ref, left_ref, right_ref, grad_ref, given_ref, out_ref, s0, s4, sums):
    _, cols, channels = fields_ref.shape
    rows, edge, _ = left_ref.shape
    taps = out_ref.shape[0] - 1
    blocks = cols // 8

    sums[...] = jnp.zeros_like(sums)

    def one_row(r, carry):
        stage_row(s0, s4, left_ref[r], fields_ref[start + r], right_ref[r])
        for lane in lane_groups(channels):
            lanes = pl.ds(lane * 128, 128)
            grads = [grad_ref[start + r, pl.ds(8 * j, 8), lanes] for j in range(blocks)]
            acc = [None] * taps
            for i, half, uses in tap_uses(blocks, taps, edge):
                x = (s4 if half else s0)[pl.ds(8 * i, 8), lanes]
                for j, t in uses:
                    add_to(acc, t, grads[j] * x)
            for t in range(taps):
                sums[t, :, lanes] += acc[t]
        return carry

    lax.fori_loop(0, rows, one_row, 0)

    for t in range(taps):
        here = jnp.sum(sums[t], axis=0, keepdims=True)
        out_ref[pl.ds(t, 1), :] = given_ref[pl.ds(t, 1), :] + here
    out_ref[pl.ds(taps, 1), :] = jnp.zeros((1, channels), F32)


def staging(cols, edge, channels):
    return [
        pltpu.VMEM((cols + 2 * edge, channels), F32),
        pltpu.VMEM((cols + 2 * edge - 8, channels), F32),
    ]


def kernel_grad(fields, left, right, grad, given, start):
    _, cols, channels = fields.shape
    count, edge, _ = left.shape
    taps = given.shape[0] - 1
    return pl.pallas_call(
        functools.partial(kernel_grad_kernel, start),
        in_specs=[resident()] * 5,
        out_specs=resident(),
        out_shape=resident_shape(taps + 1, channels),
        scratch_shapes=staging(cols, edge, channels) + [pltpu.VMEM((taps, 8, channels), F32)],
        compiler_params=pltpu.CompilerParams(vmem_limit_bytes=8 * 2**20),
        cost_estimate=pl.CostEstimate(
            flops=360 * taps * count * cols * channels, transcendentals=0,
            bytes_accessed=count * cols * channels * 8,
        ),
        name="kernel_grad",
    )(fields, left, right, grad, given)


def backward_kernel(start, grad_ref, left_ref, right_ref, cot_ref, kernel_ref, *refs):
    out_ref, s0, s4, kb = refs[-4:]
    _, cols, channels = grad_ref.shape
    rows, edge, _ = left_ref.shape
    base = start + pl.program_id(0) * rows
    taps = kernel_ref.shape[0]

    @pl.when(pl.program_id(0) == 0)
    def _():
        spread_taps(kb, kernel_ref, True)

    def one_row(r, carry):
        stage_row(s0, s4, left_ref[r], grad_ref[base + r], right_ref[r])
        for lane in lane_groups(channels):
            acc = conv_lane(s0, s4, kb, lane, cols, taps, edge)
            lanes = pl.ds(lane * 128, 128)
            back = jnp.concatenate(acc, axis=0) + cot_ref[r, :, lanes].astype(F32)
            out_ref[r, :, lanes] = back.astype(BF16)
        return carry

    lax.fori_loop(0, rows, one_row, 0)


def backward(grad, left, right, cot, kernel, carried, start):
    rows, cols, channels = grad.shape
    count, edge, _ = left.shape
    taps = kernel.shape[0]
    own = functools.partial(row_spec, BLOCK)
    at = pl.BlockSpec((BLOCK, cols, channels), lambda i: (i + start // BLOCK, 0, 0))
    return pl.pallas_call(
        functools.partial(backward_kernel, start),
        grid=(count // BLOCK,),
        in_specs=[resident(), own(edge, channels), own(edge, channels), at, resident()]
        + [pl.BlockSpec(memory_space=pl.ANY)] * len(carried),
        out_specs=at,
        out_shape=jax.ShapeDtypeStruct((rows, cols, channels), BF16),
        input_output_aliases={5: 0} if carried else {},
        scratch_shapes=staging(cols, edge, channels) + [pltpu.VMEM((taps, 8, channels), F32)],
        compiler_params=params(8),
        cost_estimate=pl.CostEstimate(
            flops=360 * taps * count * cols * channels, transcendentals=0,
            bytes_accessed=count * cols * channels * 10,
        ),
        name="backward",
    )(grad, left, right, cot, kernel, *carried)


def after(values, *others):
    held, _ = lax.optimization_barrier((values, others))
    return held


def chunk_starts(rows):
    half = rows // 2 // BLOCK * BLOCK
    return [0, half, rows]


def with_places(fields):
    found = groups()
    core = found[0][0][0]
    fields, places, index, even = lax.optimization_barrier(
        (fields, [places for places, _ in found], core.astype(jnp.int32).reshape(1), core == 0)
    )
    return fields, [(p, masks) for p, (_, masks) in zip(places, found)], index, even


def per_device(fields, cotangent, kernel, up_weight, down_weight):
    rows, cols, channels = fields.shape
    taps, hid = kernel.shape[0], up_weight.shape[1]
    edge = -(-KERNEL_SPACING * (taps // 2) // 8) * 8
    fields, (core, plane, depth), index, even = with_places(fields)
    bounds = chunk_starts(rows)
    chunks = list(zip(bounds[:-1], bounds[1:]))
    halos = []
    source, conv_inner = fields, None
    for begin, end in chunks:
        to_right, to_left = source[begin:end, cols - edge :], source[begin:end, :edge]
        halos.append((passed_along(to_right, 1), passed_along(to_left, -1)))
        if conv_inner is None:
            held = after(fields, to_right, to_left)
            conv_inner, up_t, down_t = inner(held, kernel, up_weight, down_weight)
            source = after(fields, conv_inner)
    carried = ()
    grad_halos = []
    for (begin, end), (left, right) in zip(chunks, halos):
        *carried, edge_left, edge_right = forward(
            index, conv_inner, left, right, fields, cotangent, kernel, up_weight, up_t, down_weight, down_t,
            carried, begin, end == rows,
        )
        if end < rows:
            grad_halos.append((passed_along(edge_right, 1), passed_along(edge_left, -1)))
    output, grad, mine, theirs = carried

    kgrad = jnp.zeros((taps + 1, channels), F32)

    def add_kernel_grad(total, which):
        left, right = halos[which]
        return kernel_grad(fields, left, right, grad, total, chunks[which][0])

    def add_field_grad(so_far, which):
        left, right = grad_halos[which]
        return (backward(grad, left, right, cotangent, kernel, so_far, chunks[which][0]),)

    theirs = after(theirs, grad_halos[0])
    part = mine + xor_permute(theirs, core[1][1]).astype(F32)
    sends, total = scatter_stage(part, plane)
    kgrad = after(kgrad, *sends)
    kgrad = add_kernel_grad(kgrad, 0)
    part = scatter_finish(sends, total, plane)
    part, edge_left, edge_right = lax.optimization_barrier((part, edge_left, edge_right))
    grad_halos.append((passed_along(edge_right, 1), passed_along(edge_left, -1)))
    sends, total = scatter_stage(part, depth)
    sends, kgrad = lax.optimization_barrier((sends, kgrad))
    kgrad = add_kernel_grad(kgrad, 1)
    part = scatter_finish(sends, total, depth).astype(BF16)
    packed = pack(part, kgrad)
    packed, halo = lax.optimization_barrier((packed, grad_halos[0]))
    grad_halos[0] = halo
    field_grad = add_field_grad((), 0)
    part, kgrad = gather_finish(packed, kgrad, depth)
    packed, field_grad, halo = lax.optimization_barrier((pack(part, kgrad), field_grad, grad_halos[1]))
    grad_halos[1] = halo
    field_grad = add_field_grad(field_grad, 1)
    part, kgrad = gather_finish(packed, kgrad, plane)
    packed = after(pack(part, kgrad), field_grad)
    got = xor_permute(packed, core[1][1])
    kgrad = kgrad + got[hid:].astype(F32)
    part = packed[:hid]
    factor = 1.0 / math.sqrt(rows * cols * lax.axis_size("lon") * lax.axis_size("lat"))
    got = got[:hid]
    gup = jnp.where(even, part, got).astype(F32) * factor
    gdown = jnp.where(even, got, part).astype(F32) * factor
    up_grad = gup.reshape(hid // 256, channels, 256).transpose(1, 0, 2).reshape(channels, hid)
    return (output, field_grad[0], kgrad[:taps] * factor, up_grad, gdown)


def solution(mesh):
    placed = (P("lat", "lon", None), P("lat", "lon", None), P(), P(), P())
    return jax.shard_map(
        per_device,
        mesh=mesh,
        in_specs=placed,
        out_specs=(P("lat", "lon", None), P("lat", "lon", None), P(), P(), P()),
        check_vma=False,
    )
```

time: 283 us -> 99.4 us (0.35)
  other arithmetic: 72.4 us -> 2.09 us
  waiting for transfers between devices: 65.1 us -> 7.05 us
  blocking collectives: 56 us -> 0 us
  Pallas kernels: 0 us -> 49 us
  matrix products: 38.9 us -> 0 us
  between operations: 14.3 us -> 0.98 us
  starting transfers between devices: 23.9 us -> 35.1 us
  local copies, waits for them, and re-layouts: 11.7 us -> 4.99 us
    psum x1 -> x0, blocking collectives: 56 us -> none  [per_device(): summed = lax.psum((kernel_terms, grad_up, grad_down), ('lon', 'lat'))]
    pallas_call x0 -> x7, Pallas kernels: none -> 49 us  [the longest x2 24 us: forward(): pl.pallas_call(functools.partial(forward_kernel, not carried, last, start...]
    psum x1 -> x0, waiting for transfers between devices: 45.9 us -> none  [per_device(): summed = lax.psum((kernel_terms, grad_up, grad_down), ('lon', 'lat'))]
    dot_general x6 -> x0, matrix products: 38.9 us -> none  [the longest x1 15.9 us: per_device(): lax.dot_general(flat_cot, down_weight, contract_last, preferred_element_t...]
    reduce_sum x4 -> x0, other arithmetic: 38.2 us -> none  [the longest x2 18.9 us: per_device(): jnp.sum(wrapped_input[:, KERNEL_SPACING * index_of_tap:KERNEL_SPACING * i...]
    convert_element_type x2 -> x4, other arithmetic: 26.2 us -> 0.06 us  [the longest x3 0.04 us: pack(): return jnp.concatenate([value, extra.astype(BF16)], axis=0)]
    ppermute x4 -> x22, waiting for transfers between devices: 19.2 us -> 7.05 us  [the longest x14 7.02 us: xor_permute(): return lax.ppermute(value, AXES, pairs)]
    ppermute x4 -> x22, starting transfers between devices: 23.9 us -> 35.1 us  [the longest x8 19 us: passed_along(): lax.ppermute(value, 'lon', [(i, (i + by) % count) for i in range(count)])]
  transfers between devices with their start and end apart: 5 -> 22, of which waited for: 2 -> 6; matrix products, arithmetic and copies ran while one was open for 14% -> 0% of each run, Pallas kernels for 0% -> 49%
where the time goes in v2:
time: 99.4 us; the launch traced here: 99.1 us
  Pallas kernels  49 us (49%)
  starting transfers between devices  35.1 us (35%)
  waiting for transfers between devices  7.05 us (7%)
  local copies, waits for them, and re-layouts  4.99 us (5%)
  other arithmetic  2.09 us (2%)
    pallas_call x2, Pallas kernels, forward(): pl.pallas_call(functools.partial(forward_kernel, not carried, last, start...  24 us
    ppermute x8, starting transfers between devices, passed_along(): lax.ppermute(value, 'lon', [(i, (i + by) % count) for i in range(count)])  19 us
    ppermute x14, starting transfers between devices, xor_permute(): return lax.ppermute(value, AXES, pairs)  16.1 us
    pallas_call x2, Pallas kernels, backward(): pl.pallas_call(functools.partial(backward_kernel, start), grid=(count //...  10 us
    pallas_call x2, Pallas kernels, kernel_grad(): pl.pallas_call(functools.partial(kernel_grad_kernel, start), in_specs=[re...  8.65 us
    ppermute x14, waiting for transfers between devices, xor_permute(): return lax.ppermute(value, AXES, pairs)  7.02 us
    pallas_call x1, Pallas kernels, inner(): pl.pallas_call(inner_kernel, in_specs=[resident()] * 2 + [pl.BlockSpec(me...  6.26 us
    unnamed x14, local copies, waits for them, and re-layouts  2.11 us
  transfers between devices with their start and end apart: 22, of which 6 were waited for; matrix products, arithmetic and copies ran while one was open for 0% of the time, Pallas kernels for 49%

profile of v2, /device:TPU:0, one launch (start us, length us, event | category | flops | bytes accessed | tf_op | source)
XLA Modules:
  0.0 99.1 jit_solution(6119764309145706388)
XLA Ops:
  0.6 0.0 copy-start
  0.6 0.0 copy-start.6
  0.7 1.4 %fusion.21 = (bf16[16,64,256]{2,1,0:T(8,128)(2,1)S(1)}, bf16[16,64,256]{2,1,0:T(8,128)(2,1)S(1)}) fusion(bf16[32,112,256]{2,1,0:T(8,128)(2,1)} %fields_ref.4), kind=kLoop, calls=%fused_computation.46 | loop fusion | bytes 2097152 | tf_op jit(solution)/shard_map/slice | solution.py:511
  2.1 0.5 collective-permute-start.2
  2.6 5.0 %collective-permute-start.3 = (bf16[16,64,256]{2,1,0:T(8,128)(2,1)S(1)}, bf16[16,64,256]{2,1,0:T(8,128)(2,1)S(1)}, u32[]{:S(2)}, u32[]{:S(2)}) collective-permute-start(bf16[16,64,256]{2,1,0:T(8,128)(2,1)S(1)} %get-tuple-element.99), channel_id=1, source_target_pairs={{0,30},{2,0},{4,2},{6,4},{8,6},{10,8},{12,10},{14,12},{16,14},{18,... | collective-permute-start | bytes 1572872 | tf_op jit(solution)/shard_map/ppermute | solution.py:33
  7.6 0.0 copy-done
  7.6 1.0 %copy-done.2 = bf16[256,1024]{1,0:T(8,128)(2,1)S(1)} copy-done((bf16[256,1024]{1,0:T(8,128)(2,1)S(1)}, bf16[256,1024]{1,0:T(8,128)(2,1)}, u32[]{:S(2)}) %copy-start.2) | copy-done | bytes 524312
  8.7 1.0 %copy-done.4 = bf16[1024,256]{1,0:T(8,128)(2,1)S(1)} copy-done((bf16[1024,256]{1,0:T(8,128)(2,1)S(1)}, bf16[1024,256]{1,0:T(8,128)(2,1)}, u32[]{:S(2)}) %copy-start.4) | copy-done | bytes 524312
  9.7 6.3 %inner.1 = (f32[32,112,256]{2,1,0:T(8,128)S(1)}, bf16[1024,256]{1,0:T(8,128)(2,1)S(1)}, bf16[256,1024]{1,0:T(8,128)(2,1)S(1)}) custom-call(bf16[32,112,256]{2,1,0:T(8,128)(2,1)S(1)} %copy-done, f32[31,256]{1,0:T(8,128)S(1)} %copy-done.6, bf16[256,1024]{1,0:T(8,128)(2,1)S(1)} %copy-done.2, bf16[1024,256]{1,0:T(8,128)(2,1)S(1)} %copy-done.4), custom_call_target="tpu_custom_call" | custom-call | flops 7395082240 | bytes 5505024 | tf_op jit(solution)/shard_map/inner/pallas_call | solution.py:203
  16.0 0.0 copy-start.1
  16.0 0.1 fusion.20
  16.1 0.1 collective-permute-start
  16.2 4.4 %collective-permute-start.1 = (bf16[16,64,256]{2,1,0:T(8,128)(2,1)S(1)}, bf16[16,64,256]{2,1,0:T(8,128)(2,1)S(1)}, u32[]{:S(2)}, u32[]{:S(2)}) collective-permute-start(bf16[16,64,256]{2,1,0:T(8,128)(2,1)S(1)} %get-tuple-element.97), channel_id=1, source_target_pairs={{0,30},{2,0},{4,2},{6,4},{8,6},{10,8},{12,10},{14,12},{16,14},{18,... | collective-permute-start | bytes 1572872 | tf_op jit(solution)/shard_map/ppermute | solution.py:33
  20.6 0.0 collective-permute-done.2.left_ref
  20.6 0.0 collective-permute-done.3.right_ref
  20.7 11.7 %forward.2 = (bf16[32,112,256]{2,1,0:T(8,128)(2,1)}, f32[32,112,256]{2,1,0:T(8,128)S(1)}, f32[4,256,256]{2,1,0:T(8,128)S(1)}, f32[256,1024]{1,0:T(8,128)S(1)}, b...) custom-call(s32[1]{0:T(128)} %bitcast.core_ref, f32[32,112,256]{2,1,0:T(8,128)S(1)} %get-tuple-element.53.inner_ref, ...), custom_call_target="tpu_custom_call" | custom-call | flops 13153337344 | bytes 5505024 | tf_op jit(solution)/shard_map/forward/pallas_call | solution.py:349
  32.3 0.0 collective-permute-start.4
  32.3 4.4 %collective-permute-start.5 = (bf16[16,64,256]{2,1,0:T(8,128)(2,1)S(1)}, bf16[16,64,256]{2,1,0:T(8,128)(2,1)S(1)}, u32[]{:S(2)}, u32[]{:S(2)}) collective-permute-start(bf16[16,64,256]{2,1,0:T(8,128)(2,1)S(1)} %get-tuple-element.66), channel_id=1, source_target_pairs={{0,30},{2,0},{4,2},{6,4},{8,6},{10,8},{12,10},{14,12},{16,14},{18,... | collective-permute-start | bytes 1572872 | tf_op jit(solution)/shard_map/ppermute | solution.py:33
  36.8 0.0 collective-permute-done.left_ref
  36.8 0.0 collective-permute-done.1.right_ref
  36.8 12.4 %forward.3 = (bf16[32,112,256]{2,1,0:T(8,128)(2,1)}, f32[32,112,256]{2,1,0:T(8,128)S(1)}, f32[1024,256]{1,0:T(8,128)S(1)}, bf16[1024,256]{1,0:T(8,128)(2,1)S(1)}...) custom-call(s32[1]{0:T(128)} %bitcast.core_ref, ...), custom_call_target="tpu_custom_call", output_to_operand_aliasing={{0}: (11, {}), {1}: (12, {})} | custom-call | flops 13153337344 | bytes 5505024 | tf_op jit(solution)/shard_map/forward/pallas_call | solution.py:349
  49.1 0.0 collective-permute-done.4.left_ref
  49.1 0.0 collective-permute-done.5.right_ref
  49.1 0.0 collective-permute-start.6
  49.2 1.9 %collective-permute-done.6 = bf16[1024,256]{1,0:T(8,128)(2,1)S(1)} collective-permute-done((bf16[1024,256]{1,0:T(8,128)(2,1)S(1)}, bf16[1024,256]{1,0:T(8,128)(2,1)S(1)}, u32[]{:S(2)}, u32[]{:S(2)}) %collective-permute-start.6) | collective-permute-done | bytes 524320 | tf_op jit(solution)/shard_map/ppermute | solution.py:28
  51.1 0.1 convert_add_fusion
  51.2 0.1 collective-permute-start.7
  51.3 2.0 %collective-permute-start.8 = (bf16[256,256]{1,0:T(8,128)(2,1)S(1)}, bf16[256,256]{1,0:T(8,128)(2,1)S(1)}, u32[]{:S(2)}, u32[]{:S(2)}) collective-permute-start(bf16[256,256]{1,0:T(8,128)(2,1)S(1)} %get-tuple-element.105), channel_id=1, source_target_pairs={{0,1},{1,0},{2,3},{3,2},{4,5},{5,4},{6,7},{7,6},{8,9},{9,8},{10,11... | collective-permute-start | bytes 393224 | tf_op jit(solution)/shard_map/ppermute | solution.py:28
  53.3 1.5 %collective-permute-start.9 = (bf16[256,256]{1,0:T(8,128)(2,1)S(1)}, bf16[256,256]{1,0:T(8,128)(2,1)S(1)}, u32[]{:S(2)}, u32[]{:S(2)}) collective-permute-start(bf16[256,256]{1,0:T(8,128)(2,1)S(1)} %get-tuple-element.104), channel_id=1, source_target_pairs={{0,5},{1,4},{2,7},{3,6},{4,1},{5,0},{6,3},{7,2},{8,13},{9,12},{10,... | collective-permute-start | bytes 393224 | tf_op jit(solution)/shard_map/ppermute | solution.py:28
  54.8 4.3 %kernel_grad.2.given_ref = f32[32,256]{1,0:T(8,128)S(1)} custom-call(bf16[32,112,256]{2,1,0:T(8,128)(2,1)S(1)} %copy-done, bf16[16,64,256]{2,1,0:T(8,128)(2,1)S(1)} %collective-permute-done.2.left_ref, bf16[16,64,256]{2,1,0:T(8,128)(2,1)S(1)} %collective-permute-done.3.right_ref, f32[32,112,256]{2,1,0:T(8,128)S(1)} %get-tuple-element.62.grad_ref, ...), custom_call_target="tpu_custom_call" | custom-call | flops 5119672320 | bytes 3670016 | tf_op jit(solution)/shard_map/kernel_grad/pallas_call | solution.py:420
  59.1 0.0 collective-permute-done.7
  59.1 0.1 collective-permute-done.8
  59.2 1.8 %collective-permute-done.9 = bf16[256,256]{1,0:T(8,128)(2,1)S(1)} collective-permute-done((bf16[256,256]{1,0:T(8,128)(2,1)S(1)}, bf16[256,256]{1,0:T(8,128)(2,1)S(1)}, u32[]{:S(2)}, u32[]{:S(2)}) %collective-permute-start.9) | collective-permute-done | bytes 131104 | tf_op jit(solution)/shard_map/ppermute | solution.py:28
  61.0 0.1 fusion.1
  61.1 0.1 collective-permute-start.10
  61.2 0.1 collective-permute-start.11
  61.3 4.3 %collective-permute-start.12 = (bf16[64,256]{1,0:T(8,128)(2,1)S(1)}, bf16[64,256]{1,0:T(8,128)(2,1)S(1)}, u32[]{:S(2)}, u32[]{:S(2)}) collective-permute-start(bf16[64,256]{1,0:T(8,128)(2,1)S(1)} %get-tuple-element.82), channel_id=1, source_target_pairs={{0,24},{1,25},{2,26},{3,27},{4,28},{5,29},{6,30},{7,31},{8,16},{9,... | collective-permute-start | bytes 98312 | tf_op jit(solution)/shard_map/ppermute | solution.py:28
  65.6 4.3 %kernel_grad.3 = f32[32,256]{1,0:T(8,128)S(1)} custom-call(bf16[32,112,256]{2,1,0:T(8,128)(2,1)S(1)} %copy-done, bf16[16,64,256]{2,1,0:T(8,128)(2,1)S(1)} %collective-permute-done.left_ref, bf16[16,64,256]{2,1,0:T(8,128)(2,1)S(1)} %collective-permute-done.1.right_ref, f32[32,112,256]{2,1,0:T(8,128)S(1)} %get-tuple-element.62.grad_ref, ...), custom_call_target="tpu_custom_call" | custom-call | flops 5119672320 | bytes 3670016 | tf_op jit(solution)/shard_map/kernel_grad/pallas_call | solution.py:420
  69.9 0.1 collective-permute-start.16
  70.0 4.4 %collective-permute-start.17 = (bf16[16,64,256]{2,1,0:T(8,128)(2,1)S(1)}, bf16[16,64,256]{2,1,0:T(8,128)(2,1)S(1)}, u32[]{:S(2)}, u32[]{:S(2)}) collective-permute-start(bf16[16,64,256]{2,1,0:T(8,128)(2,1)S(1)} %get-tuple-element.88), channel_id=1, source_target_pairs={{0,30},{2,0},{4,2},{6,4},{8,6},{10,8},{12,10},{14,12},{16,14},{18,... | collective-permute-start | bytes 1572872 | tf_op jit(solution)/shard_map/ppermute | solution.py:33
  74.4 0.0 collective-permute-done.10
  74.4 0.0 collective-permute-done.11
  74.4 0.0 collective-permute-done.12
  74.4 0.1 collective-permute-start.13
  74.5 0.1 collective-permute-start.14
  74.6 4.3 %collective-permute-start.15 = (bf16[96,256]{1,0:T(8,128)(2,1)S(1)}, bf16[96,256]{1,0:T(8,128)(2,1)S(1)}, u32[]{:S(2)}, u32[]{:S(2)}) collective-permute-start(bf16[96,256]{1,0:T(8,128)(2,1)S(1)} %pad_maximum_fusion.2), channel_id=1, source_target_pairs={{0,24},{1,25},{2,26},{3,27},{4,28},{5,29},{6,30},{7,31},{8,16},{9,... | collective-permute-start | bytes 147464 | tf_op jit(solution)/shard_map/ppermute | solution.py:28
  78.9 5.0 %backward.2.refs_0_ = bf16[32,112,256]{2,1,0:T(8,128)(2,1)} custom-call(f32[32,112,256]{2,1,0:T(8,128)S(1)} %get-tuple-element.62.grad_ref, bf16[16,64,256]{2,1,0:T(8,128)(2,1)S(1)} %collective-permute-done.4.left_ref, bf16[16,64,256]{2,1,0:T(8,128)(2,1)S(1)} %collective-permute-done.5.right_ref, bf16[32,112,256]{2,1,0:T(8,128)(2,1)S(1)} %copy-done.1, ...), custom_call_target="tpu_custom_call" | custom-call | flops 5119672320 | bytes 4587520 | tf_op jit(solution)/shard_map/backward/pallas_call | solution.py:464
  84.0 0.0 collective-permute-done.13
  84.0 0.0 collective-permute-done.14
  84.0 0.0 collective-permute-done.15
  84.1 0.0 collective-permute-done.16.left_ref
  84.1 0.0 collective-permute-done.17.right_ref
  84.1 1.1 %collective-permute-start.18 = (bf16[288,256]{1,0:T(8,128)(2,1)S(1)}, bf16[288,256]{1,0:T(8,128)(2,1)S(1)}, u32[]{:S(2)}, u32[]{:S(2)}) collective-permute-start(bf16[288,256]{1,0:T(8,128)(2,1)S(1)} %pad_maximum_fusion.1), channel_id=1, source_target_pairs={{0,4},{1,5},{2,6},{3,7},{4,0},{5,1},{6,2},{7,3},{8,12},{9,13},{10,... | collective-permute-start | bytes 442376 | tf_op jit(solution)/shard_map/ppermute | solution.py:28
  85.2 1.3 %collective-permute-start.19 = (bf16[288,256]{1,0:T(8,128)(2,1)S(1)}, bf16[288,256]{1,0:T(8,128)(2,1)S(1)}, u32[]{:S(2)}, u32[]{:S(2)}) collective-permute-start(bf16[288,256]{1,0:T(8,128)(2,1)S(1)} %pad_maximum_fusion.1), channel_id=1, source_target_pairs={{0,1},{1,0},{2,3},{3,2},{4,5},{5,4},{6,7},{7,6},{8,9},{9,8},{10,11... | collective-permute-start | bytes 442376 | tf_op jit(solution)/shard_map/ppermute | solution.py:28
  86.5 1.2 %collective-permute-start.20 = (bf16[288,256]{1,0:T(8,128)(2,1)S(1)}, bf16[288,256]{1,0:T(8,128)(2,1)S(1)}, u32[]{:S(2)}, u32[]{:S(2)}) collective-permute-start(bf16[288,256]{1,0:T(8,128)(2,1)S(1)} %pad_maximum_fusion.1), channel_id=1, source_target_pairs={{0,5},{1,4},{2,7},{3,6},{4,1},{5,0},{6,3},{7,2},{8,13},{9,12},{10,... | collective-permute-start | bytes 442376 | tf_op jit(solution)/shard_map/ppermute | solution.py:28
  87.6 5.0 %backward.3 = bf16[32,112,256]{2,1,0:T(8,128)(2,1)} custom-call(f32[32,112,256]{2,1,0:T(8,128)S(1)} %get-tuple-element.62.grad_ref, bf16[16,64,256]{2,1,0:T(8,128)(2,1)S(1)} %collective-permute-done.16.left_ref, bf16[16,64,256]{2,1,0:T(8,128)(2,1)S(1)} %collective-permute-done.17.right_ref, ...), custom_call_target="tpu_custom_call", output_to_operand_aliasing={{}: (5, {})} | custom-call | flops 5119672320 | bytes 4587520 | tf_op jit(solution)/shard_map/backward/pallas_call | solution.py:464
  92.7 0.0 collective-permute-done.18
  92.8 0.3 collective-permute-done.19
  93.1 1.0 %collective-permute-done.20 = bf16[288,256]{1,0:T(8,128)(2,1)S(1)} collective-permute-done((bf16[288,256]{1,0:T(8,128)(2,1)S(1)}, bf16[288,256]{1,0:T(8,128)(2,1)S(1)}, u32[]{:S(2)}, u32[]{:S(2)}) %collective-permute-start.20) | collective-permute-done | bytes 147488 | tf_op jit(solution)/shard_map/ppermute | solution.py:28
  94.2 0.1 collective-permute-start.21
  94.3 1.9 %collective-permute-done.21 = bf16[1056,256]{1,0:T(8,128)(2,1)S(1)} collective-permute-done((bf16[1056,256]{1,0:T(8,128)(2,1)S(1)}, bf16[1056,256]{1,0:T(8,128)(2,1)S(1)}, u32[]{:S(2)}, u32[]{:S(2)}) %collective-permute-start.21) | collective-permute-done | bytes 540704 | tf_op jit(solution)/shard_map/ppermute | solution.py:28
  96.2 1.2 %convert_multiply_fusion = (f32[1024,256]{1,0:T(8,128)}, f32[1024,256]{1,0:T(8,128)S(1)}) fusion(pred[]{:T(512)S(6)} %eq.3, bf16[1056,256]{1,0:T(8,128)(2,1)S(1)} %collective-permute-done.21, bf16[1056,256]{1,0:T(8,128)(2,1)S(1)} %pad_maximum_fusion), kind=kLoop, calls=%fused_computation | loop fusion | flops 1572864 | bytes 3145729 | tf_op jit(solution)/shard_map/mul | solution.py:566
  97.4 1.1 %copy.14 = f32[4,32,8,256]{3,2,0,1:T(8,128)} copy(f32[4,32,8,256]{3,2,1,0:T(8,128)S(1)} %bitcast.64) | data formatting | bytes 2097152 | tf_op jit(solution)/shard_map/reshape | solution.py:567
  98.5 0.6 fusion.14
  (29 shorter events, 0.3 us)
Async XLA Ops:
  0.6 7.0 %copy-start = (bf16[32,112,256]{2,1,0:T(8,128)(2,1)S(1)}, bf16[32,112,256]{2,1,0:T(8,128)(2,1)}, u32[]{:S(2)}) copy-start(bf16[32,112,256]{2,1,0:T(8,128)(2,1)} %fields_ref.4) | copy-start | bytes 5505028
  0.6 7.0 %copy-start.6 = (f32[31,256]{1,0:T(8,128)S(1)}, f32[31,256]{1,0:T(8,128)}, u32[]{:S(2)}) copy-start(f32[31,256]{1,0:T(8,128)} %kernel_ref.9) | copy-start | bytes 95236
  2.1 18.5 %collective-permute-start.2 = (bf16[16,64,256]{2,1,0:T(8,128)(2,1)S(1)}, bf16[16,64,256]{2,1,0:T(8,128)(2,1)S(1)}, u32[]{:S(2)}, u32[]{:S(2)}) collective-permute-start(bf16[16,64,256]{2,1,0:T(8,128)(2,1)S(1)} %get-tuple-element.100), channel_id=1, source_target_pairs={{0,2},{2,4},{4,6},{6,8},{8,10},{10,12},{12,14},{14,16},{16,18},{18... | collective-permute-start | bytes 1572872 | tf_op jit(solution)/shard_map/ppermute | solution.py:33
  2.6 18.0 %collective-permute-start.3 = (bf16[16,64,256]{2,1,0:T(8,128)(2,1)S(1)}, bf16[16,64,256]{2,1,0:T(8,128)(2,1)S(1)}, u32[]{:S(2)}, u32[]{:S(2)}) collective-permute-start(bf16[16,64,256]{2,1,0:T(8,128)(2,1)S(1)} %get-tuple-element.99), channel_id=1, source_target_pairs={{0,30},{2,0},{4,2},{6,4},{8,6},{10,8},{12,10},{14,12},{16,14},{18,... | collective-permute-start | bytes 1572872 | tf_op jit(solution)/shard_map/ppermute | solution.py:33
  7.6 1.0 %copy-start.2 = (bf16[256,1024]{1,0:T(8,128)(2,1)S(1)}, bf16[256,1024]{1,0:T(8,128)(2,1)}, u32[]{:S(2)}) copy-start(bf16[256,1024]{1,0:T(8,128)(2,1)} %up_ref.3) | copy-start | bytes 1572868
  8.7 1.0 %copy-start.4 = (bf16[1024,256]{1,0:T(8,128)(2,1)S(1)}, bf16[1024,256]{1,0:T(8,128)(2,1)}, u32[]{:S(2)}) copy-start(bf16[1024,256]{1,0:T(8,128)(2,1)} %down_ref.3) | copy-start | bytes 1572868
  9.7 10.9 %copy-start.3 = (bf16[256,1024]{1,0:T(8,128)(2,1)S(1)}, bf16[256,1024]{1,0:T(8,128)(2,1)}, u32[]{:S(2)}) copy-start(bf16[256,1024]{1,0:T(8,128)(2,1)} %up_ref.3) | copy-start | bytes 1572868
  9.7 10.9 %copy-start.5 = (bf16[1024,256]{1,0:T(8,128)(2,1)S(1)}, bf16[1024,256]{1,0:T(8,128)(2,1)}, u32[]{:S(2)}) copy-start(bf16[1024,256]{1,0:T(8,128)(2,1)} %down_ref.3) | copy-start | bytes 1572868
  16.0 4.7 %copy-start.1 = (bf16[32,112,256]{2,1,0:T(8,128)(2,1)S(1)}, bf16[32,112,256]{2,1,0:T(8,128)(2,1)}, u32[]{:S(2)}) copy-start(bf16[32,112,256]{2,1,0:T(8,128)(2,1)} %cot_ref.7) | copy-start | bytes 5505028
  16.1 20.6 %collective-permute-start = (bf16[16,64,256]{2,1,0:T(8,128)(2,1)S(1)}, bf16[16,64,256]{2,1,0:T(8,128)(2,1)S(1)}, u32[]{:S(2)}, u32[]{:S(2)}) collective-permute-start(bf16[16,64,256]{2,1,0:T(8,128)(2,1)S(1)} %get-tuple-element.98), channel_id=1, source_target_pairs={{0,2},{2,4},{4,6},{6,8},{8,10},{10,12},{12,14},{14,16},{16,18},{18... | collective-permute-start | bytes 1572872 | tf_op jit(solution)/shard_map/ppermute | solution.py:33
  16.2 20.6 %collective-permute-start.1 = (bf16[16,64,256]{2,1,0:T(8,128)(2,1)S(1)}, bf16[16,64,256]{2,1,0:T(8,128)(2,1)S(1)}, u32[]{:S(2)}, u32[]{:S(2)}) collective-permute-start(bf16[16,64,256]{2,1,0:T(8,128)(2,1)S(1)} %get-tuple-element.97), channel_id=1, source_target_pairs={{0,30},{2,0},{4,2},{6,4},{8,6},{10,8},{12,10},{14,12},{16,14},{18,... | collective-permute-start | bytes 1572872 | tf_op jit(solution)/shard_map/ppermute | solution.py:33
  32.3 16.8 %collective-permute-start.4 = (bf16[16,64,256]{2,1,0:T(8,128)(2,1)S(1)}, bf16[16,64,256]{2,1,0:T(8,128)(2,1)S(1)}, u32[]{:S(2)}, u32[]{:S(2)}) collective-permute-start(bf16[16,64,256]{2,1,0:T(8,128)(2,1)S(1)} %get-tuple-element.65), channel_id=1, source_target_pairs={{0,2},{2,4},{4,6},{6,8},{8,10},{10,12},{12,14},{14,16},{16,18},{18... | collective-permute-start | bytes 1572872 | tf_op jit(solution)/shard_map/ppermute | solution.py:33
  32.3 16.8 %collective-permute-start.5 = (bf16[16,64,256]{2,1,0:T(8,128)(2,1)S(1)}, bf16[16,64,256]{2,1,0:T(8,128)(2,1)S(1)}, u32[]{:S(2)}, u32[]{:S(2)}) collective-permute-start(bf16[16,64,256]{2,1,0:T(8,128)(2,1)S(1)} %get-tuple-element.66), channel_id=1, source_target_pairs={{0,30},{2,0},{4,2},{6,4},{8,6},{10,8},{12,10},{14,12},{16,14},{18,... | collective-permute-start | bytes 1572872 | tf_op jit(solution)/shard_map/ppermute | solution.py:33
  49.1 1.9 %collective-permute-start.6 = (bf16[1024,256]{1,0:T(8,128)(2,1)S(1)}, bf16[1024,256]{1,0:T(8,128)(2,1)S(1)}, u32[]{:S(2)}, u32[]{:S(2)}) collective-permute-start(bf16[1024,256]{1,0:T(8,128)(2,1)S(1)} %get-tuple-element.67), channel_id=1, source_target_pairs={{0,2},{1,3},{2,0},{3,1},{4,6},{5,7},{6,4},{7,5},{8,10},{9,11},{10,... | collective-permute-start | bytes 1572872 | tf_op jit(solution)/shard_map/ppermute | solution.py:28
  51.2 7.9 %collective-permute-start.7 = (bf16[256,256]{1,0:T(8,128)(2,1)S(1)}, bf16[256,256]{1,0:T(8,128)(2,1)S(1)}, u32[]{:S(2)}, u32[]{:S(2)}) collective-permute-start(bf16[256,256]{1,0:T(8,128)(2,1)S(1)} %get-tuple-element.103), channel_id=1, source_target_pairs={{0,4},{1,5},{2,6},{3,7},{4,0},{5,1},{6,2},{7,3},{8,12},{9,13},{10,... | collective-permute-start | bytes 393224 | tf_op jit(solution)/shard_map/ppermute | solution.py:28
  51.3 7.9 %collective-permute-start.8 = (bf16[256,256]{1,0:T(8,128)(2,1)S(1)}, bf16[256,256]{1,0:T(8,128)(2,1)S(1)}, u32[]{:S(2)}, u32[]{:S(2)}) collective-permute-start(bf16[256,256]{1,0:T(8,128)(2,1)S(1)} %get-tuple-element.105), channel_id=1, source_target_pairs={{0,1},{1,0},{2,3},{3,2},{4,5},{5,4},{6,7},{7,6},{8,9},{9,8},{10,11... | collective-permute-start | bytes 393224 | tf_op jit(solution)/shard_map/ppermute | solution.py:28
  53.3 7.7 %collective-permute-start.9 = (bf16[256,256]{1,0:T(8,128)(2,1)S(1)}, bf16[256,256]{1,0:T(8,128)(2,1)S(1)}, u32[]{:S(2)}, u32[]{:S(2)}) collective-permute-start(bf16[256,256]{1,0:T(8,128)(2,1)S(1)} %get-tuple-element.104), channel_id=1, source_target_pairs={{0,5},{1,4},{2,7},{3,6},{4,1},{5,0},{6,3},{7,2},{8,13},{9,12},{10,... | collective-permute-start | bytes 393224 | tf_op jit(solution)/shard_map/ppermute | solution.py:28
  61.1 13.3 %collective-permute-start.10 = (bf16[64,256]{1,0:T(8,128)(2,1)S(1)}, bf16[64,256]{1,0:T(8,128)(2,1)S(1)}, u32[]{:S(2)}, u32[]{:S(2)}) collective-permute-start(bf16[64,256]{1,0:T(8,128)(2,1)S(1)} %get-tuple-element.80), channel_id=1, source_target_pairs={{0,8},{1,9},{2,10},{3,11},{4,12},{5,13},{6,14},{7,15},{8,0},{9,1},... | collective-permute-start | bytes 98312 | tf_op jit(solution)/shard_map/ppermute | solution.py:28
  61.2 13.2 %collective-permute-start.11 = (bf16[64,256]{1,0:T(8,128)(2,1)S(1)}, bf16[64,256]{1,0:T(8,128)(2,1)S(1)}, u32[]{:S(2)}, u32[]{:S(2)}) collective-permute-start(bf16[64,256]{1,0:T(8,128)(2,1)S(1)} %get-tuple-element.81), channel_id=1, source_target_pairs={{0,16},{1,17},{2,18},{3,19},{4,20},{5,21},{6,22},{7,23},{8,24},{9,... | collective-permute-start | bytes 98312 | tf_op jit(solution)/shard_map/ppermute | solution.py:28
  61.3 13.1 %collective-permute-start.12 = (bf16[64,256]{1,0:T(8,128)(2,1)S(1)}, bf16[64,256]{1,0:T(8,128)(2,1)S(1)}, u32[]{:S(2)}, u32[]{:S(2)}) collective-permute-start(bf16[64,256]{1,0:T(8,128)(2,1)S(1)} %get-tuple-element.82), channel_id=1, source_target_pairs={{0,24},{1,25},{2,26},{3,27},{4,28},{5,29},{6,30},{7,31},{8,16},{9,... | collective-permute-start | bytes 98312 | tf_op jit(solution)/shard_map/ppermute | solution.py:28
  69.9 14.2 %collective-permute-start.16 = (bf16[16,64,256]{2,1,0:T(8,128)(2,1)S(1)}, bf16[16,64,256]{2,1,0:T(8,128)(2,1)S(1)}, u32[]{:S(2)}, u32[]{:S(2)}) collective-permute-start(bf16[16,64,256]{2,1,0:T(8,128)(2,1)S(1)} %get-tuple-element.87), channel_id=1, source_target_pairs={{0,2},{2,4},{4,6},{6,8},{8,10},{10,12},{12,14},{14,16},{16,18},{18... | collective-permute-start | bytes 1572872 | tf_op jit(solution)/shard_map/ppermute | solution.py:33
  70.0 14.1 %collective-permute-start.17 = (bf16[16,64,256]{2,1,0:T(8,128)(2,1)S(1)}, bf16[16,64,256]{2,1,0:T(8,128)(2,1)S(1)}, u32[]{:S(2)}, u32[]{:S(2)}) collective-permute-start(bf16[16,64,256]{2,1,0:T(8,128)(2,1)S(1)} %get-tuple-element.88), channel_id=1, source_target_pairs={{0,30},{2,0},{4,2},{6,4},{8,6},{10,8},{12,10},{14,12},{16,14},{18,... | collective-permute-start | bytes 1572872 | tf_op jit(solution)/shard_map/ppermute | solution.py:33
  74.4 9.5 %collective-permute-start.13 = (bf16[96,256]{1,0:T(8,128)(2,1)S(1)}, bf16[96,256]{1,0:T(8,128)(2,1)S(1)}, u32[]{:S(2)}, u32[]{:S(2)}) collective-permute-start(bf16[96,256]{1,0:T(8,128)(2,1)S(1)} %pad_maximum_fusion.2), channel_id=1, source_target_pairs={{0,8},{1,9},{2,10},{3,11},{4,12},{5,13},{6,14},{7,15},{8,0},{9,1},... | collective-permute-start | bytes 147464 | tf_op jit(solution)/shard_map/ppermute | solution.py:28
  74.5 9.5 %collective-permute-start.14 = (bf16[96,256]{1,0:T(8,128)(2,1)S(1)}, bf16[96,256]{1,0:T(8,128)(2,1)S(1)}, u32[]{:S(2)}, u32[]{:S(2)}) collective-permute-start(bf16[96,256]{1,0:T(8,128)(2,1)S(1)} %pad_maximum_fusion.2), channel_id=1, source_target_pairs={{0,16},{1,17},{2,18},{3,19},{4,20},{5,21},{6,22},{7,23},{8,24},{9,... | collective-permute-start | bytes 147464 | tf_op jit(solution)/shard_map/ppermute | solution.py:28
  74.6 9.4 %collective-permute-start.15 = (bf16[96,256]{1,0:T(8,128)(2,1)S(1)}, bf16[96,256]{1,0:T(8,128)(2,1)S(1)}, u32[]{:S(2)}, u32[]{:S(2)}) collective-permute-start(bf16[96,256]{1,0:T(8,128)(2,1)S(1)} %pad_maximum_fusion.2), channel_id=1, source_target_pairs={{0,24},{1,25},{2,26},{3,27},{4,28},{5,29},{6,30},{7,31},{8,16},{9,... | collective-permute-start | bytes 147464 | tf_op jit(solution)/shard_map/ppermute | solution.py:28
  84.1 8.6 %collective-permute-start.18 = (bf16[288,256]{1,0:T(8,128)(2,1)S(1)}, bf16[288,256]{1,0:T(8,128)(2,1)S(1)}, u32[]{:S(2)}, u32[]{:S(2)}) collective-permute-start(bf16[288,256]{1,0:T(8,128)(2,1)S(1)} %pad_maximum_fusion.1), channel_id=1, source_target_pairs={{0,4},{1,5},{2,6},{3,7},{4,0},{5,1},{6,2},{7,3},{8,12},{9,13},{10,... | collective-permute-start | bytes 442376 | tf_op jit(solution)/shard_map/ppermute | solution.py:28
  85.2 7.9 %collective-permute-start.19 = (bf16[288,256]{1,0:T(8,128)(2,1)S(1)}, bf16[288,256]{1,0:T(8,128)(2,1)S(1)}, u32[]{:S(2)}, u32[]{:S(2)}) collective-permute-start(bf16[288,256]{1,0:T(8,128)(2,1)S(1)} %pad_maximum_fusion.1), channel_id=1, source_target_pairs={{0,1},{1,0},{2,3},{3,2},{4,5},{5,4},{6,7},{7,6},{8,9},{9,8},{10,11... | collective-permute-start | bytes 442376 | tf_op jit(solution)/shard_map/ppermute | solution.py:28
  86.5 7.6 %collective-permute-start.20 = (bf16[288,256]{1,0:T(8,128)(2,1)S(1)}, bf16[288,256]{1,0:T(8,128)(2,1)S(1)}, u32[]{:S(2)}, u32[]{:S(2)}) collective-permute-start(bf16[288,256]{1,0:T(8,128)(2,1)S(1)} %pad_maximum_fusion.1), channel_id=1, source_target_pairs={{0,5},{1,4},{2,7},{3,6},{4,1},{5,0},{6,3},{7,2},{8,13},{9,12},{10,... | collective-permute-start | bytes 442376 | tf_op jit(solution)/shard_map/ppermute | solution.py:28
  94.2 2.0 %collective-permute-start.21 = (bf16[1056,256]{1,0:T(8,128)(2,1)S(1)}, bf16[1056,256]{1,0:T(8,128)(2,1)S(1)}, u32[]{:S(2)}, u32[]{:S(2)}) collective-permute-start(bf16[1056,256]{1,0:T(8,128)(2,1)S(1)} %pad_maximum_fusion), channel_id=1, source_target_pairs={{0,2},{1,3},{2,0},{3,1},{4,6},{5,7},{6,4},{7,5},{8,10},{9,11},{10,... | collective-permute-start | bytes 1622024 | tf_op jit(solution)/shard_map/ppermute | solution.py:28

commit v3 on v2

v3 whole, which is shorter than its diff:
```python
import functools
import math

import jax
import jax.numpy as jnp
from jax import lax
from jax.experimental import pallas as pl
from jax.experimental.pallas import tpu as pltpu
from jax.sharding import PartitionSpec as P

KERNEL_SPACING = 4
BLOCK = 8
NEAR_BLOCK = 16
FAR_BLOCK = 16
AXES = ("lon", "lat")
F32 = jnp.float32
BF16 = jnp.bfloat16
GELU_A = math.sqrt(2.0 / math.pi)
GELU_B = GELU_A * 0.044715


def xor_permute(value, mask):
    nlon, nlat = lax.axis_size("lon"), lax.axis_size("lat")
    lat_mask, lon_mask = mask
    pairs = [
        (lon * nlat + lat, (lon ^ lon_mask) * nlat + (lat ^ lat_mask))
        for lon in range(nlon)
        for lat in range(nlat)
    ]
    return lax.ppermute(value, AXES, pairs)


def on_chip(value):
    return xor_permute(value, (0, 1))


def off_chip(value):
    count = lax.axis_size("lon")
    pairs = [(i, (i + (1 if i % 2 else -1)) % count) for i in range(count)]
    return lax.ppermute(value, "lon", pairs)


def groups():
    nlon, nlat = lax.axis_size("lon"), lax.axis_size("lat")
    lon, lat = lax.axis_index("lon").astype(jnp.uint32), lax.axis_index("lat").astype(jnp.uint32)
    core = (lon & 1, [(0, s) for s in range(2)])
    plane = (lat * 2 + ((lon >> 1) & 1), [(s >> 1, (s & 1) * 2) for s in range(2 * nlat)])
    depth = (lon >> 2, [(0, s * 4) for s in range(nlon // 4)])
    return [([own ^ jnp.uint32(s) for s in range(len(masks))], masks) for own, masks in (core, plane, depth)]


def piece(parts, place):
    zero = jnp.uint32(0)
    return lax.dynamic_slice(parts, (place, zero, zero), (1,) + parts.shape[1:])[0]


def scatter_stage(value, group):
    places, _ = group
    size = len(places)
    parts = value.reshape(size, value.shape[0] // size, value.shape[1])
    return [piece(parts, p).astype(BF16) for p in places[1:]], piece(parts, places[0])


def scatter_finish(sends, total, group):
    _, masks = group
    for send, mask in zip(sends, masks[1:]):
        total = total + xor_permute(send, mask).astype(F32)
    return total


def gather_finish(packed, extra, group, beside):
    places, masks = group
    size = len(places)
    rows = packed.shape[0] - extra.shape[0]
    got = [packed[:rows]]
    parts, beside = lax.optimization_barrier(([xor_permute(packed, m) for m in masks[1:]], beside))
    for part in parts:
        got.append(part[:rows])
        extra = extra + part[rows:].astype(F32)
    whole = jnp.zeros((size, rows, packed.shape[1]), packed.dtype)
    zero = jnp.uint32(0)
    for part, place in zip(got, places):
        whole = lax.dynamic_update_slice(whole, part[None], (place, zero, zero))
    return whole.reshape(size * rows, packed.shape[1]), extra, beside


def pack(value, extra):
    return jnp.concatenate([value, extra.astype(BF16)], axis=0)


def lane_groups(channels):
    return range(channels // 128)


def halo_row(even, near, far):
    return jnp.where(even, far, near), jnp.where(even, near, far)


def stage_row(s0, s4, left, middle, right):
    edge, cols = left.shape[0], middle.shape[0]
    left, middle, right = left.astype(F32), middle.astype(F32), right.astype(F32)
    s0[pl.ds(0, edge), :] = left
    s0[pl.ds(edge, cols), :] = middle
    s0[pl.ds(edge + cols, edge), :] = right
    s4[pl.ds(0, edge - 4), :] = left[4:]
    s4[pl.ds(edge - 4, cols), :] = middle
    s4[pl.ds(edge - 4 + cols, edge - 4), :] = right[: edge - 4]


def spread_taps(kb, kernel_ref, flip):
    taps = kernel_ref.shape[0]
    for t in range(taps):
        row = kernel_ref[pl.ds(taps - 1 - t if flip else t, 1), :]
        kb[t] = jnp.broadcast_to(row, kb.shape[1:])


def tap_uses(blocks, taps, edge):
    lead = (edge - KERNEL_SPACING * (taps // 2)) // 4
    result = []
    for i in range(blocks + 2 * edge // 8):
        for half in (0, 1):
            uses = []
            for j in range(blocks):
                t = 2 * (i - j) + half - lead
                if 0 <= t < taps:
                    uses.append((j, t))
            if uses:
                result.append((i, half, uses))
    return result


def add_to(acc, at, term):
    acc[at] = term if acc[at] is None else acc[at] + term


def conv_lane(s0, s4, kb, lane, cols, taps, edge):
    lanes = pl.ds(lane * 128, 128)
    acc = [None] * (cols // 8)
    weights = [kb[t, :, lanes] for t in range(taps)]
    for i, half, uses in tap_uses(cols // 8, taps, edge):
        x = (s4 if half else s0)[pl.ds(8 * i, 8), lanes]
        for j, t in uses:
            add_to(acc, j, weights[t] * x)
    return acc


def row_spec(block, n, width):
    return pl.BlockSpec((block, n, width), lambda i: (i, 0, 0))


def whole_spec(*shape):
    return pl.BlockSpec(shape, lambda i: (0,) * len(shape))


def resident():
    return pl.BlockSpec(memory_space=pltpu.VMEM)


def resident_shape(*shape):
    return pltpu.VMEM(shape, F32)


def params(mib):
    return pltpu.CompilerParams(dimension_semantics=("arbitrary",), vmem_limit_bytes=mib * 2**20)


def halo_terms(edges, kb, lane, cols, taps, side):
    edge = edges.shape[1]
    lanes = pl.ds(lane * 128, 128)
    acc = {}
    for shifted in (0, 1):
        for i in range(edge // 8):
            column = ((-edge, 4 - edge), (cols, cols - 4))[side][shifted] + 8 * i
            x = None
            for j in range(cols // 8):
                t = (column - 8 * j) // 4 + taps // 2
                if 0 <= t < taps:
                    if x is None:
                        x = edges[shifted, pl.ds(8 * i, 8), lanes]
                    term = kb[t, :, lanes] * x
                    acc[j] = acc[j] + term if j in acc else term
    return acc


def stage_edges(edges, halo, side):
    edge = edges.shape[1]
    halo = halo.astype(F32)
    edges[0] = halo
    if side == 0:
        edges[1, pl.ds(0, edge - 4), :] = halo[4:]
    else:
        edges[1, pl.ds(4, edge - 4), :] = halo[: edge - 4]


def inner_kernel(
    core_ref, fields_ref, near_ref, kernel_ref, up_hbm, down_hbm, out_ref, upt_ref, downt_ref,
    s0, s4, kb, edges, up_ref, down_ref, sems,
):
    rows, cols, channels = fields_ref.shape
    taps = kernel_ref.shape[0]
    copies = [
        pltpu.make_async_copy(up_hbm, up_ref, sems.at[0]),
        pltpu.make_async_copy(down_hbm, down_ref, sems.at[1]),
    ]
    for copy in copies:
        copy.start()
    spread_taps(kb, kernel_ref, False)
    s4[...] = jnp.zeros_like(s4)
    edges[...] = jnp.zeros_like(edges)

    def one_row(side, r, carry):
        middle = fields_ref[r].astype(F32)
        s0[...] = middle
        s4[pl.ds(4, cols), :] = middle
        stage_edges(edges, near_ref[r], side)
        for lane in lane_groups(channels):
            lanes = pl.ds(lane * 128, 128)
            weights = [kb[t, :, lanes] for t in range(taps)]
            acc = [None] * (cols // 8)
            for i in range(cols // 8 + 1):
                for half, ref in ((0, s0), (1, s4)):
                    if half == 0 and i == cols // 8:
                        continue
                    x = ref[pl.ds(8 * i, 8), lanes]
                    for j in range(cols // 8):
                        t = 2 * (i - j) - half + taps // 2
                        if 0 <= t < taps:
                            add_to(acc, j, weights[t] * x)
            for j, value in halo_terms(edges, kb, lane, cols, taps, side).items():
                add_to(acc, j, value)
            for j, value in enumerate(acc):
                out_ref[r, pl.ds(8 * j, 8), lanes] = value
        return carry

    for side, here in ((1, core_ref[0] == 0), (0, core_ref[0] != 0)):

        @pl.when(here)
        def _(side=side):
            lax.fori_loop(0, rows, functools.partial(one_row, side), 0)

    for copy in copies:
        copy.wait()
    for j in range(up_ref.shape[1] // 256):
        part = pl.ds(256 * j, 256)
        upt_ref[part, :] = up_ref[:, part].T
        downt_ref[:, part] = down_ref[part, :].T


def inner(core, fields, near, kernel, up, down):
    rows, cols, channels = fields.shape
    taps, edge = kernel.shape[0], near.shape[1]
    return pl.pallas_call(
        inner_kernel,
        in_specs=[pl.BlockSpec(memory_space=pltpu.SMEM)]
        + [resident()] * 3
        + [pl.BlockSpec(memory_space=pltpu.HBM)] * 2,
        out_specs=[resident()] * 3,
        out_shape=[resident_shape(rows, cols, channels), pltpu.VMEM(down.shape, BF16), pltpu.VMEM(up.shape, BF16)],
        scratch_shapes=[
            pltpu.VMEM((cols, channels), F32),
            pltpu.VMEM((cols + 8, channels), F32),
            pltpu.VMEM((taps, 8, channels), F32),
            pltpu.VMEM((2, edge, channels), F32),
            pltpu.VMEM(up.shape, BF16),
            pltpu.VMEM(down.shape, BF16),
            pltpu.SemaphoreType.DMA((2,)),
        ],
        compiler_params=pltpu.CompilerParams(vmem_limit_bytes=8 * 2**20),
        cost_estimate=pl.CostEstimate(
            flops=260 * taps * rows * cols * channels, transcendentals=0,
            bytes_accessed=rows * cols * channels * 6,
        ),
        name="inner",
    )(core, fields, near, kernel, up, down)


def forward_kernel(
    reach, first, last, start, core_ref, inner_ref, far_ref, fields_ref, cot_ref, kernel_ref,
    up_ref, upt_ref, down_ref, downt_ref, *refs,
):
    given, refs = ((), refs) if first else (refs[2:4], refs[4:])
    (out_ref, grad_ref, gup_ref, gdt_ref), refs = refs[:4], refs[4:]
    if reach:
        (near_out_ref, far_out_ref), refs = refs[:2], refs[2:]
        edges, kb, conv_s = refs[:3]
        refs = refs[3:]
    normed_s, act_s, hg_s = refs[:3]
    gup_s, gdt_s = refs[3:] if last else (gup_ref, gdt_ref)
    step = pl.program_id(0)
    _, cols, channels = inner_ref.shape
    edge, taps = far_ref.shape[1], kernel_ref.shape[0]
    rows = FAR_BLOCK if reach else NEAR_BLOCK
    base_row = start + step * rows
    here = pl.ds(base_row, rows)
    even = core_ref[0] == 0
    hid = up_ref.shape[1]
    width = 256
    count = edge if reach else cols - edge
    cells = rows * count
    if reach:
        place = jnp.where(even, 0, cols - edge)
    else:
        place = jnp.where(even, edge, 0)
    span = pl.ds(pl.multiple_of(place, 16), count)

    @pl.when(step == 0)
    def _():
        if first:
            gup_s[...] = jnp.zeros_like(gup_s)
            gdt_s[...] = jnp.zeros_like(gdt_s)
        if last:
            gup_s[...] = given[0][...]
            gdt_s[...] = given[1][...]
        if reach:
            spread_taps(kb, kernel_ref, False)
            edges[...] = jnp.zeros_like(edges)

    if reach:

        def one_row(side, r, carry):
            stage_edges(edges, far_ref[r], side)
            for lane in lane_groups(channels):
                lanes = pl.ds(lane * 128, 128)
                terms = halo_terms(edges, kb, lane, cols, taps, side)
                skip = (cols - edge) // 8 if side else 0
                for j in range(count // 8):
                    base = inner_ref[base_row + r, pl.ds(8 * (j + skip), 8), lanes]
                    conv_s[r, pl.ds(8 * j, 8), lanes] = base + terms[j + skip] if j + skip in terms else base
            return carry

        for side, mine in ((0, even), (1, jnp.logical_not(even))):

            @pl.when(mine)
            def _(side=side):
                lax.fori_loop(0, rows, functools.partial(one_row, side), 0)

        conv = conv_s[...].reshape(cells, channels)
    else:
        conv = inner_ref[here, span, :].reshape(cells, channels)
    center = jnp.mean(conv, axis=-1, keepdims=True)
    deviation = conv - center
    spread = jnp.mean(deviation * deviation, axis=-1, keepdims=True)
    inv_scale = lax.rsqrt(spread + 1e-06)
    normed = deviation * inv_scale
    normed_s[...] = normed
    low = normed.astype(BF16)
    cot = cot_ref[here, span, :].reshape(cells, channels)
    over_cells = (((0,), (0,)), ((), ()))
    for j in range(hid // width):
        part = pl.ds(j * width, width)
        h = jnp.dot(low, up_ref[:, part], preferred_element_type=F32)
        u = jnp.dot(cot, downt_ref[:, part], preferred_element_type=F32)
        sq = h * h
        t = jnp.tanh(h * (GELU_A + GELU_B * sq))
        half = 0.5 * h
        act_s[:, part] = (half + half * t).astype(BF16)
        slope = (0.5 + 0.5 * t) + half * (1.0 - t * t) * (GELU_A + (3.0 * GELU_B) * sq)
        hg_s[:, part] = (u * slope).astype(BF16)
    out = jnp.dot(act_s[...], down_ref[...], preferred_element_type=F32)
    out = out + fields_ref[here, span, :].reshape(cells, channels).astype(F32)
    normed_grad = jnp.dot(hg_s[...], upt_ref[...], preferred_element_type=F32)
    for j in range(hid // width):
        part = pl.ds(j * width, width)
        gup_s[j] += lax.dot_general(low, hg_s[:, part], over_cells, preferred_element_type=F32)
        gdt_s[:, part] += lax.dot_general(cot, act_s[:, part], over_cells, preferred_element_type=F32)
    out_ref[here, span, :] = out.astype(BF16).reshape(rows, count, channels)
    normed = normed_s[...]
    mean_grad = jnp.mean(normed_grad, axis=-1, keepdims=True)
    mean_cross = jnp.mean(normed_grad * normed, axis=-1, keepdims=True)
    grad = inv_scale * (normed_grad - mean_grad - normed * mean_cross)
    grad = grad.reshape(rows, count, channels)
    grad_ref[here, span, :] = grad
    if reach:
        far_out_ref[...] = grad.astype(BF16)
        near_place = jnp.where(even, cols - edge, 0)
        near_out_ref[...] = grad_ref[here, pl.ds(pl.multiple_of(near_place, 16), edge), :].astype(BF16)

    if last:
        mine_ref, theirs_ref = gup_ref, gdt_ref
        ending = step == pl.num_programs(0) - 1

        @pl.when(ending & even)
        def _():
            for j in range(hid // width):
                part = pl.ds(j * width, width)
                mine_ref[part, :] = gup_s[j]
                theirs_ref[part, :] = gdt_s[:, part].T.astype(BF16)

        @pl.when(ending & jnp.logical_not(even))
        def _():
            for j in range(hid // width):
                part = pl.ds(j * width, width)
                theirs_ref[part, :] = gup_s[j].astype(BF16)
                mine_ref[part, :] = gdt_s[:, part].T


def forward(core, conv_inner, far, fields, cot, kernel, up, up_t, down, down_t, carried, reach, begin, end):
    rows, cols, channels = cot.shape
    edge = far.shape[1]
    taps, hid = kernel.shape[0], up.shape[1]
    count = edge if reach else cols - edge
    cells = (end - begin) * count
    last = reach and end == rows
    block = FAR_BLOCK if reach else NEAR_BLOCK
    own = row_spec(block, edge, channels)
    sums = [(hid // 256, channels, 256), (channels, hid)]
    ends = [((hid, channels), F32), ((hid, channels), BF16)] if last else [(s, F32) for s in sums]
    edges_out = [jax.ShapeDtypeStruct((end - begin, edge, channels), BF16)] * (2 if reach else 0)
    block_cells = block * count
    return pl.pallas_call(
        functools.partial(forward_kernel, reach, not carried, last, begin),
        grid=((end - begin) // block,),
        in_specs=[pl.BlockSpec(memory_space=pltpu.SMEM), resident(), own if reach else resident()]
        + [resident()] * (7 + len(carried)),
        out_specs=[resident()] * 4 + [own] * len(edges_out),
        out_shape=[pltpu.VMEM((rows, cols, channels), BF16), resident_shape(rows, cols, channels)]
        + [pltpu.VMEM(s, d) for s, d in ends]
        + edges_out,
        input_output_aliases={} if not carried else {10: 0, 11: 1} if last else {10: 0, 11: 1, 12: 2, 13: 3},
        scratch_shapes=(
            [
                pltpu.VMEM((2, edge, channels), F32),
                pltpu.VMEM((taps, 8, channels), F32),
                pltpu.VMEM((block, count, channels), F32),
            ]
            if reach
            else []
        )
        + [
            pltpu.VMEM((block_cells, channels), F32),
            pltpu.VMEM((block_cells, hid), BF16),
            pltpu.VMEM((block_cells, hid), BF16),
        ]
        + ([pltpu.VMEM(s, F32) for s in sums] if last else []),
        compiler_params=params(28),
        cost_estimate=pl.CostEstimate(
            flops=28 * cells * channels * hid, transcendentals=cells * hid,
            bytes_accessed=cells * channels * 12,
        ),
        name="forward",
    )(core, conv_inner, far, fields, cot, kernel, up, up_t, down, down_t, *carried)


def kernel_grad_kernel(start, core_ref, fields_ref, near_ref, far_ref, grad_ref, given_ref, out_ref, s0, s4, sums):
    _, cols, channels = fields_ref.shape
    rows, edge, _ = far_ref.shape
    even = core_ref[0] == 0
    taps = out_ref.shape[0] - 1
    blocks = cols // 8

    sums[...] = jnp.zeros_like(sums)

    def one_row(r, carry):
        left, right = halo_row(even, near_ref[start + r], far_ref[r])
        stage_row(s0, s4, left, fields_ref[start + r], right)
        for lane in lane_groups(channels):
            lanes = pl.ds(lane * 128, 128)
            grads = [grad_ref[start + r, pl.ds(8 * j, 8), lanes] for j in range(blocks)]
            acc = [None] * taps
            for i, half, uses in tap_uses(blocks, taps, edge):
                x = (s4 if half else s0)[pl.ds(8 * i, 8), lanes]
                for j, t in uses:
                    add_to(acc, t, grads[j] * x)
            for t in range(taps):
                sums[t, :, lanes] += acc[t]
        return carry

    lax.fori_loop(0, rows, one_row, 0)

    for t in range(taps):
        here = jnp.sum(sums[t], axis=0, keepdims=True)
        out_ref[pl.ds(t, 1), :] = given_ref[pl.ds(t, 1), :] + here
    out_ref[pl.ds(taps, 1), :] = jnp.zeros((1, channels), F32)


def staging(cols, edge, channels):
    return [
        pltpu.VMEM((cols + 2 * edge, channels), F32),
        pltpu.VMEM((cols + 2 * edge - 8, channels), F32),
    ]


def kernel_grad(core, fields, near, far, grad, given, start):
    _, cols, channels = fields.shape
    count, edge, _ = far.shape
    taps = given.shape[0] - 1
    return pl.pallas_call(
        functools.partial(kernel_grad_kernel, start),
        in_specs=[pl.BlockSpec(memory_space=pltpu.SMEM)] + [resident()] * 5,
        out_specs=resident(),
        out_shape=resident_shape(taps + 1, channels),
        scratch_shapes=staging(cols, edge, channels) + [pltpu.VMEM((taps, 8, channels), F32)],
        compiler_params=pltpu.CompilerParams(vmem_limit_bytes=8 * 2**20),
        cost_estimate=pl.CostEstimate(
            flops=360 * taps * count * cols * channels, transcendentals=0,
            bytes_accessed=count * cols * channels * 8,
        ),
        name="kernel_grad",
    )(core, fields, near, far, grad, given)


def backward_kernel(start, core_ref, grad_ref, near_ref, far_ref, cot_ref, kernel_ref, *refs):
    out_ref, s0, s4, kb = refs[-4:]
    _, cols, channels = grad_ref.shape
    rows, edge, _ = far_ref.shape
    even = core_ref[0] == 0
    base = start + pl.program_id(0) * rows
    taps = kernel_ref.shape[0]

    @pl.when(pl.program_id(0) == 0)
    def _():
        spread_taps(kb, kernel_ref, True)

    def one_row(r, carry):
        left, right = halo_row(even, near_ref[base + r], far_ref[r])
        stage_row(s0, s4, left, grad_ref[base + r], right)
        for lane in lane_groups(channels):
            acc = conv_lane(s0, s4, kb, lane, cols, taps, edge)
            lanes = pl.ds(lane * 128, 128)
            back = jnp.concatenate(acc, axis=0) + cot_ref[r, :, lanes].astype(F32)
            out_ref[r, :, lanes] = back.astype(BF16)
        return carry

    lax.fori_loop(0, rows, one_row, 0)


def backward(core, grad, near, far, cot, kernel, carried, start):
    rows, cols, channels = grad.shape
    count, edge, _ = far.shape
    taps = kernel.shape[0]
    own = functools.partial(row_spec, BLOCK)
    at = pl.BlockSpec((BLOCK, cols, channels), lambda i: (i + start // BLOCK, 0, 0))
    return pl.pallas_call(
        functools.partial(backward_kernel, start),
        grid=(count // BLOCK,),
        in_specs=[
            pl.BlockSpec(memory_space=pltpu.SMEM), resident(), resident(), own(edge, channels), at, resident(),
        ]
        + [pl.BlockSpec(memory_space=pl.ANY)] * len(carried),
        out_specs=at,
        out_shape=jax.ShapeDtypeStruct((rows, cols, channels), BF16),
        input_output_aliases={6: 0} if carried else {},
        scratch_shapes=staging(cols, edge, channels) + [pltpu.VMEM((taps, 8, channels), F32)],
        compiler_params=params(8),
        cost_estimate=pl.CostEstimate(
            flops=360 * taps * count * cols * channels, transcendentals=0,
            bytes_accessed=count * cols * channels * 10,
        ),
        name="backward",
    )(core, grad, near, far, cot, kernel, *carried)


def finish_kernel(factor, core_ref, own_ref, got_ref, tail_ref, kgrad_ref, up_ref, down_ref, taps_ref):
    even = core_ref[0] == 0
    own, got = own_ref[...].astype(F32) * factor, got_ref[...].astype(F32) * factor
    up_ref[...] = jnp.where(even, own, got)
    down_ref[...] = jnp.where(even, got, own)
    taps = taps_ref.shape[0]
    taps_ref[...] = (kgrad_ref[pl.ds(0, taps), :] + tail_ref[pl.ds(0, taps), :].astype(F32)) * factor


def finish(core, own, got, kgrad, taps, factor):
    hid, channels = own.shape[0] - kgrad.shape[0], own.shape[1]
    part = pl.BlockSpec((256, channels), lambda j: (j, 0))
    return pl.pallas_call(
        functools.partial(finish_kernel, factor),
        grid=(hid // 256,),
        in_specs=[
            pl.BlockSpec(memory_space=pltpu.SMEM), part, part,
            pl.BlockSpec(kgrad.shape, lambda j: (hid // kgrad.shape[0], 0)), whole_spec(*kgrad.shape),
        ],
        out_specs=[
            pl.BlockSpec((channels, 256), lambda j: (0, j)), part, whole_spec(taps, channels),
        ],
        out_shape=[
            jax.ShapeDtypeStruct((channels, hid), F32),
            jax.ShapeDtypeStruct((hid, channels), F32),
            jax.ShapeDtypeStruct((taps, channels), F32),
        ],
        compiler_params=params(8),
        name="finish",
    )(core, own, got, got, kgrad)


def after(values, *others):
    held, _ = lax.optimization_barrier((values, others))
    return held


def chunk_starts(rows):
    half = rows // 2 // BLOCK * BLOCK
    return [0, half, rows]


def with_places(fields):
    found = groups()
    core = found[0][0][0]
    fields, places, index, even = lax.optimization_barrier(
        (fields, [places for places, _ in found], core.astype(jnp.int32).reshape(1), core == 0)
    )
    return fields, [(p, masks) for p, (_, masks) in zip(places, found)], index, even


def per_device(fields, cotangent, kernel, up_weight, down_weight):
    rows, cols, channels = fields.shape
    taps, hid = kernel.shape[0], up_weight.shape[1]
    edge = -(-KERNEL_SPACING * (taps // 2) // 8) * 8
    fields, (core, plane, depth), index, even = with_places(fields)
    bounds = chunk_starts(rows)
    chunks = list(zip(bounds[:-1], bounds[1:]))
    to_left, to_right = fields[:, :edge], fields[:, cols - edge :]
    near_out, far_out = jnp.where(even, to_right, to_left), jnp.where(even, to_left, to_right)
    middle = chunks[0][1]
    near = on_chip(near_out)
    far = [off_chip(far_out[:middle])]
    near, _ = lax.optimization_barrier((near, far_out))
    conv_inner, up_t, down_t = inner(index, fields, near, kernel, up_weight, down_weight)
    far_out = after(far_out, conv_inner)
    far.append(off_chip(far_out[middle:]))

    def cells_of(carried, reach, halo, begin, end):
        return forward(
            index, conv_inner, halo, fields, cotangent, kernel, up_weight, up_t, down_weight, down_t,
            carried, reach, begin, end,
        )

    carried = cells_of((), False, near, 0, rows)
    grad_near, grad_far = [], []
    for (begin, end), arrived in zip(chunks, far):
        *carried, near_edge, far_edge = cells_of(carried, True, arrived, begin, end)
        grad_near.append(near_edge)
        if end < rows:
            grad_far.append(off_chip(far_edge))
    output, grad, mine, theirs = carried

    kgrad = jnp.zeros((taps + 1, channels), F32)

    def add_kernel_grad(total, which):
        return kernel_grad(index, fields, near, far[which], grad, total, chunks[which][0])

    def add_field_grad(so_far, which):
        return (
            backward(index, grad, grad_near, grad_far[which], cotangent, kernel, so_far, chunks[which][0]),
        )

    theirs = after(theirs, grad_far[0])
    part = mine + xor_permute(theirs, core[1][1]).astype(F32)
    sends, total = scatter_stage(part, plane)
    kgrad = after(kgrad, *sends)
    kgrad = add_kernel_grad(kgrad, 0)
    part = scatter_finish(sends, total, plane)
    part, far_edge = lax.optimization_barrier((part, far_edge))
    grad_far.append(off_chip(far_edge))
    grad_near = on_chip(jnp.concatenate(grad_near, axis=0))
    sends, total = scatter_stage(part, depth)
    sends, kgrad = lax.optimization_barrier((sends, kgrad))
    kgrad = add_kernel_grad(kgrad, 1)
    part = scatter_finish(sends, total, depth).astype(BF16)
    packed = pack(part, kgrad)
    packed, halo = lax.optimization_barrier((packed, grad_far[0]))
    grad_far[0] = halo
    field_grad = add_field_grad((), 0)
    part, kgrad, field_grad = gather_finish(packed, kgrad, depth, field_grad)
    packed, halo = lax.optimization_barrier((pack(part, kgrad), grad_far[1]))
    grad_far[1] = halo
    field_grad = add_field_grad(field_grad, 1)
    part, kgrad, field_grad = gather_finish(packed, kgrad, plane, field_grad)
    packed = pack(part, kgrad)
    got = on_chip(packed)
    factor = 1.0 / math.sqrt(rows * cols * lax.axis_size("lon") * lax.axis_size("lat"))
    up_grad, down_grad, tap_grad = finish(index, packed, got, kgrad, taps, factor)
    return (output, field_grad[0], tap_grad, up_grad, down_grad)


def solution(mesh):
    placed = (P("lat", "lon", None), P("lat", "lon", None), P(), P(), P())
    return jax.shard_map(
        per_device,
        mesh=mesh,
        in_specs=placed,
        out_specs=(P("lat", "lon", None), P("lat", "lon", None), P(), P(), P()),
        check_vma=False,
    )
```

time: 99.4 us -> 93 us (0.936)
  starting transfers between devices: 35.1 us -> 29.1 us
  local copies, waits for them, and re-layouts: 4.99 us -> 1.54 us
  waiting for transfers between devices: 7.05 us -> 10.3 us
    ppermute x8 -> x4, starting transfers between devices: 19 us -> 11.8 us  [off_chip(): return lax.ppermute(value, 'lon', pairs)]
    ppermute x8 -> x4, waiting for transfers between devices: 0.02 us -> 2.64 us  [off_chip(): return lax.ppermute(value, 'lon', pairs)]
    select_n x0 -> x1, other arithmetic: none -> 1.84 us  [per_device(): jnp.where(even, to_left, to_right)]
    mul x2 -> x0, other arithmetic: 1.8 us -> none  [the longest x1 1.17 us: per_device(): gdown = jnp.where(even, got, part).astype(F32) * factor]
    slice x3 -> x2, local copies, waits for them, and re-layouts: 1.56 us -> 0.08 us  [the longest x1 0.04 us: per_device(): far.append(off_chip(far_out[middle:]))]
    reshape x1 -> x0, local copies, waits for them, and re-layouts: 1.11 us -> none  [per_device(): gup.reshape(hid // 256, channels, 256).transpose(1, 0, 2)]
    ppermute x14 -> x16, starting transfers between devices: 16.1 us -> 17.2 us  [xor_permute(): return lax.ppermute(value, AXES, pairs)]
    unnamed x14 -> x11, local copies, waits for them, and re-layouts: 2.11 us -> 1.25 us
  transfers between devices with their start and end apart: 22 -> 20, of which waited for: 6 -> 7; matrix products, arithmetic and copies ran while one was open for 0% -> 2% of each run, Pallas kernels for 49% -> 51%
where the time goes in v3:
time: 93 us; the launch traced here: 92.9 us
  Pallas kernels  48.8 us (52%)
  starting transfers between devices  29.1 us (31%)
  waiting for transfers between devices  10.3 us (11%)
  other arithmetic  2.21 us (2%)
  local copies, waits for them, and re-layouts  1.54 us (2%)
  between operations  0.96 us (1%)
    pallas_call x3, Pallas kernels, forward(): pl.pallas_call(functools.partial(forward_kernel, reach, not carried, last...  20.3 us
    ppermute x16, starting transfers between devices, xor_permute(): return lax.ppermute(value, AXES, pairs)  17.2 us
    ppermute x4, starting transfers between devices, off_chip(): return lax.ppermute(value, 'lon', pairs)  11.8 us
    pallas_call x2, Pallas kernels, backward(): pl.pallas_call(functools.partial(backward_kernel, start), grid=(count //...  10.3 us
    pallas_call x2, Pallas kernels, kernel_grad(): pl.pallas_call(functools.partial(kernel_grad_kernel, start), in_specs=[pl...  8.69 us
    ppermute x16, waiting for transfers between devices, xor_permute(): return lax.ppermute(value, AXES, pairs)  7.66 us
    pallas_call x1, Pallas kernels, inner(): pl.pallas_call(inner_kernel, in_specs=[pl.BlockSpec(memory_space=pltpu.SM...  7.6 us
    ppermute x4, waiting for transfers between devices, off_chip(): return lax.ppermute(value, 'lon', pairs)  2.64 us
  transfers between devices with their start and end apart: 20, of which 7 were waited for; matrix products, arithmetic and copies ran while one was open for 2% of the time, Pallas kernels for 51%

profile of v3, /device:TPU:0, one launch (start us, length us, event | category | flops | bytes accessed | tf_op | source)
XLA Modules:
  0.0 92.9 jit_solution(1986083703824950130)
XLA Ops:
  0.6 0.0 copy-start
  0.7 0.0 copy-start.2
  0.7 0.0 copy-start.3
  0.7 0.0 copy-start.4
  0.7 1.8 %broadcast_select_fusion = (bf16[32,64,256]{2,1,0:T(8,128)(2,1)S(1)}, bf16[32,64,256]{2,1,0:T(8,128)(2,1)S(1)}) fusion(pred[]{:T(512)S(6)} %eq.3, bf16[32,112,256]{2,1,0:T(8,128)(2,1)} %fields_ref.5), kind=kLoop, calls=%fused_computation.2 | loop fusion | flops 1048576 | bytes 4194305 | tf_op jit(solution)/shard_map/jit(_where)/select_n | solution.py:612
  2.5 0.5 collective-permute-start
  3.1 0.0 copy-start.1
  3.1 5.7 %collective-permute-start.2 = (bf16[16,64,256]{2,1,0:T(8,128)(2,1)S(1)}, bf16[16,64,256]{2,1,0:T(8,128)(2,1)S(1)}, u32[]{:S(2)}, u32[]{:S(2)}) collective-permute-start(bf16[16,64,256]{2,1,0:T(8,128)(2,1)S(1)} %slice.72), channel_id=1, source_target_pairs={{0,30},{2,4},{4,2},{6,8},{8,6},{10,12},{12,10},{14,16},{16,14},{18... | collective-permute-start | bytes 1572872 | tf_op jit(solution)/shard_map/ppermute | solution.py:40
  8.8 0.0 collective-permute-done.near_ref.far_ref
  8.8 0.0 copy-done
  8.8 0.0 copy-done.2
  8.8 0.0 copy-done.3
  8.8 0.0 copy-done.4
  8.8 7.6 %inner.1 = (f32[32,112,256]{2,1,0:T(8,128)S(1)}, bf16[1024,256]{1,0:T(8,128)(2,1)S(1)}, bf16[256,1024]{1,0:T(8,128)(2,1)S(1)}) custom-call(s32[1]{0:T(128)} %bitcast.core_ref, bf16[32,112,256]{2,1,0:T(8,128)(2,1)S(1)} %copy-done, bf16[32,64,256]{2,1,0:T(8,128)(2,1)S(1)} %collective-permute-done.near_ref.far_ref, f32[31,256]{1,0:T(8,128)S(1)} %copy-done.4, ...), custom_call_target="tpu_custom_call" | custom-call | flops 7395082240 | bytes 5505024 | tf_op jit(solution)/shard_map/inner/pallas_call | solution.py:252
  16.5 2.2 %collective-permute-start.1 = (bf16[16,64,256]{2,1,0:T(8,128)(2,1)S(1)}, bf16[16,64,256]{2,1,0:T(8,128)(2,1)S(1)}, u32[]{:S(2)}, u32[]{:S(2)}) collective-permute-start(bf16[16,64,256]{2,1,0:T(8,128)(2,1)S(1)} %slice.56), channel_id=1, source_target_pairs={{0,30},{2,4},{4,2},{6,8},{8,6},{10,12},{12,10},{14,16},{16,14},{18... | collective-permute-start | bytes 1572872 | tf_op jit(solution)/shard_map/ppermute | solution.py:40
  18.7 0.0 copy-done.1
  18.7 7.9 %forward.3 = (bf16[32,112,256]{2,1,0:T(8,128)(2,1)S(1)}, f32[32,112,256]{2,1,0:T(8,128)S(1)}, f32[4,256,256]{2,1,0:T(8,128)S(1)}, f32[256,1024]{1,0:T(8,128)S(1)}) custom-call(s32[1]{0:T(128)} %bitcast.core_ref, f32[32,112,256]{2,1,0:T(8,128)S(1)} %get-tuple-element.64.inner_ref, bf16[32,64,256]{2,1,0:T(8,128)(2,1)S(1)} %collective-permute-done.near_ref.far_ref, ...), custom_call_target="tpu_custom_call" | custom-call | flops 11274289152 | bytes 4718592 | tf_op jit(solution)/shard_map/forward/pallas_call | solution.py:410
  26.6 0.0 collective-permute-done.2.far_ref
  26.6 6.0 %forward.4 = (bf16[32,112,256]{2,1,0:T(8,128)(2,1)S(1)}, f32[32,112,256]{2,1,0:T(8,128)S(1)}, f32[4,256,256]{2,1,0:T(8,128)S(1)}, f32[256,1024]{1,0:T(8,128)S(1)...) custom-call(s32[1]{0:T(128)} %bitcast.core_ref, ...), custom_call_target="tpu_custom_call", output_to_operand_aliasing={{0}: (10, {}), {1}: (11, {}), {2}: (12, {}), {3}: (13, {})} | custom-call | flops 7516192768 | bytes 3145728 | tf_op jit(solution)/shard_map/forward/pallas_call | solution.py:410
  32.6 2.4 %collective-permute-start.3 = (bf16[16,64,256]{2,1,0:T(8,128)(2,1)S(1)}, bf16[16,64,256]{2,1,0:T(8,128)(2,1)S(1)}, u32[]{:S(2)}, u32[]{:S(2)}) collective-permute-start(bf16[16,64,256]{2,1,0:T(8,128)(2,1)S(1)} %get-tuple-element.79), channel_id=1, source_target_pairs={{0,30},{2,4},{4,2},{6,8},{8,6},{10,12},{12,10},{14,16},{16,14},{18... | collective-permute-start | bytes 1572872 | tf_op jit(solution)/shard_map/ppermute | solution.py:40
  35.0 0.0 collective-permute-done.1.far_ref
  35.0 6.4 %forward.5 = (bf16[32,112,256]{2,1,0:T(8,128)(2,1)S(1)}, f32[32,112,256]{2,1,0:T(8,128)S(1)}, f32[1024,256]{1,0:T(8,128)S(1)}, bf16[1024,256]{1,0:T(8,128)(2,1)S...) custom-call(s32[1]{0:T(128)} %bitcast.core_ref, ...), custom_call_target="tpu_custom_call", output_to_operand_aliasing={{0}: (10, {}), {1}: (11, {})} | custom-call | flops 7516192768 | bytes 3145728 | tf_op jit(solution)/shard_map/forward/pallas_call | solution.py:410
  41.5 2.6 %collective-permute-done.3.far_ref = bf16[16,64,256]{2,1,0:T(8,128)(2,1)S(1)} collective-permute-done((bf16[16,64,256]{2,1,0:T(8,128)(2,1)S(1)}, bf16[16,64,256]{2,1,0:T(8,128)(2,1)S(1)}, u32[]{:S(2)}, u32[]{:S(2)}) %collective-permute-start.3) | collective-permute-done | bytes 524320 | tf_op jit(solution)/shard_map/ppermute | solution.py:40
  44.1 0.2 collective-permute-start.4
  44.3 0.1 pad_maximum_fusion
  44.4 0.4 collective-permute-start.14
  44.8 1.2 %collective-permute-done.4 = bf16[1024,256]{1,0:T(8,128)(2,1)S(1)} collective-permute-done((bf16[1024,256]{1,0:T(8,128)(2,1)S(1)}, bf16[1024,256]{1,0:T(8,128)(2,1)S(1)}, u32[]{:S(2)}, u32[]{:S(2)}) %collective-permute-start.4) | collective-permute-done | bytes 524320 | tf_op jit(solution)/shard_map/ppermute | solution.py:30
  46.0 0.1 convert_add_fusion
  46.2 0.2 collective-permute-start.5
  46.3 1.7 %collective-permute-start.6 = (bf16[256,256]{1,0:T(8,128)(2,1)S(1)}, bf16[256,256]{1,0:T(8,128)(2,1)S(1)}, u32[]{:S(2)}, u32[]{:S(2)}) collective-permute-start(bf16[256,256]{1,0:T(8,128)(2,1)S(1)} %get-tuple-element.121), channel_id=1, source_target_pairs={{0,1},{1,0},{2,3},{3,2},{4,5},{5,4},{6,7},{7,6},{8,9},{9,8},{10,11... | collective-permute-start | bytes 393224 | tf_op jit(solution)/shard_map/ppermute | solution.py:30
  48.1 1.7 %collective-permute-start.7 = (bf16[256,256]{1,0:T(8,128)(2,1)S(1)}, bf16[256,256]{1,0:T(8,128)(2,1)S(1)}, u32[]{:S(2)}, u32[]{:S(2)}) collective-permute-start(bf16[256,256]{1,0:T(8,128)(2,1)S(1)} %get-tuple-element.120), channel_id=1, source_target_pairs={{0,5},{1,4},{2,7},{3,6},{4,1},{5,0},{6,3},{7,2},{8,13},{9,12},{10,... | collective-permute-start | bytes 393224 | tf_op jit(solution)/shard_map/ppermute | solution.py:30
  49.7 4.3 %kernel_grad.2.given_ref = f32[32,256]{1,0:T(8,128)S(1)} custom-call(s32[1]{0:T(128)} %bitcast.core_ref, bf16[32,112,256]{2,1,0:T(8,128)(2,1)S(1)} %copy-done, bf16[32,64,256]{2,1,0:T(8,128)(2,1)S(1)} %collective-permute-done.near_ref.far_ref, bf16[16,64,256]{2,1,0:T(8,128)(2,1)S(1)} %collective-permute-done.2.far_ref, ...), custom_call_target="tpu_custom_call" | custom-call | flops 5119672320 | bytes 3670016 | tf_op jit(solution)/shard_map/kernel_grad/pallas_call | solution.py:487
  54.1 0.0 collective-permute-done.5
  54.1 0.0 collective-permute-done.6
  54.1 1.5 %collective-permute-done.7 = bf16[256,256]{1,0:T(8,128)(2,1)S(1)} collective-permute-done((bf16[256,256]{1,0:T(8,128)(2,1)S(1)}, bf16[256,256]{1,0:T(8,128)(2,1)S(1)}, u32[]{:S(2)}, u32[]{:S(2)}) %collective-permute-start.7) | collective-permute-done | bytes 131104 | tf_op jit(solution)/shard_map/ppermute | solution.py:30
  55.6 0.1 fusion.1
  55.7 3.8 %collective-permute-start.10 = (bf16[64,256]{1,0:T(8,128)(2,1)S(1)}, bf16[64,256]{1,0:T(8,128)(2,1)S(1)}, u32[]{:S(2)}, u32[]{:S(2)}) collective-permute-start(bf16[64,256]{1,0:T(8,128)(2,1)S(1)} %get-tuple-element.95), channel_id=1, source_target_pairs={{0,24},{1,25},{2,26},{3,27},{4,28},{5,29},{6,30},{7,31},{8,16},{9,... | collective-permute-start | bytes 98312 | tf_op jit(solution)/shard_map/ppermute | solution.py:30
  59.5 0.0 collective-permute-start.8
  59.5 0.6 collective-permute-start.9
  60.2 4.3 %kernel_grad.3 = f32[32,256]{1,0:T(8,128)S(1)} custom-call(s32[1]{0:T(128)} %bitcast.core_ref, bf16[32,112,256]{2,1,0:T(8,128)(2,1)S(1)} %copy-done, bf16[32,64,256]{2,1,0:T(8,128)(2,1)S(1)} %collective-permute-done.near_ref.far_ref, bf16[16,64,256]{2,1,0:T(8,128)(2,1)S(1)} %collective-permute-done.1.far_ref, ...), custom_call_target="tpu_custom_call" | custom-call | flops 5119672320 | bytes 3670016 | tf_op jit(solution)/shard_map/kernel_grad/pallas_call | solution.py:487
  64.5 1.5 %collective-permute-start.15 = (bf16[16,64,256]{2,1,0:T(8,128)(2,1)S(1)}, bf16[16,64,256]{2,1,0:T(8,128)(2,1)S(1)}, u32[]{:S(2)}, u32[]{:S(2)}) collective-permute-start(bf16[16,64,256]{2,1,0:T(8,128)(2,1)S(1)} %get-tuple-element.104), channel_id=1, source_target_pairs={{0,30},{2,4},{4,2},{6,8},{8,6},{10,12},{12,10},{14,16},{16,14},{18... | collective-permute-start | bytes 1572872 | tf_op jit(solution)/shard_map/ppermute | solution.py:40
  66.1 0.0 collective-permute-done.10
  66.1 0.0 collective-permute-done.8
  66.1 0.0 collective-permute-done.9
  66.1 0.3 collective-permute-start.11
  66.5 2.6 %collective-permute-start.12 = (bf16[96,256]{1,0:T(8,128)(2,1)S(1)}, bf16[96,256]{1,0:T(8,128)(2,1)S(1)}, u32[]{:S(2)}, u32[]{:S(2)}) collective-permute-start(bf16[96,256]{1,0:T(8,128)(2,1)S(1)} %pad_maximum_fusion.3), channel_id=1, source_target_pairs={{0,16},{1,17},{2,18},{3,19},{4,20},{5,21},{6,22},{7,23},{8,24},{9,... | collective-permute-start | bytes 147464 | tf_op jit(solution)/shard_map/ppermute | solution.py:30
  69.1 1.5 %collective-permute-start.13 = (bf16[96,256]{1,0:T(8,128)(2,1)S(1)}, bf16[96,256]{1,0:T(8,128)(2,1)S(1)}, u32[]{:S(2)}, u32[]{:S(2)}) collective-permute-start(bf16[96,256]{1,0:T(8,128)(2,1)S(1)} %pad_maximum_fusion.3), channel_id=1, source_target_pairs={{0,24},{1,25},{2,26},{3,27},{4,28},{5,29},{6,30},{7,31},{8,16},{9,... | collective-permute-start | bytes 147464 | tf_op jit(solution)/shard_map/ppermute | solution.py:30
  70.6 0.0 collective-permute-done.14.near_ref
  70.6 5.2 %backward.2.refs_0_ = bf16[32,112,256]{2,1,0:T(8,128)(2,1)} custom-call(s32[1]{0:T(128)} %bitcast.core_ref, f32[32,112,256]{2,1,0:T(8,128)S(1)} %get-tuple-element.91.grad_ref, bf16[32,64,256]{2,1,0:T(8,128)(2,1)S(1)} %collective-permute-done.14.near_ref, bf16[16,64,256]{2,1,0:T(8,128)(2,1)S(1)} %collective-permute-done.3.far_ref, ...), custom_call_target="tpu_custom_call" | custom-call | flops 5119672320 | bytes 4587520 | tf_op jit(solution)/shard_map/backward/pallas_call | solution.py:533
  75.8 0.0 collective-permute-done.11
  75.8 0.9 collective-permute-done.12
  76.7 1.9 %collective-permute-done.13 = bf16[96,256]{1,0:T(8,128)(2,1)S(1)} collective-permute-done((bf16[96,256]{1,0:T(8,128)(2,1)S(1)}, bf16[96,256]{1,0:T(8,128)(2,1)S(1)}, u32[]{:S(2)}, u32[]{:S(2)}) %collective-permute-start.13) | collective-permute-done | bytes 49184 | tf_op jit(solution)/shard_map/ppermute | solution.py:30
  78.7 0.0 collective-permute-done.15.far_ref
  78.8 1.3 %collective-permute-start.16 = (bf16[288,256]{1,0:T(8,128)(2,1)S(1)}, bf16[288,256]{1,0:T(8,128)(2,1)S(1)}, u32[]{:S(2)}, u32[]{:S(2)}) collective-permute-start(bf16[288,256]{1,0:T(8,128)(2,1)S(1)} %pad_maximum_fusion.2), channel_id=1, source_target_pairs={{0,4},{1,5},{2,6},{3,7},{4,0},{5,1},{6,2},{7,3},{8,12},{9,13},{10,... | collective-permute-start | bytes 442376 | tf_op jit(solution)/shard_map/ppermute | solution.py:30
  80.1 0.8 collective-permute-start.17
  80.9 1.4 %collective-permute-start.18 = (bf16[288,256]{1,0:T(8,128)(2,1)S(1)}, bf16[288,256]{1,0:T(8,128)(2,1)S(1)}, u32[]{:S(2)}, u32[]{:S(2)}) collective-permute-start(bf16[288,256]{1,0:T(8,128)(2,1)S(1)} %pad_maximum_fusion.2), channel_id=1, source_target_pairs={{0,5},{1,4},{2,7},{3,6},{4,1},{5,0},{6,3},{7,2},{8,13},{9,12},{10,... | collective-permute-start | bytes 442376 | tf_op jit(solution)/shard_map/ppermute | solution.py:30
  82.3 5.1 %backward.3 = bf16[32,112,256]{2,1,0:T(8,128)(2,1)} custom-call(s32[1]{0:T(128)} %bitcast.core_ref, f32[32,112,256]{2,1,0:T(8,128)S(1)} %get-tuple-element.91.grad_ref, bf16[32,64,256]{2,1,0:T(8,128)(2,1)S(1)} %collective-permute-done.14.near_ref, bf16[16,64,256]{2,1,0:T(8,128)(2,1)S(1)} %collective-permute-done.15.far_ref, ...), custom_call_target="tpu_custom_call", output_to_operand_aliasing={{}: (6, {})} | custom-call | flops 5119672320 | bytes 4587520 | tf_op jit(solution)/shard_map/backward/pallas_call | solution.py:533
  87.5 0.0 collective-permute-done.16
  87.5 1.3 %collective-permute-done.17 = bf16[288,256]{1,0:T(8,128)(2,1)S(1)} collective-permute-done((bf16[288,256]{1,0:T(8,128)(2,1)S(1)}, bf16[288,256]{1,0:T(8,128)(2,1)S(1)}, u32[]{:S(2)}, u32[]{:S(2)}) %collective-permute-start.17) | collective-permute-done | bytes 147488 | tf_op jit(solution)/shard_map/ppermute | solution.py:30
  88.9 0.0 collective-permute-done.18
  89.0 0.1 collective-permute-start.19
  89.1 1.2 %copy.32 = bf16[32,112,256]{2,1,0:T(8,128)(2,1)} copy(bf16[32,112,256]{2,1,0:T(8,128)(2,1)S(1)} %get-tuple-element.125) | data formatting | bytes 3670016
  90.3 0.7 collective-permute-done.19.got_ref.tail_ref
  91.0 1.9 %finish.1 = (f32[256,1024]{1,0:T(8,128)}, f32[1024,256]{1,0:T(8,128)}, f32[31,256]{1,0:T(8,128)}) custom-call(s32[1]{0:T(128)} %bitcast.core_ref, bf16[1056,256]{1,0:T(8,128)(2,1)S(1)} %pad_maximum_fusion.1.own_ref, bf16[1056,256]{1,0:T(8,128)(2,1)S(1)} %collective-permute-done.19.got_ref.tail_ref, ...), custom_call_target="tpu_custom_call" | custom-call | tf_op jit(solution)/shard_map/finish/pallas_call | solution.py:565
  (22 shorter events, 0.4 us)
Async XLA Ops:
  0.6 8.2 %copy-start = (bf16[32,112,256]{2,1,0:T(8,128)(2,1)S(1)}, bf16[32,112,256]{2,1,0:T(8,128)(2,1)}, u32[]{:S(2)}) copy-start(bf16[32,112,256]{2,1,0:T(8,128)(2,1)} %fields_ref.5) | copy-start | bytes 5505028
  0.7 8.2 %copy-start.2 = (bf16[256,1024]{1,0:T(8,128)(2,1)S(1)}, bf16[256,1024]{1,0:T(8,128)(2,1)}, u32[]{:S(2)}) copy-start(bf16[256,1024]{1,0:T(8,128)(2,1)} %up_ref.5) | copy-start | bytes 1572868
  0.7 8.2 %copy-start.3 = (bf16[1024,256]{1,0:T(8,128)(2,1)S(1)}, bf16[1024,256]{1,0:T(8,128)(2,1)}, u32[]{:S(2)}) copy-start(bf16[1024,256]{1,0:T(8,128)(2,1)} %down_ref.5) | copy-start | bytes 1572868
  0.7 8.2 %copy-start.4 = (f32[31,256]{1,0:T(8,128)S(1)}, f32[31,256]{1,0:T(8,128)}, u32[]{:S(2)}) copy-start(f32[31,256]{1,0:T(8,128)} %kernel_ref.11) | copy-start | bytes 95236
  2.5 6.3 %collective-permute-start = (bf16[32,64,256]{2,1,0:T(8,128)(2,1)S(1)}, bf16[32,64,256]{2,1,0:T(8,128)(2,1)S(1)}, u32[]{:S(2)}, u32[]{:S(2)}) collective-permute-start(bf16[32,64,256]{2,1,0:T(8,128)(2,1)S(1)} %get-tuple-element.118), channel_id=1, source_target_pairs={{0,2},{1,3},{2,0},{3,1},{4,6},{5,7},{6,4},{7,5},{8,10},{9,11},{10,... | collective-permute-start | bytes 3145736 | tf_op jit(solution)/shard_map/ppermute | solution.py:30
  3.1 15.6 %copy-start.1 = (bf16[32,112,256]{2,1,0:T(8,128)(2,1)S(1)}, bf16[32,112,256]{2,1,0:T(8,128)(2,1)}, u32[]{:S(2)}) copy-start(bf16[32,112,256]{2,1,0:T(8,128)(2,1)} %cot_ref.9) | copy-start | bytes 5505028
  3.1 23.5 %collective-permute-start.2 = (bf16[16,64,256]{2,1,0:T(8,128)(2,1)S(1)}, bf16[16,64,256]{2,1,0:T(8,128)(2,1)S(1)}, u32[]{:S(2)}, u32[]{:S(2)}) collective-permute-start(bf16[16,64,256]{2,1,0:T(8,128)(2,1)S(1)} %slice.72), channel_id=1, source_target_pairs={{0,30},{2,4},{4,2},{6,8},{8,6},{10,12},{12,10},{14,16},{16,14},{18... | collective-permute-start | bytes 1572872 | tf_op jit(solution)/shard_map/ppermute | solution.py:40
  16.5 18.5 %collective-permute-start.1 = (bf16[16,64,256]{2,1,0:T(8,128)(2,1)S(1)}, bf16[16,64,256]{2,1,0:T(8,128)(2,1)S(1)}, u32[]{:S(2)}, u32[]{:S(2)}) collective-permute-start(bf16[16,64,256]{2,1,0:T(8,128)(2,1)S(1)} %slice.56), channel_id=1, source_target_pairs={{0,30},{2,4},{4,2},{6,8},{8,6},{10,12},{12,10},{14,16},{16,14},{18... | collective-permute-start | bytes 1572872 | tf_op jit(solution)/shard_map/ppermute | solution.py:40
  32.6 11.5 %collective-permute-start.3 = (bf16[16,64,256]{2,1,0:T(8,128)(2,1)S(1)}, bf16[16,64,256]{2,1,0:T(8,128)(2,1)S(1)}, u32[]{:S(2)}, u32[]{:S(2)}) collective-permute-start(bf16[16,64,256]{2,1,0:T(8,128)(2,1)S(1)} %get-tuple-element.79), channel_id=1, source_target_pairs={{0,30},{2,4},{4,2},{6,8},{8,6},{10,12},{12,10},{14,16},{16,14},{18... | collective-permute-start | bytes 1572872 | tf_op jit(solution)/shard_map/ppermute | solution.py:40
  44.1 1.9 %collective-permute-start.4 = (bf16[1024,256]{1,0:T(8,128)(2,1)S(1)}, bf16[1024,256]{1,0:T(8,128)(2,1)S(1)}, u32[]{:S(2)}, u32[]{:S(2)}) collective-permute-start(bf16[1024,256]{1,0:T(8,128)(2,1)S(1)} %get-tuple-element.80), channel_id=1, source_target_pairs={{0,2},{1,3},{2,0},{3,1},{4,6},{5,7},{6,4},{7,5},{8,10},{9,11},{10,... | collective-permute-start | bytes 1572872 | tf_op jit(solution)/shard_map/ppermute | solution.py:30
  44.4 26.2 %collective-permute-start.14 = (bf16[32,64,256]{2,1,0:T(8,128)(2,1)S(1)}, bf16[32,64,256]{2,1,0:T(8,128)(2,1)S(1)}, u32[]{:S(2)}, u32[]{:S(2)}) collective-permute-start(bf16[32,64,256]{2,1,0:T(8,128)(2,1)S(1)} %pad_maximum_fusion), channel_id=1, source_target_pairs={{0,2},{1,3},{2,0},{3,1},{4,6},{5,7},{6,4},{7,5},{8,10},{9,11},{10,... | collective-permute-start | bytes 3145736 | tf_op jit(solution)/shard_map/ppermute | solution.py:30
  46.2 7.9 %collective-permute-start.5 = (bf16[256,256]{1,0:T(8,128)(2,1)S(1)}, bf16[256,256]{1,0:T(8,128)(2,1)S(1)}, u32[]{:S(2)}, u32[]{:S(2)}) collective-permute-start(bf16[256,256]{1,0:T(8,128)(2,1)S(1)} %get-tuple-element.119), channel_id=1, source_target_pairs={{0,4},{1,5},{2,6},{3,7},{4,0},{5,1},{6,2},{7,3},{8,12},{9,13},{10,... | collective-permute-start | bytes 393224 | tf_op jit(solution)/shard_map/ppermute | solution.py:30
  46.3 7.8 %collective-permute-start.6 = (bf16[256,256]{1,0:T(8,128)(2,1)S(1)}, bf16[256,256]{1,0:T(8,128)(2,1)S(1)}, u32[]{:S(2)}, u32[]{:S(2)}) collective-permute-start(bf16[256,256]{1,0:T(8,128)(2,1)S(1)} %get-tuple-element.121), channel_id=1, source_target_pairs={{0,1},{1,0},{2,3},{3,2},{4,5},{5,4},{6,7},{7,6},{8,9},{9,8},{10,11... | collective-permute-start | bytes 393224 | tf_op jit(solution)/shard_map/ppermute | solution.py:30
  48.1 7.5 %collective-permute-start.7 = (bf16[256,256]{1,0:T(8,128)(2,1)S(1)}, bf16[256,256]{1,0:T(8,128)(2,1)S(1)}, u32[]{:S(2)}, u32[]{:S(2)}) collective-permute-start(bf16[256,256]{1,0:T(8,128)(2,1)S(1)} %get-tuple-element.120), channel_id=1, source_target_pairs={{0,5},{1,4},{2,7},{3,6},{4,1},{5,0},{6,3},{7,2},{8,13},{9,12},{10,... | collective-permute-start | bytes 393224 | tf_op jit(solution)/shard_map/ppermute | solution.py:30
  55.7 10.4 %collective-permute-start.10 = (bf16[64,256]{1,0:T(8,128)(2,1)S(1)}, bf16[64,256]{1,0:T(8,128)(2,1)S(1)}, u32[]{:S(2)}, u32[]{:S(2)}) collective-permute-start(bf16[64,256]{1,0:T(8,128)(2,1)S(1)} %get-tuple-element.95), channel_id=1, source_target_pairs={{0,24},{1,25},{2,26},{3,27},{4,28},{5,29},{6,30},{7,31},{8,16},{9,... | collective-permute-start | bytes 98312 | tf_op jit(solution)/shard_map/ppermute | solution.py:30
  59.5 6.6 %collective-permute-start.8 = (bf16[64,256]{1,0:T(8,128)(2,1)S(1)}, bf16[64,256]{1,0:T(8,128)(2,1)S(1)}, u32[]{:S(2)}, u32[]{:S(2)}) collective-permute-start(bf16[64,256]{1,0:T(8,128)(2,1)S(1)} %get-tuple-element.93), channel_id=1, source_target_pairs={{0,8},{1,9},{2,10},{3,11},{4,12},{5,13},{6,14},{7,15},{8,0},{9,1},... | collective-permute-start | bytes 98312 | tf_op jit(solution)/shard_map/ppermute | solution.py:30
  59.5 6.6 %collective-permute-start.9 = (bf16[64,256]{1,0:T(8,128)(2,1)S(1)}, bf16[64,256]{1,0:T(8,128)(2,1)S(1)}, u32[]{:S(2)}, u32[]{:S(2)}) collective-permute-start(bf16[64,256]{1,0:T(8,128)(2,1)S(1)} %get-tuple-element.94), channel_id=1, source_target_pairs={{0,16},{1,17},{2,18},{3,19},{4,20},{5,21},{6,22},{7,23},{8,24},{9,... | collective-permute-start | bytes 98312 | tf_op jit(solution)/shard_map/ppermute | solution.py:30
  64.5 14.2 %collective-permute-start.15 = (bf16[16,64,256]{2,1,0:T(8,128)(2,1)S(1)}, bf16[16,64,256]{2,1,0:T(8,128)(2,1)S(1)}, u32[]{:S(2)}, u32[]{:S(2)}) collective-permute-start(bf16[16,64,256]{2,1,0:T(8,128)(2,1)S(1)} %get-tuple-element.104), channel_id=1, source_target_pairs={{0,30},{2,4},{4,2},{6,8},{8,6},{10,12},{12,10},{14,16},{16,14},{18... | collective-permute-start | bytes 1572872 | tf_op jit(solution)/shard_map/ppermute | solution.py:40
  66.1 9.7 %collective-permute-start.11 = (bf16[96,256]{1,0:T(8,128)(2,1)S(1)}, bf16[96,256]{1,0:T(8,128)(2,1)S(1)}, u32[]{:S(2)}, u32[]{:S(2)}) collective-permute-start(bf16[96,256]{1,0:T(8,128)(2,1)S(1)} %pad_maximum_fusion.3), channel_id=1, source_target_pairs={{0,8},{1,9},{2,10},{3,11},{4,12},{5,13},{6,14},{7,15},{8,0},{9,1},... | collective-permute-start | bytes 147464 | tf_op jit(solution)/shard_map/ppermute | solution.py:30
  66.5 10.3 %collective-permute-start.12 = (bf16[96,256]{1,0:T(8,128)(2,1)S(1)}, bf16[96,256]{1,0:T(8,128)(2,1)S(1)}, u32[]{:S(2)}, u32[]{:S(2)}) collective-permute-start(bf16[96,256]{1,0:T(8,128)(2,1)S(1)} %pad_maximum_fusion.3), channel_id=1, source_target_pairs={{0,16},{1,17},{2,18},{3,19},{4,20},{5,21},{6,22},{7,23},{8,24},{9,... | collective-permute-start | bytes 147464 | tf_op jit(solution)/shard_map/ppermute | solution.py:30
  69.1 9.6 %collective-permute-start.13 = (bf16[96,256]{1,0:T(8,128)(2,1)S(1)}, bf16[96,256]{1,0:T(8,128)(2,1)S(1)}, u32[]{:S(2)}, u32[]{:S(2)}) collective-permute-start(bf16[96,256]{1,0:T(8,128)(2,1)S(1)} %pad_maximum_fusion.3), channel_id=1, source_target_pairs={{0,24},{1,25},{2,26},{3,27},{4,28},{5,29},{6,30},{7,31},{8,16},{9,... | collective-permute-start | bytes 147464 | tf_op jit(solution)/shard_map/ppermute | solution.py:30
  78.8 8.8 %collective-permute-start.16 = (bf16[288,256]{1,0:T(8,128)(2,1)S(1)}, bf16[288,256]{1,0:T(8,128)(2,1)S(1)}, u32[]{:S(2)}, u32[]{:S(2)}) collective-permute-start(bf16[288,256]{1,0:T(8,128)(2,1)S(1)} %pad_maximum_fusion.2), channel_id=1, source_target_pairs={{0,4},{1,5},{2,6},{3,7},{4,0},{5,1},{6,2},{7,3},{8,12},{9,13},{10,... | collective-permute-start | bytes 442376 | tf_op jit(solution)/shard_map/ppermute | solution.py:30
  80.1 8.8 %collective-permute-start.17 = (bf16[288,256]{1,0:T(8,128)(2,1)S(1)}, bf16[288,256]{1,0:T(8,128)(2,1)S(1)}, u32[]{:S(2)}, u32[]{:S(2)}) collective-permute-start(bf16[288,256]{1,0:T(8,128)(2,1)S(1)} %pad_maximum_fusion.2), channel_id=1, source_target_pairs={{0,1},{1,0},{2,3},{3,2},{4,5},{5,4},{6,7},{7,6},{8,9},{9,8},{10,11... | collective-permute-start | bytes 442376 | tf_op jit(solution)/shard_map/ppermute | solution.py:30
  80.9 8.0 %collective-permute-start.18 = (bf16[288,256]{1,0:T(8,128)(2,1)S(1)}, bf16[288,256]{1,0:T(8,128)(2,1)S(1)}, u32[]{:S(2)}, u32[]{:S(2)}) collective-permute-start(bf16[288,256]{1,0:T(8,128)(2,1)S(1)} %pad_maximum_fusion.2), channel_id=1, source_target_pairs={{0,5},{1,4},{2,7},{3,6},{4,1},{5,0},{6,3},{7,2},{8,13},{9,12},{10,... | collective-permute-start | bytes 442376 | tf_op jit(solution)/shard_map/ppermute | solution.py:30
  89.0 2.0 %collective-permute-start.19 = (bf16[1056,256]{1,0:T(8,128)(2,1)S(1)}, bf16[1056,256]{1,0:T(8,128)(2,1)S(1)}, u32[]{:S(2)}, u32[]{:S(2)}) collective-permute-start(bf16[1056,256]{1,0:T(8,128)(2,1)S(1)} %pad_maximum_fusion.1.own_ref), channel_id=1, source_target_pairs={{0,2},{1,3},{2,0},{3,1},{4,6},{5,7},{6,4},{7,5},{8,10},{9,11},{10,... | collective-permute-start | bytes 1622024 | tf_op jit(solution)/shard_map/ppermute | solution.py:30

commit v4 on v3

--- a/solution.py
+++ b/solution.py
@@ -9,7 +9,7 @@
 from jax.sharding import PartitionSpec as P
 
 KERNEL_SPACING = 4
-BLOCK = 8
+BLOCK = 4
 NEAR_BLOCK = 16
 FAR_BLOCK = 16
 AXES = ("lon", "lat")
@@ -61,11 +61,12 @@
     return [piece(parts, p).astype(BF16) for p in places[1:]], piece(parts, places[0])
 
 
-def scatter_finish(sends, total, group):
+def scatter_finish(sends, total, group, beside):
     _, masks = group
-    for send, mask in zip(sends, masks[1:]):
-        total = total + xor_permute(send, mask).astype(F32)
-    return total
+    got, beside = lax.optimization_barrier(([xor_permute(v, m) for v, m in zip(sends, masks[1:])], beside))
+    for part in got:
+        total = total + part.astype(F32)
+    return total, beside
 
 
 def gather_finish(packed, extra, group, beside):
@@ -289,7 +290,7 @@
     step = pl.program_id(0)
     _, cols, channels = inner_ref.shape
     edge, taps = far_ref.shape[1], kernel_ref.shape[0]
-    rows = FAR_BLOCK if reach else NEAR_BLOCK
+    rows = far_ref.shape[0] if reach else NEAR_BLOCK
     base_row = start + step * rows
     here = pl.ds(base_row, rows)
     even = core_ref[0] == 0
@@ -401,7 +402,7 @@
     count = edge if reach else cols - edge
     cells = (end - begin) * count
     last = reach and end == rows
-    block = FAR_BLOCK if reach else NEAR_BLOCK
+    block = end - begin if reach else NEAR_BLOCK
     own = row_spec(block, edge, channels)
     sums = [(hid // 256, channels, 256), (channels, hid)]
     ends = [((hid, channels), F32), ((hid, channels), BF16)] if last else [(s, F32) for s in sums]
@@ -492,7 +493,7 @@
         scratch_shapes=staging(cols, edge, channels) + [pltpu.VMEM((taps, 8, channels), F32)],
         compiler_params=pltpu.CompilerParams(vmem_limit_bytes=8 * 2**20),
         cost_estimate=pl.CostEstimate(
-            flops=360 * taps * count * cols * channels, transcendentals=0,
+            flops=60 * taps * count * cols * channels, transcendentals=0,
             bytes_accessed=count * cols * channels * 8,
         ),
         name="kernel_grad",
@@ -543,7 +544,7 @@
         scratch_shapes=staging(cols, edge, channels) + [pltpu.VMEM((taps, 8, channels), F32)],
         compiler_params=params(8),
         cost_estimate=pl.CostEstimate(
-            flops=360 * taps * count * cols * channels, transcendentals=0,
+            flops=60 * taps * count * cols * channels, transcendentals=0,
             bytes_accessed=count * cols * channels * 10,
         ),
         name="backward",
@@ -588,8 +589,8 @@
 
 
 def chunk_starts(rows):
-    half = rows // 2 // BLOCK * BLOCK
-    return [0, half, rows]
+    first = rows * 3 // 8 // BLOCK * BLOCK
+    return [0, first, rows]
 
 
 def with_places(fields):
@@ -648,21 +649,21 @@
     sends, total = scatter_stage(part, plane)
     kgrad = after(kgrad, *sends)
     kgrad = add_kernel_grad(kgrad, 0)
-    part = scatter_finish(sends, total, plane)
+    part, kgrad = scatter_finish(sends, total, plane, kgrad)
     part, far_edge = lax.optimization_barrier((part, far_edge))
     grad_far.append(off_chip(far_edge))
     grad_near = on_chip(jnp.concatenate(grad_near, axis=0))
     sends, total = scatter_stage(part, depth)
     sends, kgrad = lax.optimization_barrier((sends, kgrad))
     kgrad = add_kernel_grad(kgrad, 1)
-    part = scatter_finish(sends, total, depth).astype(BF16)
+    part, kgrad = scatter_finish(sends, total, depth, kgrad)
+    part = part.astype(BF16)
     packed = pack(part, kgrad)
-    packed, halo = lax.optimization_barrier((packed, grad_far[0]))
-    grad_far[0] = halo
+    grad_far, _ = lax.optimization_barrier((grad_far, packed))
     field_grad = add_field_grad((), 0)
     part, kgrad, field_grad = gather_finish(packed, kgrad, depth, field_grad)
-    packed, halo = lax.optimization_barrier((pack(part, kgrad), grad_far[1]))
-    grad_far[1] = halo
+    packed = pack(part, kgrad)
+    field_grad, grad_far[1] = lax.optimization_barrier((field_grad, after(grad_far[1], packed)))
     field_grad = add_field_grad(field_grad, 1)
     part, kgrad, field_grad = gather_finish(packed, kgrad, plane, field_grad)
     packed = pack(part, kgrad)

time: 93 us -> 90.1 us (0.969)
  waiting for transfers between devices: 10.3 us -> 6.67 us
    ppermute x4, waiting for transfers between devices: 2.64 us -> 0.01 us  [off_chip(): return lax.ppermute(value, 'lon', pairs)]
    ppermute x16, waiting for transfers between devices: 7.66 us -> 6.66 us  [xor_permute(): return lax.ppermute(value, AXES, pairs)]
  transfers between devices with their start and end apart: 20 -> 20, of which waited for: 7 -> 6; matrix products, arithmetic and copies ran while one was open for 2% -> 2% of each run, Pallas kernels for 51% -> 52%
where the time goes in v4:
time: 90.1 us; the launch traced here: 89.9 us
  Pallas kernels  48.8 us (54%)
  starting transfers between devices  29.7 us (33%)
  waiting for transfers between devices  6.67 us (7%)
  other arithmetic  2.21 us (2%)
  local copies, waits for them, and re-layouts  1.52 us (2%)
  between operations  0.97 us (1%)
    pallas_call x3, Pallas kernels, forward(): pl.pallas_call(functools.partial(forward_kernel, reach, not carried, last...  20.5 us
    ppermute x16, starting transfers between devices, xor_permute(): return lax.ppermute(value, AXES, pairs)  17.7 us
    ppermute x4, starting transfers between devices, off_chip(): return lax.ppermute(value, 'lon', pairs)  12.1 us
    pallas_call x2, Pallas kernels, backward(): pl.pallas_call(functools.partial(backward_kernel, start), grid=(count //...  10.2 us
    pallas_call x2, Pallas kernels, kernel_grad(): pl.pallas_call(functools.partial(kernel_grad_kernel, start), in_specs=[pl...  8.69 us
    pallas_call x1, Pallas kernels, inner(): pl.pallas_call(inner_kernel, in_specs=[pl.BlockSpec(memory_space=pltpu.SM...  7.6 us
    ppermute x16, waiting for transfers between devices, xor_permute(): return lax.ppermute(value, AXES, pairs)  6.66 us
    pallas_call x1, Pallas kernels, finish(): pl.pallas_call(functools.partial(finish_kernel, factor), grid=(hid // 256...  1.86 us
  transfers between devices with their start and end apart: 20, of which 6 were waited for; matrix products, arithmetic and copies ran while one was open for 2% of the time, Pallas kernels for 52%

profile of v4, /device:TPU:0, one launch (start us, length us, event | category | flops | bytes accessed | tf_op | source)
XLA Modules:
  0.0 89.9 jit_solution(10786103167901146635)
XLA Ops:
  0.6 0.0 copy-start
  0.7 0.0 copy-start.2
  0.7 0.0 copy-start.3
  0.7 0.0 copy-start.4
  0.7 1.8 %broadcast_select_fusion = (bf16[32,64,256]{2,1,0:T(8,128)(2,1)S(1)}, bf16[32,64,256]{2,1,0:T(8,128)(2,1)S(1)}) fusion(pred[]{:T(512)S(6)} %eq.3, bf16[32,112,256]{2,1,0:T(8,128)(2,1)} %fields_ref.5), kind=kLoop, calls=%fused_computation.2 | loop fusion | flops 1048576 | bytes 4194305 | tf_op jit(solution)/shard_map/jit(_where)/select_n | solution.py:613
  2.5 0.5 collective-permute-start
  3.1 0.0 copy-start.1
  3.1 5.7 %collective-permute-start.2 = (bf16[12,64,256]{2,1,0:T(8,128)(2,1)S(1)}, bf16[12,64,256]{2,1,0:T(8,128)(2,1)S(1)}, u32[]{:S(2)}, u32[]{:S(2)}) collective-permute-start(bf16[12,64,256]{2,1,0:T(8,128)(2,1)S(1)} %slice.64), channel_id=1, source_target_pairs={{0,30},{2,4},{4,2},{6,8},{8,6},{10,12},{12,10},{14,16},{16,14},{18... | collective-permute-start | bytes 1179656 | tf_op jit(solution)/shard_map/ppermute | solution.py:40
  8.8 0.0 collective-permute-done.near_ref.far_ref
  8.8 0.0 copy-done
  8.8 0.0 copy-done.2
  8.8 0.0 copy-done.3
  8.8 7.6 %inner.1 = (f32[32,112,256]{2,1,0:T(8,128)S(1)}, bf16[1024,256]{1,0:T(8,128)(2,1)S(1)}, bf16[256,1024]{1,0:T(8,128)(2,1)S(1)}) custom-call(s32[1]{0:T(128)} %bitcast.core_ref, bf16[32,112,256]{2,1,0:T(8,128)(2,1)S(1)} %copy-done, bf16[32,64,256]{2,1,0:T(8,128)(2,1)S(1)} %collective-permute-done.near_ref.far_ref, f32[31,256]{1,0:T(8,128)S(1)} %copy-done.2, ...), custom_call_target="tpu_custom_call" | custom-call | flops 7395082240 | bytes 5505024 | tf_op jit(solution)/shard_map/inner/pallas_call | solution.py:253
  16.4 0.1 slice.50
  16.5 2.2 %collective-permute-start.1 = (bf16[20,64,256]{2,1,0:T(8,128)(2,1)S(1)}, bf16[20,64,256]{2,1,0:T(8,128)(2,1)S(1)}, u32[]{:S(2)}, u32[]{:S(2)}) collective-permute-start(bf16[20,64,256]{2,1,0:T(8,128)(2,1)S(1)} %slice.50), channel_id=1, source_target_pairs={{0,30},{2,4},{4,2},{6,8},{8,6},{10,12},{12,10},{14,16},{16,14},{18... | collective-permute-start | bytes 1966088 | tf_op jit(solution)/shard_map/ppermute | solution.py:40
  18.7 0.0 copy-done.1
  18.7 7.9 %forward.3 = (bf16[32,112,256]{2,1,0:T(8,128)(2,1)S(1)}, f32[32,112,256]{2,1,0:T(8,128)S(1)}, f32[4,256,256]{2,1,0:T(8,128)S(1)}, f32[256,1024]{1,0:T(8,128)S(1)}) custom-call(s32[1]{0:T(128)} %bitcast.core_ref, f32[32,112,256]{2,1,0:T(8,128)S(1)} %get-tuple-element.73.inner_ref, bf16[32,64,256]{2,1,0:T(8,128)(2,1)S(1)} %collective-permute-done.near_ref.far_ref, ...), custom_call_target="tpu_custom_call" | custom-call | flops 11274289152 | bytes 4718592 | tf_op jit(solution)/shard_map/forward/pallas_call | solution.py:411
  26.6 0.0 collective-permute-done.2.far_ref
  26.7 4.6 %forward.4 = (bf16[32,112,256]{2,1,0:T(8,128)(2,1)S(1)}, f32[32,112,256]{2,1,0:T(8,128)S(1)}, f32[4,256,256]{2,1,0:T(8,128)S(1)}, f32[256,1024]{1,0:T(8,128)S(1)...) custom-call(s32[1]{0:T(128)} %bitcast.core_ref, ...), custom_call_target="tpu_custom_call", output_to_operand_aliasing={{0}: (10, {}), {1}: (11, {}), {2}: (12, {}), {3}: (13, {})} | custom-call | flops 5637144576 | bytes 2359296 | tf_op jit(solution)/shard_map/forward/pallas_call | solution.py:411
  31.3 2.4 %collective-permute-start.3 = (bf16[12,64,256]{2,1,0:T(8,128)(2,1)S(1)}, bf16[12,64,256]{2,1,0:T(8,128)(2,1)S(1)}, u32[]{:S(2)}, u32[]{:S(2)}) collective-permute-start(bf16[12,64,256]{2,1,0:T(8,128)(2,1)S(1)} %get-tuple-element.88), channel_id=1, source_target_pairs={{0,30},{2,4},{4,2},{6,8},{8,6},{10,12},{12,10},{14,16},{16,14},{18... | collective-permute-start | bytes 1179656 | tf_op jit(solution)/shard_map/ppermute | solution.py:40
  33.7 0.0 collective-permute-done.1.far_ref
  33.7 7.9 %forward.5 = (bf16[32,112,256]{2,1,0:T(8,128)(2,1)S(1)}, f32[32,112,256]{2,1,0:T(8,128)S(1)}, f32[1024,256]{1,0:T(8,128)S(1)}, bf16[1024,256]{1,0:T(8,128)(2,1)S...) custom-call(s32[1]{0:T(128)} %bitcast.core_ref, ...), custom_call_target="tpu_custom_call", output_to_operand_aliasing={{0}: (10, {}), {1}: (11, {})} | custom-call | flops 9395240960 | bytes 3932160 | tf_op jit(solution)/shard_map/forward/pallas_call | solution.py:411
  41.6 0.0 collective-permute-done.3.far_ref
  41.6 0.1 collective-permute-start.4
  41.7 0.1 pad_maximum_fusion
  41.8 0.6 collective-permute-start.14
  42.3 1.2 %collective-permute-done.4 = bf16[1024,256]{1,0:T(8,128)(2,1)S(1)} collective-permute-done((bf16[1024,256]{1,0:T(8,128)(2,1)S(1)}, bf16[1024,256]{1,0:T(8,128)(2,1)S(1)}, u32[]{:S(2)}, u32[]{:S(2)}) %collective-permute-start.4) | collective-permute-done | bytes 524320 | tf_op jit(solution)/shard_map/ppermute | solution.py:30
  43.6 0.1 convert_add_fusion
  43.7 0.1 collective-permute-start.5
  43.8 1.6 %collective-permute-start.6 = (bf16[256,256]{1,0:T(8,128)(2,1)S(1)}, bf16[256,256]{1,0:T(8,128)(2,1)S(1)}, u32[]{:S(2)}, u32[]{:S(2)}) collective-permute-start(bf16[256,256]{1,0:T(8,128)(2,1)S(1)} %get-tuple-element.140), channel_id=1, source_target_pairs={{0,1},{1,0},{2,3},{3,2},{4,5},{5,4},{6,7},{7,6},{8,9},{9,8},{10,11... | collective-permute-start | bytes 393224 | tf_op jit(solution)/shard_map/ppermute | solution.py:30
  45.4 1.9 %collective-permute-start.7 = (bf16[256,256]{1,0:T(8,128)(2,1)S(1)}, bf16[256,256]{1,0:T(8,128)(2,1)S(1)}, u32[]{:S(2)}, u32[]{:S(2)}) collective-permute-start(bf16[256,256]{1,0:T(8,128)(2,1)S(1)} %get-tuple-element.139), channel_id=1, source_target_pairs={{0,5},{1,4},{2,7},{3,6},{4,1},{5,0},{6,3},{7,2},{8,13},{9,12},{10,... | collective-permute-start | bytes 393224 | tf_op jit(solution)/shard_map/ppermute | solution.py:30
  47.3 3.3 %kernel_grad.2.given_ref = f32[32,256]{1,0:T(8,128)S(1)} custom-call(s32[1]{0:T(128)} %bitcast.core_ref, bf16[32,112,256]{2,1,0:T(8,128)(2,1)S(1)} %copy-done, bf16[32,64,256]{2,1,0:T(8,128)(2,1)S(1)} %collective-permute-done.near_ref.far_ref, bf16[12,64,256]{2,1,0:T(8,128)(2,1)S(1)} %collective-permute-done.2.far_ref, ...), custom_call_target="tpu_custom_call" | custom-call | flops 639959040 | bytes 2752512 | tf_op jit(solution)/shard_map/kernel_grad/pallas_call | solution.py:488
  50.6 0.0 collective-permute-done.5
  50.6 0.0 collective-permute-done.6
  50.6 2.5 %collective-permute-done.7 = bf16[256,256]{1,0:T(8,128)(2,1)S(1)} collective-permute-done((bf16[256,256]{1,0:T(8,128)(2,1)S(1)}, bf16[256,256]{1,0:T(8,128)(2,1)S(1)}, u32[]{:S(2)}, u32[]{:S(2)}) %collective-permute-start.7) | collective-permute-done | bytes 131104 | tf_op jit(solution)/shard_map/ppermute | solution.py:30
  53.1 0.1 fusion.1
  53.2 1.8 %collective-permute-start.15 = (bf16[20,64,256]{2,1,0:T(8,128)(2,1)S(1)}, bf16[20,64,256]{2,1,0:T(8,128)(2,1)S(1)}, u32[]{:S(2)}, u32[]{:S(2)}) collective-permute-start(bf16[20,64,256]{2,1,0:T(8,128)(2,1)S(1)} %get-tuple-element.116), channel_id=1, source_target_pairs={{0,30},{2,4},{4,2},{6,8},{8,6},{10,12},{12,10},{14,16},{16,14},{18... | collective-permute-start | bytes 1966088 | tf_op jit(solution)/shard_map/ppermute | solution.py:40
  54.9 0.5 collective-permute-start.10
  55.5 0.0 collective-permute-start.8
  55.5 3.9 %collective-permute-start.9 = (bf16[64,256]{1,0:T(8,128)(2,1)S(1)}, bf16[64,256]{1,0:T(8,128)(2,1)S(1)}, u32[]{:S(2)}, u32[]{:S(2)}) collective-permute-start(bf16[64,256]{1,0:T(8,128)(2,1)S(1)} %get-tuple-element.107), channel_id=1, source_target_pairs={{0,16},{1,17},{2,18},{3,19},{4,20},{5,21},{6,22},{7,23},{8,24},{9,... | collective-permute-start | bytes 98312 | tf_op jit(solution)/shard_map/ppermute | solution.py:30
  59.4 5.4 %kernel_grad.3 = f32[32,256]{1,0:T(8,128)S(1)} custom-call(s32[1]{0:T(128)} %bitcast.core_ref, bf16[32,112,256]{2,1,0:T(8,128)(2,1)S(1)} %copy-done, bf16[32,64,256]{2,1,0:T(8,128)(2,1)S(1)} %collective-permute-done.near_ref.far_ref, bf16[20,64,256]{2,1,0:T(8,128)(2,1)S(1)} %collective-permute-done.1.far_ref, ...), custom_call_target="tpu_custom_call" | custom-call | flops 1066598400 | bytes 4587520 | tf_op jit(solution)/shard_map/kernel_grad/pallas_call | solution.py:488
  64.8 0.6 collective-permute-done.10
  65.4 0.0 collective-permute-done.8
  65.4 0.3 collective-permute-done.9
  65.7 2.2 %collective-permute-start.11 = (bf16[96,256]{1,0:T(8,128)(2,1)S(1)}, bf16[96,256]{1,0:T(8,128)(2,1)S(1)}, u32[]{:S(2)}, u32[]{:S(2)}) collective-permute-start(bf16[96,256]{1,0:T(8,128)(2,1)S(1)} %pad_maximum_fusion.3), channel_id=1, source_target_pairs={{0,8},{1,9},{2,10},{3,11},{4,12},{5,13},{6,14},{7,15},{8,0},{9,1},... | collective-permute-start | bytes 147464 | tf_op jit(solution)/shard_map/ppermute | solution.py:30
  67.9 2.2 %collective-permute-start.12 = (bf16[96,256]{1,0:T(8,128)(2,1)S(1)}, bf16[96,256]{1,0:T(8,128)(2,1)S(1)}, u32[]{:S(2)}, u32[]{:S(2)}) collective-permute-start(bf16[96,256]{1,0:T(8,128)(2,1)S(1)} %pad_maximum_fusion.3), channel_id=1, source_target_pairs={{0,16},{1,17},{2,18},{3,19},{4,20},{5,21},{6,22},{7,23},{8,24},{9,... | collective-permute-start | bytes 147464 | tf_op jit(solution)/shard_map/ppermute | solution.py:30
  70.1 0.5 collective-permute-start.13
  70.6 0.0 collective-permute-done.15.far_ref
  70.6 0.0 collective-permute-done.14.near_ref
  70.6 4.0 %backward.2.refs_0_ = bf16[32,112,256]{2,1,0:T(8,128)(2,1)} custom-call(s32[1]{0:T(128)} %bitcast.core_ref, f32[32,112,256]{2,1,0:T(8,128)S(1)} %get-tuple-element.94.grad_ref, bf16[32,64,256]{2,1,0:T(8,128)(2,1)S(1)} %collective-permute-done.14.near_ref, bf16[12,64,256]{2,1,0:T(8,128)(2,1)S(1)} %collective-permute-done.3.far_ref, ...), custom_call_target="tpu_custom_call" | custom-call | flops 639959040 | bytes 3440640 | tf_op jit(solution)/shard_map/backward/pallas_call | solution.py:534
  74.6 0.0 collective-permute-done.11
  74.6 0.0 collective-permute-done.12
  74.6 1.4 %collective-permute-done.13 = bf16[96,256]{1,0:T(8,128)(2,1)S(1)} collective-permute-done((bf16[96,256]{1,0:T(8,128)(2,1)S(1)}, bf16[96,256]{1,0:T(8,128)(2,1)S(1)}, u32[]{:S(2)}, u32[]{:S(2)}) %collective-permute-start.13) | collective-permute-done | bytes 49184 | tf_op jit(solution)/shard_map/ppermute | solution.py:30
  76.1 1.5 %collective-permute-start.16 = (bf16[288,256]{1,0:T(8,128)(2,1)S(1)}, bf16[288,256]{1,0:T(8,128)(2,1)S(1)}, u32[]{:S(2)}, u32[]{:S(2)}) collective-permute-start(bf16[288,256]{1,0:T(8,128)(2,1)S(1)} %pad_maximum_fusion.2), channel_id=1, source_target_pairs={{0,4},{1,5},{2,6},{3,7},{4,0},{5,1},{6,2},{7,3},{8,12},{9,13},{10,... | collective-permute-start | bytes 442376 | tf_op jit(solution)/shard_map/ppermute | solution.py:30
  77.6 0.6 collective-permute-start.17
  78.2 1.5 %collective-permute-start.18 = (bf16[288,256]{1,0:T(8,128)(2,1)S(1)}, bf16[288,256]{1,0:T(8,128)(2,1)S(1)}, u32[]{:S(2)}, u32[]{:S(2)}) collective-permute-start(bf16[288,256]{1,0:T(8,128)(2,1)S(1)} %pad_maximum_fusion.2), channel_id=1, source_target_pairs={{0,5},{1,4},{2,7},{3,6},{4,1},{5,0},{6,3},{7,2},{8,13},{9,12},{10,... | collective-permute-start | bytes 442376 | tf_op jit(solution)/shard_map/ppermute | solution.py:30
  79.6 6.2 %backward.3 = bf16[32,112,256]{2,1,0:T(8,128)(2,1)} custom-call(s32[1]{0:T(128)} %bitcast.core_ref, f32[32,112,256]{2,1,0:T(8,128)S(1)} %get-tuple-element.94.grad_ref, bf16[32,64,256]{2,1,0:T(8,128)(2,1)S(1)} %collective-permute-done.14.near_ref, bf16[20,64,256]{2,1,0:T(8,128)(2,1)S(1)} %collective-permute-done.15.far_ref, ...), custom_call_target="tpu_custom_call", output_to_operand_aliasing={{}: (6, {})} | custom-call | flops 1066598400 | bytes 5734400 | tf_op jit(solution)/shard_map/backward/pallas_call | solution.py:534
  85.9 0.0 collective-permute-done.16
  85.9 0.0 collective-permute-done.17
  85.9 0.0 collective-permute-done.18
  86.1 0.1 collective-permute-start.19
  86.1 1.2 %copy.32 = bf16[32,112,256]{2,1,0:T(8,128)(2,1)} copy(bf16[32,112,256]{2,1,0:T(8,128)(2,1)S(1)} %get-tuple-element.145) | data formatting | bytes 3670016
  87.4 0.7 collective-permute-done.19.got_ref.tail_ref
  88.1 1.9 %finish.1 = (f32[256,1024]{1,0:T(8,128)}, f32[1024,256]{1,0:T(8,128)}, f32[31,256]{1,0:T(8,128)}) custom-call(s32[1]{0:T(128)} %bitcast.core_ref, bf16[1056,256]{1,0:T(8,128)(2,1)S(1)} %pad_maximum_fusion.1.own_ref, bf16[1056,256]{1,0:T(8,128)(2,1)S(1)} %collective-permute-done.19.got_ref.tail_ref, ...), custom_call_target="tpu_custom_call" | custom-call | tf_op jit(solution)/shard_map/finish/pallas_call | solution.py:566
  (21 shorter events, 0.3 us)
Async XLA Ops:
  0.6 8.2 %copy-start = (bf16[32,112,256]{2,1,0:T(8,128)(2,1)S(1)}, bf16[32,112,256]{2,1,0:T(8,128)(2,1)}, u32[]{:S(2)}) copy-start(bf16[32,112,256]{2,1,0:T(8,128)(2,1)} %fields_ref.5) | copy-start | bytes 5505028
  0.7 8.1 %copy-start.2 = (f32[31,256]{1,0:T(8,128)S(1)}, f32[31,256]{1,0:T(8,128)}, u32[]{:S(2)}) copy-start(f32[31,256]{1,0:T(8,128)} %kernel_ref.11) | copy-start | bytes 95236
  0.7 8.1 %copy-start.3 = (bf16[256,1024]{1,0:T(8,128)(2,1)S(1)}, bf16[256,1024]{1,0:T(8,128)(2,1)}, u32[]{:S(2)}) copy-start(bf16[256,1024]{1,0:T(8,128)(2,1)} %up_ref.5) | copy-start | bytes 1572868
  0.7 8.1 %copy-start.4 = (bf16[1024,256]{1,0:T(8,128)(2,1)S(1)}, bf16[1024,256]{1,0:T(8,128)(2,1)}, u32[]{:S(2)}) copy-start(bf16[1024,256]{1,0:T(8,128)(2,1)} %down_ref.5) | copy-start | bytes 1572868
  2.5 6.3 %collective-permute-start = (bf16[32,64,256]{2,1,0:T(8,128)(2,1)S(1)}, bf16[32,64,256]{2,1,0:T(8,128)(2,1)S(1)}, u32[]{:S(2)}, u32[]{:S(2)}) collective-permute-start(bf16[32,64,256]{2,1,0:T(8,128)(2,1)S(1)} %get-tuple-element.138), channel_id=1, source_target_pairs={{0,2},{1,3},{2,0},{3,1},{4,6},{5,7},{6,4},{7,5},{8,10},{9,11},{10,... | collective-permute-start | bytes 3145736 | tf_op jit(solution)/shard_map/ppermute | solution.py:30
  3.1 15.6 %copy-start.1 = (bf16[32,112,256]{2,1,0:T(8,128)(2,1)S(1)}, bf16[32,112,256]{2,1,0:T(8,128)(2,1)}, u32[]{:S(2)}) copy-start(bf16[32,112,256]{2,1,0:T(8,128)(2,1)} %cot_ref.9) | copy-start | bytes 5505028
  3.1 23.6 %collective-permute-start.2 = (bf16[12,64,256]{2,1,0:T(8,128)(2,1)S(1)}, bf16[12,64,256]{2,1,0:T(8,128)(2,1)S(1)}, u32[]{:S(2)}, u32[]{:S(2)}) collective-permute-start(bf16[12,64,256]{2,1,0:T(8,128)(2,1)S(1)} %slice.64), channel_id=1, source_target_pairs={{0,30},{2,4},{4,2},{6,8},{8,6},{10,12},{12,10},{14,16},{16,14},{18... | collective-permute-start | bytes 1179656 | tf_op jit(solution)/shard_map/ppermute | solution.py:40
  16.5 17.2 %collective-permute-start.1 = (bf16[20,64,256]{2,1,0:T(8,128)(2,1)S(1)}, bf16[20,64,256]{2,1,0:T(8,128)(2,1)S(1)}, u32[]{:S(2)}, u32[]{:S(2)}) collective-permute-start(bf16[20,64,256]{2,1,0:T(8,128)(2,1)S(1)} %slice.50), channel_id=1, source_target_pairs={{0,30},{2,4},{4,2},{6,8},{8,6},{10,12},{12,10},{14,16},{16,14},{18... | collective-permute-start | bytes 1966088 | tf_op jit(solution)/shard_map/ppermute | solution.py:40
  31.3 10.3 %collective-permute-start.3 = (bf16[12,64,256]{2,1,0:T(8,128)(2,1)S(1)}, bf16[12,64,256]{2,1,0:T(8,128)(2,1)S(1)}, u32[]{:S(2)}, u32[]{:S(2)}) collective-permute-start(bf16[12,64,256]{2,1,0:T(8,128)(2,1)S(1)} %get-tuple-element.88), channel_id=1, source_target_pairs={{0,30},{2,4},{4,2},{6,8},{8,6},{10,12},{12,10},{14,16},{16,14},{18... | collective-permute-start | bytes 1179656 | tf_op jit(solution)/shard_map/ppermute | solution.py:40
  41.6 2.0 %collective-permute-start.4 = (bf16[1024,256]{1,0:T(8,128)(2,1)S(1)}, bf16[1024,256]{1,0:T(8,128)(2,1)S(1)}, u32[]{:S(2)}, u32[]{:S(2)}) collective-permute-start(bf16[1024,256]{1,0:T(8,128)(2,1)S(1)} %get-tuple-element.89), channel_id=1, source_target_pairs={{0,2},{1,3},{2,0},{3,1},{4,6},{5,7},{6,4},{7,5},{8,10},{9,11},{10,... | collective-permute-start | bytes 1572872 | tf_op jit(solution)/shard_map/ppermute | solution.py:30
  41.8 28.9 %collective-permute-start.14 = (bf16[32,64,256]{2,1,0:T(8,128)(2,1)S(1)}, bf16[32,64,256]{2,1,0:T(8,128)(2,1)S(1)}, u32[]{:S(2)}, u32[]{:S(2)}) collective-permute-start(bf16[32,64,256]{2,1,0:T(8,128)(2,1)S(1)} %pad_maximum_fusion), channel_id=1, source_target_pairs={{0,2},{1,3},{2,0},{3,1},{4,6},{5,7},{6,4},{7,5},{8,10},{9,11},{10,... | collective-permute-start | bytes 3145736 | tf_op jit(solution)/shard_map/ppermute | solution.py:30
  43.7 6.8 %collective-permute-start.5 = (bf16[256,256]{1,0:T(8,128)(2,1)S(1)}, bf16[256,256]{1,0:T(8,128)(2,1)S(1)}, u32[]{:S(2)}, u32[]{:S(2)}) collective-permute-start(bf16[256,256]{1,0:T(8,128)(2,1)S(1)} %get-tuple-element.141), channel_id=1, source_target_pairs={{0,4},{1,5},{2,6},{3,7},{4,0},{5,1},{6,2},{7,3},{8,12},{9,13},{10,... | collective-permute-start | bytes 393224 | tf_op jit(solution)/shard_map/ppermute | solution.py:30
  43.8 6.8 %collective-permute-start.6 = (bf16[256,256]{1,0:T(8,128)(2,1)S(1)}, bf16[256,256]{1,0:T(8,128)(2,1)S(1)}, u32[]{:S(2)}, u32[]{:S(2)}) collective-permute-start(bf16[256,256]{1,0:T(8,128)(2,1)S(1)} %get-tuple-element.140), channel_id=1, source_target_pairs={{0,1},{1,0},{2,3},{3,2},{4,5},{5,4},{6,7},{7,6},{8,9},{9,8},{10,11... | collective-permute-start | bytes 393224 | tf_op jit(solution)/shard_map/ppermute | solution.py:30
  45.4 7.7 %collective-permute-start.7 = (bf16[256,256]{1,0:T(8,128)(2,1)S(1)}, bf16[256,256]{1,0:T(8,128)(2,1)S(1)}, u32[]{:S(2)}, u32[]{:S(2)}) collective-permute-start(bf16[256,256]{1,0:T(8,128)(2,1)S(1)} %get-tuple-element.139), channel_id=1, source_target_pairs={{0,5},{1,4},{2,7},{3,6},{4,1},{5,0},{6,3},{7,2},{8,13},{9,12},{10,... | collective-permute-start | bytes 393224 | tf_op jit(solution)/shard_map/ppermute | solution.py:30
  53.2 17.5 %collective-permute-start.15 = (bf16[20,64,256]{2,1,0:T(8,128)(2,1)S(1)}, bf16[20,64,256]{2,1,0:T(8,128)(2,1)S(1)}, u32[]{:S(2)}, u32[]{:S(2)}) collective-permute-start(bf16[20,64,256]{2,1,0:T(8,128)(2,1)S(1)} %get-tuple-element.116), channel_id=1, source_target_pairs={{0,30},{2,4},{4,2},{6,8},{8,6},{10,12},{12,10},{14,16},{16,14},{18... | collective-permute-start | bytes 1966088 | tf_op jit(solution)/shard_map/ppermute | solution.py:40
  54.9 10.4 %collective-permute-start.10 = (bf16[64,256]{1,0:T(8,128)(2,1)S(1)}, bf16[64,256]{1,0:T(8,128)(2,1)S(1)}, u32[]{:S(2)}, u32[]{:S(2)}) collective-permute-start(bf16[64,256]{1,0:T(8,128)(2,1)S(1)} %get-tuple-element.108), channel_id=1, source_target_pairs={{0,24},{1,25},{2,26},{3,27},{4,28},{5,29},{6,30},{7,31},{8,16},{9,... | collective-permute-start | bytes 98312 | tf_op jit(solution)/shard_map/ppermute | solution.py:30
  55.5 9.9 %collective-permute-start.8 = (bf16[64,256]{1,0:T(8,128)(2,1)S(1)}, bf16[64,256]{1,0:T(8,128)(2,1)S(1)}, u32[]{:S(2)}, u32[]{:S(2)}) collective-permute-start(bf16[64,256]{1,0:T(8,128)(2,1)S(1)} %get-tuple-element.106), channel_id=1, source_target_pairs={{0,8},{1,9},{2,10},{3,11},{4,12},{5,13},{6,14},{7,15},{8,0},{9,1},... | collective-permute-start | bytes 98312 | tf_op jit(solution)/shard_map/ppermute | solution.py:30
  55.5 10.2 %collective-permute-start.9 = (bf16[64,256]{1,0:T(8,128)(2,1)S(1)}, bf16[64,256]{1,0:T(8,128)(2,1)S(1)}, u32[]{:S(2)}, u32[]{:S(2)}) collective-permute-start(bf16[64,256]{1,0:T(8,128)(2,1)S(1)} %get-tuple-element.107), channel_id=1, source_target_pairs={{0,16},{1,17},{2,18},{3,19},{4,20},{5,21},{6,22},{7,23},{8,24},{9,... | collective-permute-start | bytes 98312 | tf_op jit(solution)/shard_map/ppermute | solution.py:30
  65.7 8.9 %collective-permute-start.11 = (bf16[96,256]{1,0:T(8,128)(2,1)S(1)}, bf16[96,256]{1,0:T(8,128)(2,1)S(1)}, u32[]{:S(2)}, u32[]{:S(2)}) collective-permute-start(bf16[96,256]{1,0:T(8,128)(2,1)S(1)} %pad_maximum_fusion.3), channel_id=1, source_target_pairs={{0,8},{1,9},{2,10},{3,11},{4,12},{5,13},{6,14},{7,15},{8,0},{9,1},... | collective-permute-start | bytes 147464 | tf_op jit(solution)/shard_map/ppermute | solution.py:30
  67.9 6.7 %collective-permute-start.12 = (bf16[96,256]{1,0:T(8,128)(2,1)S(1)}, bf16[96,256]{1,0:T(8,128)(2,1)S(1)}, u32[]{:S(2)}, u32[]{:S(2)}) collective-permute-start(bf16[96,256]{1,0:T(8,128)(2,1)S(1)} %pad_maximum_fusion.3), channel_id=1, source_target_pairs={{0,16},{1,17},{2,18},{3,19},{4,20},{5,21},{6,22},{7,23},{8,24},{9,... | collective-permute-start | bytes 147464 | tf_op jit(solution)/shard_map/ppermute | solution.py:30
  70.1 5.9 %collective-permute-start.13 = (bf16[96,256]{1,0:T(8,128)(2,1)S(1)}, bf16[96,256]{1,0:T(8,128)(2,1)S(1)}, u32[]{:S(2)}, u32[]{:S(2)}) collective-permute-start(bf16[96,256]{1,0:T(8,128)(2,1)S(1)} %pad_maximum_fusion.3), channel_id=1, source_target_pairs={{0,24},{1,25},{2,26},{3,27},{4,28},{5,29},{6,30},{7,31},{8,16},{9,... | collective-permute-start | bytes 147464 | tf_op jit(solution)/shard_map/ppermute | solution.py:30
  76.1 9.8 %collective-permute-start.16 = (bf16[288,256]{1,0:T(8,128)(2,1)S(1)}, bf16[288,256]{1,0:T(8,128)(2,1)S(1)}, u32[]{:S(2)}, u32[]{:S(2)}) collective-permute-start(bf16[288,256]{1,0:T(8,128)(2,1)S(1)} %pad_maximum_fusion.2), channel_id=1, source_target_pairs={{0,4},{1,5},{2,6},{3,7},{4,0},{5,1},{6,2},{7,3},{8,12},{9,13},{10,... | collective-permute-start | bytes 442376 | tf_op jit(solution)/shard_map/ppermute | solution.py:30
  77.6 8.3 %collective-permute-start.17 = (bf16[288,256]{1,0:T(8,128)(2,1)S(1)}, bf16[288,256]{1,0:T(8,128)(2,1)S(1)}, u32[]{:S(2)}, u32[]{:S(2)}) collective-permute-start(bf16[288,256]{1,0:T(8,128)(2,1)S(1)} %pad_maximum_fusion.2), channel_id=1, source_target_pairs={{0,1},{1,0},{2,3},{3,2},{4,5},{5,4},{6,7},{7,6},{8,9},{9,8},{10,11... | collective-permute-start | bytes 442376 | tf_op jit(solution)/shard_map/ppermute | solution.py:30
  78.2 7.8 %collective-permute-start.18 = (bf16[288,256]{1,0:T(8,128)(2,1)S(1)}, bf16[288,256]{1,0:T(8,128)(2,1)S(1)}, u32[]{:S(2)}, u32[]{:S(2)}) collective-permute-start(bf16[288,256]{1,0:T(8,128)(2,1)S(1)} %pad_maximum_fusion.2), channel_id=1, source_target_pairs={{0,5},{1,4},{2,7},{3,6},{4,1},{5,0},{6,3},{7,2},{8,13},{9,12},{10,... | collective-permute-start | bytes 442376 | tf_op jit(solution)/shard_map/ppermute | solution.py:30
  86.1 2.0 %collective-permute-start.19 = (bf16[1056,256]{1,0:T(8,128)(2,1)S(1)}, bf16[1056,256]{1,0:T(8,128)(2,1)S(1)}, u32[]{:S(2)}, u32[]{:S(2)}) collective-permute-start(bf16[1056,256]{1,0:T(8,128)(2,1)S(1)} %pad_maximum_fusion.1.own_ref), channel_id=1, source_target_pairs={{0,2},{1,3},{2,0},{3,1},{4,6},{5,7},{6,4},{7,5},{8,10},{9,11},{10,... | collective-permute-start | bytes 1622024 | tf_op jit(solution)/shard_map/ppermute | solution.py:30

commit v5 on v4

--- a/solution.py
+++ b/solution.py
@@ -351,11 +351,11 @@
         part = pl.ds(j * width, width)
         h = jnp.dot(low, up_ref[:, part], preferred_element_type=F32)
         u = jnp.dot(cot, downt_ref[:, part], preferred_element_type=F32)
-        sq = h * h
-        t = jnp.tanh(h * (GELU_A + GELU_B * sq))
-        half = 0.5 * h
-        act_s[:, part] = (half + half * t).astype(BF16)
-        slope = (0.5 + 0.5 * t) + half * (1.0 - t * t) * (GELU_A + (3.0 * GELU_B) * sq)
+        inner = h * (GELU_A + GELU_B * (h * h))
+        t = jnp.tanh(inner)
+        rise = 1.0 + t
+        act_s[:, part] = (0.5 * h * rise).astype(BF16)
+        slope = rise * (0.5 + (1.0 - t) * (1.5 * inner - GELU_A * h))
         hg_s[:, part] = (u * slope).astype(BF16)
     out = jnp.dot(act_s[...], down_ref[...], preferred_element_type=F32)
     out = out + fields_ref[here, span, :].reshape(cells, channels).astype(F32)
@@ -553,25 +553,29 @@
 
 def finish_kernel(factor, core_ref, own_ref, got_ref, tail_ref, kgrad_ref, up_ref, down_ref, taps_ref):
     even = core_ref[0] == 0
-    own, got = own_ref[...].astype(F32) * factor, got_ref[...].astype(F32) * factor
-    up_ref[...] = jnp.where(even, own, got)
-    down_ref[...] = jnp.where(even, got, own)
+    width = own_ref.shape[1]
+    for j in range(own_ref.shape[0] // width):
+        part = pl.ds(j * width, width)
+        own, got = own_ref[part, :].astype(F32) * factor, got_ref[part, :].astype(F32) * factor
+        up_ref[:, part] = jnp.where(even, own, got)
+        down_ref[part, :] = jnp.where(even, got, own)
     taps = taps_ref.shape[0]
     taps_ref[...] = (kgrad_ref[pl.ds(0, taps), :] + tail_ref[pl.ds(0, taps), :].astype(F32)) * factor
 
 
 def finish(core, own, got, kgrad, taps, factor):
     hid, channels = own.shape[0] - kgrad.shape[0], own.shape[1]
-    part = pl.BlockSpec((256, channels), lambda j: (j, 0))
+    rows = hid // 2
+    part = pl.BlockSpec((rows, channels), lambda j: (j, 0))
     return pl.pallas_call(
         functools.partial(finish_kernel, factor),
-        grid=(hid // 256,),
+        grid=(hid // rows,),
         in_specs=[
             pl.BlockSpec(memory_space=pltpu.SMEM), part, part,
             pl.BlockSpec(kgrad.shape, lambda j: (hid // kgrad.shape[0], 0)), whole_spec(*kgrad.shape),
         ],
         out_specs=[
-            pl.BlockSpec((channels, 256), lambda j: (0, j)), part, whole_spec(taps, channels),
+            pl.BlockSpec((channels, rows), lambda j: (0, j)), part, whole_spec(taps, channels),
         ],
         out_shape=[
             jax.ShapeDtypeStruct((channels, hid), F32),
@@ -589,7 +593,7 @@
 
 
 def chunk_starts(rows):
-    first = rows * 3 // 8 // BLOCK * BLOCK
+    first = rows // 2 // BLOCK * BLOCK
     return [0, first, rows]
 
 
@@ -644,9 +648,11 @@
             backward(index, grad, grad_near, grad_far[which], cotangent, kernel, so_far, chunks[which][0]),
         )
 
-    theirs = after(theirs, grad_far[0])
-    part = mine + xor_permute(theirs, core[1][1]).astype(F32)
+    quarter = hid // 4
+    got = [xor_permute(theirs[i : i + quarter], core[1][1]) for i in range(0, hid, quarter)]
+    part = mine + jnp.concatenate(got, axis=0).astype(F32)
     sends, total = scatter_stage(part, plane)
+    sends = after(sends, grad_far[0])
     kgrad = after(kgrad, *sends)
     kgrad = add_kernel_grad(kgrad, 0)
     part, kgrad = scatter_finish(sends, total, plane, kgrad)

time: 90.1 us -> 88.9 us (0.987)
  Pallas kernels: 48.8 us -> 47.4 us
    pallas_call x3, Pallas kernels: 20.5 us -> 19.5 us  [forward(): pl.pallas_call(functools.partial(forward_kernel, reach, not carried, last...]
    ppermute x16 -> x19, waiting for transfers between devices: 6.66 us -> 5.8 us  [xor_permute(): return lax.ppermute(value, AXES, pairs)]
    ppermute x16 -> x19, starting transfers between devices: 17.7 us -> 17.8 us  [xor_permute(): return lax.ppermute(value, AXES, pairs)]
  transfers between devices with their start and end apart: 20 -> 23, of which waited for: 6 -> 9; matrix products, arithmetic and copies ran while one was open for 2% -> 2% of each run, Pallas kernels for 52% -> 52%
where the time goes in v5:
time: 88.9 us; the launch traced here: 88.7 us
  Pallas kernels  47.4 us (53%)
  starting transfers between devices  30.3 us (34%)
  waiting for transfers between devices  6.32 us (7%)
  other arithmetic  2.21 us (2%)
  local copies, waits for them, and re-layouts  1.57 us (2%)
  between operations  0.97 us (1%)
    pallas_call x3, Pallas kernels, forward(): pl.pallas_call(functools.partial(forward_kernel, reach, not carried, last...  19.5 us
    ppermute x19, starting transfers between devices, xor_permute(): return lax.ppermute(value, AXES, pairs)  17.8 us
    ppermute x4, starting transfers between devices, off_chip(): return lax.ppermute(value, 'lon', pairs)  12.5 us
    pallas_call x2, Pallas kernels, backward(): pl.pallas_call(functools.partial(backward_kernel, start), grid=(count //...  10.2 us
    pallas_call x2, Pallas kernels, kernel_grad(): pl.pallas_call(functools.partial(kernel_grad_kernel, start), in_specs=[pl...  8.69 us
    pallas_call x1, Pallas kernels, inner(): pl.pallas_call(inner_kernel, in_specs=[pl.BlockSpec(memory_space=pltpu.SM...  7.6 us
    ppermute x19, waiting for transfers between devices, xor_permute(): return lax.ppermute(value, AXES, pairs)  5.8 us
    select_n x1, other arithmetic, per_device(): jnp.where(even, to_left, to_right)  1.84 us
  transfers between devices with their start and end apart: 23, of which 9 were waited for; matrix products, arithmetic and copies ran while one was open for 2% of the time, Pallas kernels for 52%

profile of v5, /device:TPU:0, one launch (start us, length us, event | category | flops | bytes accessed | tf_op | source)
XLA Modules:
  0.0 88.7 jit_solution(7043851246960069528)
XLA Ops:
  0.6 0.0 copy-start
  0.7 0.0 copy-start.2
  0.7 1.8 %broadcast_select_fusion = (bf16[32,64,256]{2,1,0:T(8,128)(2,1)S(1)}, bf16[32,64,256]{2,1,0:T(8,128)(2,1)S(1)}) fusion(pred[]{:T(512)S(6)} %eq.3, bf16[32,112,256]{2,1,0:T(8,128)(2,1)} %fields_ref.5), kind=kLoop, calls=%fused_computation.2 | loop fusion | flops 1048576 | bytes 4194305 | tf_op jit(solution)/shard_map/jit(_where)/select_n | solution.py:617
  2.5 0.5 collective-permute-start
  3.1 0.0 copy-start.1
  3.1 5.7 %collective-permute-start.2 = (bf16[16,64,256]{2,1,0:T(8,128)(2,1)S(1)}, bf16[16,64,256]{2,1,0:T(8,128)(2,1)S(1)}, u32[]{:S(2)}, u32[]{:S(2)}) collective-permute-start(bf16[16,64,256]{2,1,0:T(8,128)(2,1)S(1)} %slice.80), channel_id=1, source_target_pairs={{0,30},{2,4},{4,2},{6,8},{8,6},{10,12},{12,10},{14,16},{16,14},{18... | collective-permute-start | bytes 1572872 | tf_op jit(solution)/shard_map/ppermute | solution.py:40
  8.8 0.0 collective-permute-done.near_ref.far_ref
  8.8 7.6 %inner.1 = (f32[32,112,256]{2,1,0:T(8,128)S(1)}, bf16[1024,256]{1,0:T(8,128)(2,1)S(1)}, bf16[256,1024]{1,0:T(8,128)(2,1)S(1)}) custom-call(s32[1]{0:T(128)} %bitcast.core_ref, bf16[32,112,256]{2,1,0:T(8,128)(2,1)S(1)} %copy-done, bf16[32,64,256]{2,1,0:T(8,128)(2,1)S(1)} %collective-permute-done.near_ref.far_ref, f32[31,256]{1,0:T(8,128)S(1)} %copy-done.2, ...), custom_call_target="tpu_custom_call" | custom-call | flops 7395082240 | bytes 5505024 | tf_op jit(solution)/shard_map/inner/pallas_call | solution.py:253
  16.5 2.2 %collective-permute-start.1 = (bf16[16,64,256]{2,1,0:T(8,128)(2,1)S(1)}, bf16[16,64,256]{2,1,0:T(8,128)(2,1)S(1)}, u32[]{:S(2)}, u32[]{:S(2)}) collective-permute-start(bf16[16,64,256]{2,1,0:T(8,128)(2,1)S(1)} %slice.62), channel_id=1, source_target_pairs={{0,30},{2,4},{4,2},{6,8},{8,6},{10,12},{12,10},{14,16},{16,14},{18... | collective-permute-start | bytes 1572872 | tf_op jit(solution)/shard_map/ppermute | solution.py:40
  18.7 0.0 copy-done.1
  18.7 7.5 %forward.3 = (bf16[32,112,256]{2,1,0:T(8,128)(2,1)S(1)}, f32[32,112,256]{2,1,0:T(8,128)S(1)}, f32[4,256,256]{2,1,0:T(8,128)S(1)}, f32[256,1024]{1,0:T(8,128)S(1)}) custom-call(s32[1]{0:T(128)} %bitcast.core_ref, f32[32,112,256]{2,1,0:T(8,128)S(1)} %get-tuple-element.75.inner_ref, bf16[32,64,256]{2,1,0:T(8,128)(2,1)S(1)} %collective-permute-done.near_ref.far_ref, ...), custom_call_target="tpu_custom_call" | custom-call | flops 11274289152 | bytes 4718592 | tf_op jit(solution)/shard_map/forward/pallas_call | solution.py:411
  26.2 0.0 collective-permute-done.2.far_ref
  26.2 5.8 %forward.4 = (bf16[32,112,256]{2,1,0:T(8,128)(2,1)S(1)}, f32[32,112,256]{2,1,0:T(8,128)S(1)}, f32[4,256,256]{2,1,0:T(8,128)S(1)}, f32[256,1024]{1,0:T(8,128)S(1)...) custom-call(s32[1]{0:T(128)} %bitcast.core_ref, ...), custom_call_target="tpu_custom_call", output_to_operand_aliasing={{0}: (10, {}), {1}: (11, {}), {2}: (12, {}), {3}: (13, {})} | custom-call | flops 7516192768 | bytes 3145728 | tf_op jit(solution)/shard_map/forward/pallas_call | solution.py:411
  32.0 2.4 %collective-permute-start.7 = (bf16[16,64,256]{2,1,0:T(8,128)(2,1)S(1)}, bf16[16,64,256]{2,1,0:T(8,128)(2,1)S(1)}, u32[]{:S(2)}, u32[]{:S(2)}) collective-permute-start(bf16[16,64,256]{2,1,0:T(8,128)(2,1)S(1)} %get-tuple-element.94), channel_id=1, source_target_pairs={{0,30},{2,4},{4,2},{6,8},{8,6},{10,12},{12,10},{14,16},{16,14},{18... | collective-permute-start | bytes 1572872 | tf_op jit(solution)/shard_map/ppermute | solution.py:40
  34.4 0.0 collective-permute-done.1.far_ref
  34.4 6.2 %forward.5 = (bf16[32,112,256]{2,1,0:T(8,128)(2,1)S(1)}, f32[32,112,256]{2,1,0:T(8,128)S(1)}, f32[1024,256]{1,0:T(8,128)S(1)}, bf16[1024,256]{1,0:T(8,128)(2,1)S...) custom-call(s32[1]{0:T(128)} %bitcast.core_ref, ...), custom_call_target="tpu_custom_call", output_to_operand_aliasing={{0}: (10, {}), {1}: (11, {})} | custom-call | flops 7516192768 | bytes 3145728 | tf_op jit(solution)/shard_map/forward/pallas_call | solution.py:411
  40.6 0.1 collective-permute-start.3
  40.7 0.5 collective-permute-start.4
  41.2 0.1 collective-permute-start.5
  41.3 0.4 collective-permute-start.6
  41.7 0.1 pad_maximum_fusion
  41.8 0.2 collective-permute-done.3
  42.1 0.1 collective-permute-start.17
  42.2 0.0 collective-permute-done.4
  42.2 0.3 collective-permute-done.5
  42.6 0.2 collective-permute-done.6
  42.8 0.1 convert_add_fusion
  42.9 0.5 collective-permute-done.7.far_ref
  43.4 1.3 %collective-permute-start.10 = (bf16[256,256]{1,0:T(8,128)(2,1)S(1)}, bf16[256,256]{1,0:T(8,128)(2,1)S(1)}, u32[]{:S(2)}, u32[]{:S(2)}) collective-permute-start(bf16[256,256]{1,0:T(8,128)(2,1)S(1)} %get-tuple-element.97), channel_id=1, source_target_pairs={{0,5},{1,4},{2,7},{3,6},{4,1},{5,0},{6,3},{7,2},{8,13},{9,12},{10,... | collective-permute-start | bytes 393224 | tf_op jit(solution)/shard_map/ppermute | solution.py:30
  44.7 1.7 %collective-permute-start.8 = (bf16[256,256]{1,0:T(8,128)(2,1)S(1)}, bf16[256,256]{1,0:T(8,128)(2,1)S(1)}, u32[]{:S(2)}, u32[]{:S(2)}) collective-permute-start(bf16[256,256]{1,0:T(8,128)(2,1)S(1)} %get-tuple-element.95), channel_id=1, source_target_pairs={{0,4},{1,5},{2,6},{3,7},{4,0},{5,1},{6,2},{7,3},{8,12},{9,13},{10,... | collective-permute-start | bytes 393224 | tf_op jit(solution)/shard_map/ppermute | solution.py:30
  46.4 0.5 collective-permute-start.9
  46.9 4.3 %kernel_grad.2.given_ref = f32[32,256]{1,0:T(8,128)S(1)} custom-call(s32[1]{0:T(128)} %bitcast.core_ref, bf16[32,112,256]{2,1,0:T(8,128)(2,1)S(1)} %copy-done, bf16[32,64,256]{2,1,0:T(8,128)(2,1)S(1)} %collective-permute-done.near_ref.far_ref, bf16[16,64,256]{2,1,0:T(8,128)(2,1)S(1)} %collective-permute-done.2.far_ref, ...), custom_call_target="tpu_custom_call" | custom-call | flops 853278720 | bytes 3670016 | tf_op jit(solution)/shard_map/kernel_grad/pallas_call | solution.py:488
  51.3 0.0 collective-permute-done.10
  51.3 1.5 %collective-permute-done.8 = bf16[256,256]{1,0:T(8,128)(2,1)S(1)} collective-permute-done((bf16[256,256]{1,0:T(8,128)(2,1)S(1)}, bf16[256,256]{1,0:T(8,128)(2,1)S(1)}, u32[]{:S(2)}, u32[]{:S(2)}) %collective-permute-start.8) | collective-permute-done | bytes 131104 | tf_op jit(solution)/shard_map/ppermute | solution.py:30
  52.8 0.0 collective-permute-done.9
  52.8 0.1 fusion.1
  52.9 2.2 %collective-permute-start.18 = (bf16[16,64,256]{2,1,0:T(8,128)(2,1)S(1)}, bf16[16,64,256]{2,1,0:T(8,128)(2,1)S(1)}, u32[]{:S(2)}, u32[]{:S(2)}) collective-permute-start(bf16[16,64,256]{2,1,0:T(8,128)(2,1)S(1)} %get-tuple-element.120), channel_id=1, source_target_pairs={{0,30},{2,4},{4,2},{6,8},{8,6},{10,12},{12,10},{14,16},{16,14},{18... | collective-permute-start | bytes 1572872 | tf_op jit(solution)/shard_map/ppermute | solution.py:40
  55.1 0.1 collective-permute-start.11
  55.2 1.8 %collective-permute-start.12 = (bf16[64,256]{1,0:T(8,128)(2,1)S(1)}, bf16[64,256]{1,0:T(8,128)(2,1)S(1)}, u32[]{:S(2)}, u32[]{:S(2)}) collective-permute-start(bf16[64,256]{1,0:T(8,128)(2,1)S(1)} %get-tuple-element.111), channel_id=1, source_target_pairs={{0,16},{1,17},{2,18},{3,19},{4,20},{5,21},{6,22},{7,23},{8,24},{9,... | collective-permute-start | bytes 98312 | tf_op jit(solution)/shard_map/ppermute | solution.py:30
  57.0 2.6 %collective-permute-start.13 = (bf16[64,256]{1,0:T(8,128)(2,1)S(1)}, bf16[64,256]{1,0:T(8,128)(2,1)S(1)}, u32[]{:S(2)}, u32[]{:S(2)}) collective-permute-start(bf16[64,256]{1,0:T(8,128)(2,1)S(1)} %get-tuple-element.112), channel_id=1, source_target_pairs={{0,24},{1,25},{2,26},{3,27},{4,28},{5,29},{6,30},{7,31},{8,16},{9,... | collective-permute-start | bytes 98312 | tf_op jit(solution)/shard_map/ppermute | solution.py:30
  59.6 4.3 %kernel_grad.3 = f32[32,256]{1,0:T(8,128)S(1)} custom-call(s32[1]{0:T(128)} %bitcast.core_ref, bf16[32,112,256]{2,1,0:T(8,128)(2,1)S(1)} %copy-done, bf16[32,64,256]{2,1,0:T(8,128)(2,1)S(1)} %collective-permute-done.near_ref.far_ref, bf16[16,64,256]{2,1,0:T(8,128)(2,1)S(1)} %collective-permute-done.1.far_ref, ...), custom_call_target="tpu_custom_call" | custom-call | flops 853278720 | bytes 3670016 | tf_op jit(solution)/shard_map/kernel_grad/pallas_call | solution.py:488
  63.9 0.0 collective-permute-done.11
  64.0 0.3 collective-permute-done.12
  64.3 1.3 %collective-permute-done.13 = bf16[64,256]{1,0:T(8,128)(2,1)S(1)} collective-permute-done((bf16[64,256]{1,0:T(8,128)(2,1)S(1)}, bf16[64,256]{1,0:T(8,128)(2,1)S(1)}, u32[]{:S(2)}, u32[]{:S(2)}) %collective-permute-start.13) | collective-permute-done | bytes 32800 | tf_op jit(solution)/shard_map/ppermute | solution.py:30
  65.7 0.6 collective-permute-start.14
  66.2 2.7 %collective-permute-start.15 = (bf16[96,256]{1,0:T(8,128)(2,1)S(1)}, bf16[96,256]{1,0:T(8,128)(2,1)S(1)}, u32[]{:S(2)}, u32[]{:S(2)}) collective-permute-start(bf16[96,256]{1,0:T(8,128)(2,1)S(1)} %pad_maximum_fusion.3), channel_id=1, source_target_pairs={{0,16},{1,17},{2,18},{3,19},{4,20},{5,21},{6,22},{7,23},{8,24},{9,... | collective-permute-start | bytes 147464 | tf_op jit(solution)/shard_map/ppermute | solution.py:30
  68.9 1.2 %collective-permute-start.16 = (bf16[96,256]{1,0:T(8,128)(2,1)S(1)}, bf16[96,256]{1,0:T(8,128)(2,1)S(1)}, u32[]{:S(2)}, u32[]{:S(2)}) collective-permute-start(bf16[96,256]{1,0:T(8,128)(2,1)S(1)} %pad_maximum_fusion.3), channel_id=1, source_target_pairs={{0,24},{1,25},{2,26},{3,27},{4,28},{5,29},{6,30},{7,31},{8,16},{9,... | collective-permute-start | bytes 147464 | tf_op jit(solution)/shard_map/ppermute | solution.py:30
  70.1 0.0 collective-permute-done.18.far_ref
  70.1 0.0 collective-permute-done.17.near_ref
  70.1 5.1 %backward.2.refs_0_ = bf16[32,112,256]{2,1,0:T(8,128)(2,1)} custom-call(s32[1]{0:T(128)} %bitcast.core_ref, f32[32,112,256]{2,1,0:T(8,128)S(1)} %get-tuple-element.98.grad_ref, bf16[32,64,256]{2,1,0:T(8,128)(2,1)S(1)} %collective-permute-done.17.near_ref, bf16[16,64,256]{2,1,0:T(8,128)(2,1)S(1)} %collective-permute-done.7.far_ref, ...), custom_call_target="tpu_custom_call" | custom-call | flops 853278720 | bytes 4587520 | tf_op jit(solution)/shard_map/backward/pallas_call | solution.py:534
  75.2 0.0 collective-permute-done.14
  75.2 0.0 collective-permute-done.15
  75.2 0.0 collective-permute-done.16
  75.3 1.5 %collective-permute-start.19 = (bf16[288,256]{1,0:T(8,128)(2,1)S(1)}, bf16[288,256]{1,0:T(8,128)(2,1)S(1)}, u32[]{:S(2)}, u32[]{:S(2)}) collective-permute-start(bf16[288,256]{1,0:T(8,128)(2,1)S(1)} %pad_maximum_fusion.2), channel_id=1, source_target_pairs={{0,4},{1,5},{2,6},{3,7},{4,0},{5,1},{6,2},{7,3},{8,12},{9,13},{10,... | collective-permute-start | bytes 442376 | tf_op jit(solution)/shard_map/ppermute | solution.py:30
  76.9 1.5 %collective-permute-start.20 = (bf16[288,256]{1,0:T(8,128)(2,1)S(1)}, bf16[288,256]{1,0:T(8,128)(2,1)S(1)}, u32[]{:S(2)}, u32[]{:S(2)}) collective-permute-start(bf16[288,256]{1,0:T(8,128)(2,1)S(1)} %pad_maximum_fusion.2), channel_id=1, source_target_pairs={{0,1},{1,0},{2,3},{3,2},{4,5},{5,4},{6,7},{7,6},{8,9},{9,8},{10,11... | collective-permute-start | bytes 442376 | tf_op jit(solution)/shard_map/ppermute | solution.py:30
  78.3 0.6 collective-permute-start.21
  78.9 5.1 %backward.3 = bf16[32,112,256]{2,1,0:T(8,128)(2,1)} custom-call(s32[1]{0:T(128)} %bitcast.core_ref, f32[32,112,256]{2,1,0:T(8,128)S(1)} %get-tuple-element.98.grad_ref, bf16[32,64,256]{2,1,0:T(8,128)(2,1)S(1)} %collective-permute-done.17.near_ref, bf16[16,64,256]{2,1,0:T(8,128)(2,1)S(1)} %collective-permute-done.18.far_ref, ...), custom_call_target="tpu_custom_call", output_to_operand_aliasing={{}: (6, {})} | custom-call | flops 853278720 | bytes 4587520 | tf_op jit(solution)/shard_map/backward/pallas_call | solution.py:534
  84.0 0.0 collective-permute-done.19
  84.1 1.1 %collective-permute-done.20 = bf16[288,256]{1,0:T(8,128)(2,1)S(1)} collective-permute-done((bf16[288,256]{1,0:T(8,128)(2,1)S(1)}, bf16[288,256]{1,0:T(8,128)(2,1)S(1)}, u32[]{:S(2)}, u32[]{:S(2)}) %collective-permute-start.20) | collective-permute-done | bytes 147488 | tf_op jit(solution)/shard_map/ppermute | solution.py:30
  85.2 0.0 collective-permute-done.21
  85.3 0.1 collective-permute-start.22
  85.4 1.2 %copy.32 = bf16[32,112,256]{2,1,0:T(8,128)(2,1)} copy(bf16[32,112,256]{2,1,0:T(8,128)(2,1)S(1)} %get-tuple-element.153) | data formatting | bytes 3670016
  86.6 0.7 collective-permute-done.22.got_ref.tail_ref
  87.3 1.4 %finish.1 = (f32[256,1024]{1,0:T(8,128)}, f32[1024,256]{1,0:T(8,128)}, f32[31,256]{1,0:T(8,128)}) custom-call(s32[1]{0:T(128)} %bitcast.core_ref, bf16[1056,256]{1,0:T(8,128)(2,1)S(1)} %pad_maximum_fusion.1.own_ref, bf16[1056,256]{1,0:T(8,128)(2,1)S(1)} %collective-permute-done.22.got_ref.tail_ref, ...), custom_call_target="tpu_custom_call" | custom-call | tf_op jit(solution)/shard_map/finish/pallas_call | solution.py:570
  (28 shorter events, 0.4 us)
Async XLA Ops:
  0.6 8.2 %copy-start = (bf16[32,112,256]{2,1,0:T(8,128)(2,1)S(1)}, bf16[32,112,256]{2,1,0:T(8,128)(2,1)}, u32[]{:S(2)}) copy-start(bf16[32,112,256]{2,1,0:T(8,128)(2,1)} %fields_ref.5) | copy-start | bytes 5505028
  0.7 8.2 %copy-start.2 = (f32[31,256]{1,0:T(8,128)S(1)}, f32[31,256]{1,0:T(8,128)}, u32[]{:S(2)}) copy-start(f32[31,256]{1,0:T(8,128)} %kernel_ref.11) | copy-start | bytes 95236
  0.7 8.2 %copy-start.3 = (bf16[256,1024]{1,0:T(8,128)(2,1)S(1)}, bf16[256,1024]{1,0:T(8,128)(2,1)}, u32[]{:S(2)}) copy-start(bf16[256,1024]{1,0:T(8,128)(2,1)} %up_ref.5) | copy-start | bytes 1572868
  0.7 8.2 %copy-start.4 = (bf16[1024,256]{1,0:T(8,128)(2,1)S(1)}, bf16[1024,256]{1,0:T(8,128)(2,1)}, u32[]{:S(2)}) copy-start(bf16[1024,256]{1,0:T(8,128)(2,1)} %down_ref.5) | copy-start | bytes 1572868
  2.5 6.3 %collective-permute-start = (bf16[32,64,256]{2,1,0:T(8,128)(2,1)S(1)}, bf16[32,64,256]{2,1,0:T(8,128)(2,1)S(1)}, u32[]{:S(2)}, u32[]{:S(2)}) collective-permute-start(bf16[32,64,256]{2,1,0:T(8,128)(2,1)S(1)} %get-tuple-element.142), channel_id=1, source_target_pairs={{0,2},{1,3},{2,0},{3,1},{4,6},{5,7},{6,4},{7,5},{8,10},{9,11},{10,... | collective-permute-start | bytes 3145736 | tf_op jit(solution)/shard_map/ppermute | solution.py:30
  3.1 15.6 %copy-start.1 = (bf16[32,112,256]{2,1,0:T(8,128)(2,1)S(1)}, bf16[32,112,256]{2,1,0:T(8,128)(2,1)}, u32[]{:S(2)}) copy-start(bf16[32,112,256]{2,1,0:T(8,128)(2,1)} %cot_ref.9) | copy-start | bytes 5505028
  3.1 23.1 %collective-permute-start.2 = (bf16[16,64,256]{2,1,0:T(8,128)(2,1)S(1)}, bf16[16,64,256]{2,1,0:T(8,128)(2,1)S(1)}, u32[]{:S(2)}, u32[]{:S(2)}) collective-permute-start(bf16[16,64,256]{2,1,0:T(8,128)(2,1)S(1)} %slice.80), channel_id=1, source_target_pairs={{0,30},{2,4},{4,2},{6,8},{8,6},{10,12},{12,10},{14,16},{16,14},{18... | collective-permute-start | bytes 1572872 | tf_op jit(solution)/shard_map/ppermute | solution.py:40
  16.5 17.9 %collective-permute-start.1 = (bf16[16,64,256]{2,1,0:T(8,128)(2,1)S(1)}, bf16[16,64,256]{2,1,0:T(8,128)(2,1)S(1)}, u32[]{:S(2)}, u32[]{:S(2)}) collective-permute-start(bf16[16,64,256]{2,1,0:T(8,128)(2,1)S(1)} %slice.62), channel_id=1, source_target_pairs={{0,30},{2,4},{4,2},{6,8},{8,6},{10,12},{12,10},{14,16},{16,14},{18... | collective-permute-start | bytes 1572872 | tf_op jit(solution)/shard_map/ppermute | solution.py:40
  32.0 11.5 %collective-permute-start.7 = (bf16[16,64,256]{2,1,0:T(8,128)(2,1)S(1)}, bf16[16,64,256]{2,1,0:T(8,128)(2,1)S(1)}, u32[]{:S(2)}, u32[]{:S(2)}) collective-permute-start(bf16[16,64,256]{2,1,0:T(8,128)(2,1)S(1)} %get-tuple-element.94), channel_id=1, source_target_pairs={{0,30},{2,4},{4,2},{6,8},{8,6},{10,12},{12,10},{14,16},{16,14},{18... | collective-permute-start | bytes 1572872 | tf_op jit(solution)/shard_map/ppermute | solution.py:40
  40.6 1.4 %collective-permute-start.3 = (bf16[256,256]{1,0:T(8,128)(2,1)S(1)}, bf16[256,256]{1,0:T(8,128)(2,1)S(1)}, u32[]{:S(2)}, u32[]{:S(2)}) collective-permute-start(bf16[256,256]{1,0:T(8,128)(2,1)S(1)} %get-tuple-element.146), channel_id=1, source_target_pairs={{0,2},{1,3},{2,0},{3,1},{4,6},{5,7},{6,4},{7,5},{8,10},{9,11},{10,... | collective-permute-start | bytes 393224 | tf_op jit(solution)/shard_map/ppermute | solution.py:30
  40.7 1.5 %collective-permute-start.4 = (bf16[256,256]{1,0:T(8,128)(2,1)S(1)}, bf16[256,256]{1,0:T(8,128)(2,1)S(1)}, u32[]{:S(2)}, u32[]{:S(2)}) collective-permute-start(bf16[256,256]{1,0:T(8,128)(2,1)S(1)} %get-tuple-element.149), channel_id=1, source_target_pairs={{0,2},{1,3},{2,0},{3,1},{4,6},{5,7},{6,4},{7,5},{8,10},{9,11},{10,... | collective-permute-start | bytes 393224 | tf_op jit(solution)/shard_map/ppermute | solution.py:30
  41.2 1.3 %collective-permute-start.5 = (bf16[256,256]{1,0:T(8,128)(2,1)S(1)}, bf16[256,256]{1,0:T(8,128)(2,1)S(1)}, u32[]{:S(2)}, u32[]{:S(2)}) collective-permute-start(bf16[256,256]{1,0:T(8,128)(2,1)S(1)} %get-tuple-element.148), channel_id=1, source_target_pairs={{0,2},{1,3},{2,0},{3,1},{4,6},{5,7},{6,4},{7,5},{8,10},{9,11},{10,... | collective-permute-start | bytes 393224 | tf_op jit(solution)/shard_map/ppermute | solution.py:30
  41.3 1.5 %collective-permute-start.6 = (bf16[256,256]{1,0:T(8,128)(2,1)S(1)}, bf16[256,256]{1,0:T(8,128)(2,1)S(1)}, u32[]{:S(2)}, u32[]{:S(2)}) collective-permute-start(bf16[256,256]{1,0:T(8,128)(2,1)S(1)} %get-tuple-element.147), channel_id=1, source_target_pairs={{0,2},{1,3},{2,0},{3,1},{4,6},{5,7},{6,4},{7,5},{8,10},{9,11},{10,... | collective-permute-start | bytes 393224 | tf_op jit(solution)/shard_map/ppermute | solution.py:30
  42.1 28.1 %collective-permute-start.17 = (bf16[32,64,256]{2,1,0:T(8,128)(2,1)S(1)}, bf16[32,64,256]{2,1,0:T(8,128)(2,1)S(1)}, u32[]{:S(2)}, u32[]{:S(2)}) collective-permute-start(bf16[32,64,256]{2,1,0:T(8,128)(2,1)S(1)} %pad_maximum_fusion), channel_id=1, source_target_pairs={{0,2},{1,3},{2,0},{3,1},{4,6},{5,7},{6,4},{7,5},{8,10},{9,11},{10,... | collective-permute-start | bytes 3145736 | tf_op jit(solution)/shard_map/ppermute | solution.py:30
  43.4 7.8 %collective-permute-start.10 = (bf16[256,256]{1,0:T(8,128)(2,1)S(1)}, bf16[256,256]{1,0:T(8,128)(2,1)S(1)}, u32[]{:S(2)}, u32[]{:S(2)}) collective-permute-start(bf16[256,256]{1,0:T(8,128)(2,1)S(1)} %get-tuple-element.97), channel_id=1, source_target_pairs={{0,5},{1,4},{2,7},{3,6},{4,1},{5,0},{6,3},{7,2},{8,13},{9,12},{10,... | collective-permute-start | bytes 393224 | tf_op jit(solution)/shard_map/ppermute | solution.py:30
  44.7 8.1 %collective-permute-start.8 = (bf16[256,256]{1,0:T(8,128)(2,1)S(1)}, bf16[256,256]{1,0:T(8,128)(2,1)S(1)}, u32[]{:S(2)}, u32[]{:S(2)}) collective-permute-start(bf16[256,256]{1,0:T(8,128)(2,1)S(1)} %get-tuple-element.95), channel_id=1, source_target_pairs={{0,4},{1,5},{2,6},{3,7},{4,0},{5,1},{6,2},{7,3},{8,12},{9,13},{10,... | collective-permute-start | bytes 393224 | tf_op jit(solution)/shard_map/ppermute | solution.py:30
  46.4 6.4 %collective-permute-start.9 = (bf16[256,256]{1,0:T(8,128)(2,1)S(1)}, bf16[256,256]{1,0:T(8,128)(2,1)S(1)}, u32[]{:S(2)}, u32[]{:S(2)}) collective-permute-start(bf16[256,256]{1,0:T(8,128)(2,1)S(1)} %get-tuple-element.96), channel_id=1, source_target_pairs={{0,1},{1,0},{2,3},{3,2},{4,5},{5,4},{6,7},{7,6},{8,9},{9,8},{10,11... | collective-permute-start | bytes 393224 | tf_op jit(solution)/shard_map/ppermute | solution.py:30
  52.9 17.2 %collective-permute-start.18 = (bf16[16,64,256]{2,1,0:T(8,128)(2,1)S(1)}, bf16[16,64,256]{2,1,0:T(8,128)(2,1)S(1)}, u32[]{:S(2)}, u32[]{:S(2)}) collective-permute-start(bf16[16,64,256]{2,1,0:T(8,128)(2,1)S(1)} %get-tuple-element.120), channel_id=1, source_target_pairs={{0,30},{2,4},{4,2},{6,8},{8,6},{10,12},{12,10},{14,16},{16,14},{18... | collective-permute-start | bytes 1572872 | tf_op jit(solution)/shard_map/ppermute | solution.py:40
  55.1 8.8 %collective-permute-start.11 = (bf16[64,256]{1,0:T(8,128)(2,1)S(1)}, bf16[64,256]{1,0:T(8,128)(2,1)S(1)}, u32[]{:S(2)}, u32[]{:S(2)}) collective-permute-start(bf16[64,256]{1,0:T(8,128)(2,1)S(1)} %get-tuple-element.110), channel_id=1, source_target_pairs={{0,8},{1,9},{2,10},{3,11},{4,12},{5,13},{6,14},{7,15},{8,0},{9,1},... | collective-permute-start | bytes 98312 | tf_op jit(solution)/shard_map/ppermute | solution.py:30
  55.2 9.1 %collective-permute-start.12 = (bf16[64,256]{1,0:T(8,128)(2,1)S(1)}, bf16[64,256]{1,0:T(8,128)(2,1)S(1)}, u32[]{:S(2)}, u32[]{:S(2)}) collective-permute-start(bf16[64,256]{1,0:T(8,128)(2,1)S(1)} %get-tuple-element.111), channel_id=1, source_target_pairs={{0,16},{1,17},{2,18},{3,19},{4,20},{5,21},{6,22},{7,23},{8,24},{9,... | collective-permute-start | bytes 98312 | tf_op jit(solution)/shard_map/ppermute | solution.py:30
  57.0 8.6 %collective-permute-start.13 = (bf16[64,256]{1,0:T(8,128)(2,1)S(1)}, bf16[64,256]{1,0:T(8,128)(2,1)S(1)}, u32[]{:S(2)}, u32[]{:S(2)}) collective-permute-start(bf16[64,256]{1,0:T(8,128)(2,1)S(1)} %get-tuple-element.112), channel_id=1, source_target_pairs={{0,24},{1,25},{2,26},{3,27},{4,28},{5,29},{6,30},{7,31},{8,16},{9,... | collective-permute-start | bytes 98312 | tf_op jit(solution)/shard_map/ppermute | solution.py:30
  65.7 9.6 %collective-permute-start.14 = (bf16[96,256]{1,0:T(8,128)(2,1)S(1)}, bf16[96,256]{1,0:T(8,128)(2,1)S(1)}, u32[]{:S(2)}, u32[]{:S(2)}) collective-permute-start(bf16[96,256]{1,0:T(8,128)(2,1)S(1)} %pad_maximum_fusion.3), channel_id=1, source_target_pairs={{0,8},{1,9},{2,10},{3,11},{4,12},{5,13},{6,14},{7,15},{8,0},{9,1},... | collective-permute-start | bytes 147464 | tf_op jit(solution)/shard_map/ppermute | solution.py:30
  66.2 9.0 %collective-permute-start.15 = (bf16[96,256]{1,0:T(8,128)(2,1)S(1)}, bf16[96,256]{1,0:T(8,128)(2,1)S(1)}, u32[]{:S(2)}, u32[]{:S(2)}) collective-permute-start(bf16[96,256]{1,0:T(8,128)(2,1)S(1)} %pad_maximum_fusion.3), channel_id=1, source_target_pairs={{0,16},{1,17},{2,18},{3,19},{4,20},{5,21},{6,22},{7,23},{8,24},{9,... | collective-permute-start | bytes 147464 | tf_op jit(solution)/shard_map/ppermute | solution.py:30
  68.9 6.3 %collective-permute-start.16 = (bf16[96,256]{1,0:T(8,128)(2,1)S(1)}, bf16[96,256]{1,0:T(8,128)(2,1)S(1)}, u32[]{:S(2)}, u32[]{:S(2)}) collective-permute-start(bf16[96,256]{1,0:T(8,128)(2,1)S(1)} %pad_maximum_fusion.3), channel_id=1, source_target_pairs={{0,24},{1,25},{2,26},{3,27},{4,28},{5,29},{6,30},{7,31},{8,16},{9,... | collective-permute-start | bytes 147464 | tf_op jit(solution)/shard_map/ppermute | solution.py:30
  75.3 8.7 %collective-permute-start.19 = (bf16[288,256]{1,0:T(8,128)(2,1)S(1)}, bf16[288,256]{1,0:T(8,128)(2,1)S(1)}, u32[]{:S(2)}, u32[]{:S(2)}) collective-permute-start(bf16[288,256]{1,0:T(8,128)(2,1)S(1)} %pad_maximum_fusion.2), channel_id=1, source_target_pairs={{0,4},{1,5},{2,6},{3,7},{4,0},{5,1},{6,2},{7,3},{8,12},{9,13},{10,... | collective-permute-start | bytes 442376 | tf_op jit(solution)/shard_map/ppermute | solution.py:30
  76.9 8.3 %collective-permute-start.20 = (bf16[288,256]{1,0:T(8,128)(2,1)S(1)}, bf16[288,256]{1,0:T(8,128)(2,1)S(1)}, u32[]{:S(2)}, u32[]{:S(2)}) collective-permute-start(bf16[288,256]{1,0:T(8,128)(2,1)S(1)} %pad_maximum_fusion.2), channel_id=1, source_target_pairs={{0,1},{1,0},{2,3},{3,2},{4,5},{5,4},{6,7},{7,6},{8,9},{9,8},{10,11... | collective-permute-start | bytes 442376 | tf_op jit(solution)/shard_map/ppermute | solution.py:30
  78.3 6.9 %collective-permute-start.21 = (bf16[288,256]{1,0:T(8,128)(2,1)S(1)}, bf16[288,256]{1,0:T(8,128)(2,1)S(1)}, u32[]{:S(2)}, u32[]{:S(2)}) collective-permute-start(bf16[288,256]{1,0:T(8,128)(2,1)S(1)} %pad_maximum_fusion.2), channel_id=1, source_target_pairs={{0,5},{1,4},{2,7},{3,6},{4,1},{5,0},{6,3},{7,2},{8,13},{9,12},{10,... | collective-permute-start | bytes 442376 | tf_op jit(solution)/shard_map/ppermute | solution.py:30
  85.3 2.0 %collective-permute-start.22 = (bf16[1056,256]{1,0:T(8,128)(2,1)S(1)}, bf16[1056,256]{1,0:T(8,128)(2,1)S(1)}, u32[]{:S(2)}, u32[]{:S(2)}) collective-permute-start(bf16[1056,256]{1,0:T(8,128)(2,1)S(1)} %pad_maximum_fusion.1.own_ref), channel_id=1, source_target_pairs={{0,2},{1,3},{2,0},{3,1},{4,6},{5,7},{6,4},{7,5},{8,10},{9,11},{10,... | collective-permute-start | bytes 1622024 | tf_op jit(solution)/shard_map/ppermute | solution.py:30

commit v6 on v5

--- a/solution.py
+++ b/solution.py
@@ -10,7 +10,7 @@
 
 KERNEL_SPACING = 4
 BLOCK = 4
-NEAR_BLOCK = 16
+NEAR_BLOCK = 32
 FAR_BLOCK = 16
 AXES = ("lon", "lat")
 F32 = jnp.float32
@@ -241,10 +241,6 @@
 
     for copy in copies:
         copy.wait()
-    for j in range(up_ref.shape[1] // 256):
-        part = pl.ds(256 * j, 256)
-        upt_ref[part, :] = up_ref[:, part].T
-        downt_ref[:, part] = down_ref[part, :].T
 
 
 def inner(core, fields, near, kernel, up, down):
@@ -346,11 +342,11 @@
     normed_s[...] = normed
     low = normed.astype(BF16)
     cot = cot_ref[here, span, :].reshape(cells, channels)
-    over_cells = (((0,), (0,)), ((), ()))
+    over_cells, over_last = (((0,), (0,)), ((), ())), (((1,), (1,)), ((), ()))
     for j in range(hid // width):
         part = pl.ds(j * width, width)
         h = jnp.dot(low, up_ref[:, part], preferred_element_type=F32)
-        u = jnp.dot(cot, downt_ref[:, part], preferred_element_type=F32)
+        u = lax.dot_general(cot, down_ref[part, :], over_last, preferred_element_type=F32)
         inner = h * (GELU_A + GELU_B * (h * h))
         t = jnp.tanh(inner)
         rise = 1.0 + t
@@ -359,7 +355,7 @@
         hg_s[:, part] = (u * slope).astype(BF16)
     out = jnp.dot(act_s[...], down_ref[...], preferred_element_type=F32)
     out = out + fields_ref[here, span, :].reshape(cells, channels).astype(F32)
-    normed_grad = jnp.dot(hg_s[...], upt_ref[...], preferred_element_type=F32)
+    normed_grad = lax.dot_general(hg_s[...], up_ref[...], over_last, preferred_element_type=F32)
     for j in range(hid // width):
         part = pl.ds(j * width, width)
         gup_s[j] += lax.dot_general(low, hg_s[:, part], over_cells, preferred_element_type=F32)
@@ -652,7 +648,6 @@
     got = [xor_permute(theirs[i : i + quarter], core[1][1]) for i in range(0, hid, quarter)]
     part = mine + jnp.concatenate(got, axis=0).astype(F32)
     sends, total = scatter_stage(part, plane)
-    sends = after(sends, grad_far[0])
     kgrad = after(kgrad, *sends)
     kgrad = add_kernel_grad(kgrad, 0)
     part, kgrad = scatter_finish(sends, total, plane, kgrad)
@@ -660,6 +655,7 @@
     grad_far.append(off_chip(far_edge))
     grad_near = on_chip(jnp.concatenate(grad_near, axis=0))
     sends, total = scatter_stage(part, depth)
+    sends = after(sends, grad_far[0])
     sends, kgrad = lax.optimization_barrier((sends, kgrad))
     kgrad = add_kernel_grad(kgrad, 1)
     part, kgrad = scatter_finish(sends, total, depth, kgrad)

time: 88.9 us -> 87.2 us (0.981)
    ppermute x4, starting transfers between devices: 12.5 us -> 11.7 us  [off_chip(): return lax.ppermute(value, 'lon', pairs)]
  transfers between devices with their start and end apart: 23 -> 23, of which waited for: 9 -> 8; matrix products, arithmetic and copies ran while one was open for 2% -> 2% of each run, Pallas kernels for 52% -> 52%
where the time goes in v6:
time: 87.2 us; the launch traced here: 87.1 us
  Pallas kernels  47 us (54%)
  starting transfers between devices  29.5 us (34%)
  waiting for transfers between devices  5.89 us (7%)
  other arithmetic  2.21 us (3%)
  local copies, waits for them, and re-layouts  1.57 us (2%)
  between operations  0.99 us (1%)
    pallas_call x3, Pallas kernels, forward(): pl.pallas_call(functools.partial(forward_kernel, reach, not carried, last...  19.4 us
    ppermute x19, starting transfers between devices, xor_permute(): return lax.ppermute(value, AXES, pairs)  17.8 us
    ppermute x4, starting transfers between devices, off_chip(): return lax.ppermute(value, 'lon', pairs)  11.7 us
    pallas_call x2, Pallas kernels, backward(): pl.pallas_call(functools.partial(backward_kernel, start), grid=(count //...  10.2 us
    pallas_call x2, Pallas kernels, kernel_grad(): pl.pallas_call(functools.partial(kernel_grad_kernel, start), in_specs=[pl...  8.69 us
    pallas_call x1, Pallas kernels, inner(): pl.pallas_call(inner_kernel, in_specs=[pl.BlockSpec(memory_space=pltpu.SM...  7.21 us
    ppermute x19, waiting for transfers between devices, xor_permute(): return lax.ppermute(value, AXES, pairs)  5.88 us
    select_n x1, other arithmetic, per_device(): jnp.where(even, to_left, to_right)  1.84 us
  transfers between devices with their start and end apart: 23, of which 8 were waited for; matrix products, arithmetic and copies ran while one was open for 2% of the time, Pallas kernels for 52%

profile of v6, /device:TPU:0, one launch (start us, length us, event | category | flops | bytes accessed | tf_op | source)
XLA Modules:
  0.0 87.1 jit_solution(14107738292388868070)
XLA Ops:
  0.6 0.0 copy-start
  0.7 0.0 copy-start.2
  0.7 1.8 %broadcast_select_fusion = (bf16[32,64,256]{2,1,0:T(8,128)(2,1)S(1)}, bf16[32,64,256]{2,1,0:T(8,128)(2,1)S(1)}) fusion(pred[]{:T(512)S(6)} %eq.3, bf16[32,112,256]{2,1,0:T(8,128)(2,1)} %fields_ref.5), kind=kLoop, calls=%fused_computation.2 | loop fusion | flops 1048576 | bytes 4194305 | tf_op jit(solution)/shard_map/jit(_where)/select_n | solution.py:613
  2.5 0.5 collective-permute-start
  3.1 0.0 copy-start.1
  3.1 5.7 %collective-permute-start.2 = (bf16[16,64,256]{2,1,0:T(8,128)(2,1)S(1)}, bf16[16,64,256]{2,1,0:T(8,128)(2,1)S(1)}, u32[]{:S(2)}, u32[]{:S(2)}) collective-permute-start(bf16[16,64,256]{2,1,0:T(8,128)(2,1)S(1)} %slice.80), channel_id=1, source_target_pairs={{0,30},{2,4},{4,2},{6,8},{8,6},{10,12},{12,10},{14,16},{16,14},{18... | collective-permute-start | bytes 1572872 | tf_op jit(solution)/shard_map/ppermute | solution.py:40
  8.8 0.0 collective-permute-done.near_ref.far_ref
  8.8 0.0 copy-done.2
  8.8 7.2 %inner.1 = (f32[32,112,256]{2,1,0:T(8,128)S(1)}, bf16[1024,256]{1,0:T(8,128)(2,1)S(1)}, bf16[256,1024]{1,0:T(8,128)(2,1)S(1)}) custom-call(s32[1]{0:T(128)} %bitcast.core_ref, bf16[32,112,256]{2,1,0:T(8,128)(2,1)S(1)} %copy-done, bf16[32,64,256]{2,1,0:T(8,128)(2,1)S(1)} %collective-permute-done.near_ref.far_ref, f32[31,256]{1,0:T(8,128)S(1)} %copy-done.2, ...), custom_call_target="tpu_custom_call" | custom-call | flops 7395082240 | bytes 5505024 | tf_op jit(solution)/shard_map/inner/pallas_call | solution.py:249
  16.1 2.2 %collective-permute-start.1 = (bf16[16,64,256]{2,1,0:T(8,128)(2,1)S(1)}, bf16[16,64,256]{2,1,0:T(8,128)(2,1)S(1)}, u32[]{:S(2)}, u32[]{:S(2)}) collective-permute-start(bf16[16,64,256]{2,1,0:T(8,128)(2,1)S(1)} %slice.62), channel_id=1, source_target_pairs={{0,30},{2,4},{4,2},{6,8},{8,6},{10,12},{12,10},{14,16},{16,14},{18... | collective-permute-start | bytes 1572872 | tf_op jit(solution)/shard_map/ppermute | solution.py:40
  18.3 7.3 %forward.3 = (bf16[32,112,256]{2,1,0:T(8,128)(2,1)S(1)}, f32[32,112,256]{2,1,0:T(8,128)S(1)}, f32[4,256,256]{2,1,0:T(8,128)S(1)}, f32[256,1024]{1,0:T(8,128)S(1)}) custom-call(s32[1]{0:T(128)} %bitcast.core_ref, f32[32,112,256]{2,1,0:T(8,128)S(1)} %get-tuple-element.75.inner_ref, bf16[32,64,256]{2,1,0:T(8,128)(2,1)S(1)} %collective-permute-done.near_ref.far_ref, ...), custom_call_target="tpu_custom_call" | custom-call | flops 11274289152 | bytes 4718592 | tf_op jit(solution)/shard_map/forward/pallas_call | solution.py:407
  25.6 0.0 collective-permute-done.2.far_ref
  25.6 5.9 %forward.4 = (bf16[32,112,256]{2,1,0:T(8,128)(2,1)S(1)}, f32[32,112,256]{2,1,0:T(8,128)S(1)}, f32[4,256,256]{2,1,0:T(8,128)S(1)}, f32[256,1024]{1,0:T(8,128)S(1)...) custom-call(s32[1]{0:T(128)} %bitcast.core_ref, ...), custom_call_target="tpu_custom_call", output_to_operand_aliasing={{0}: (10, {}), {1}: (11, {}), {2}: (12, {}), {3}: (13, {})} | custom-call | flops 7516192768 | bytes 3145728 | tf_op jit(solution)/shard_map/forward/pallas_call | solution.py:407
  31.5 2.4 %collective-permute-start.10 = (bf16[16,64,256]{2,1,0:T(8,128)(2,1)S(1)}, bf16[16,64,256]{2,1,0:T(8,128)(2,1)S(1)}, u32[]{:S(2)}, u32[]{:S(2)}) collective-permute-start(bf16[16,64,256]{2,1,0:T(8,128)(2,1)S(1)} %get-tuple-element.105), channel_id=1, source_target_pairs={{0,30},{2,4},{4,2},{6,8},{8,6},{10,12},{12,10},{14,16},{16,14},{18... | collective-permute-start | bytes 1572872 | tf_op jit(solution)/shard_map/ppermute | solution.py:40
  33.9 0.0 collective-permute-done.1.far_ref
  33.9 6.3 %forward.5 = (bf16[32,112,256]{2,1,0:T(8,128)(2,1)S(1)}, f32[32,112,256]{2,1,0:T(8,128)S(1)}, f32[1024,256]{1,0:T(8,128)S(1)}, bf16[1024,256]{1,0:T(8,128)(2,1)S...) custom-call(s32[1]{0:T(128)} %bitcast.core_ref, ...), custom_call_target="tpu_custom_call", output_to_operand_aliasing={{0}: (10, {}), {1}: (11, {})} | custom-call | flops 7516192768 | bytes 3145728 | tf_op jit(solution)/shard_map/forward/pallas_call | solution.py:407
  40.2 0.1 collective-permute-start.3
  40.3 0.5 collective-permute-start.4
  40.8 0.1 collective-permute-start.5
  40.9 0.4 collective-permute-start.6
  41.3 0.1 pad_maximum_fusion
  41.4 0.2 collective-permute-done.3
  41.6 0.1 collective-permute-start.17
  41.8 0.0 collective-permute-done.4
  41.8 0.3 collective-permute-done.5
  42.1 0.2 collective-permute-done.6
  42.3 0.1 convert_add_fusion
  42.5 0.1 collective-permute-start.7
  42.6 1.6 %collective-permute-start.8 = (bf16[256,256]{1,0:T(8,128)(2,1)S(1)}, bf16[256,256]{1,0:T(8,128)(2,1)S(1)}, u32[]{:S(2)}, u32[]{:S(2)}) collective-permute-start(bf16[256,256]{1,0:T(8,128)(2,1)S(1)} %get-tuple-element.144), channel_id=1, source_target_pairs={{0,1},{1,0},{2,3},{3,2},{4,5},{5,4},{6,7},{7,6},{8,9},{9,8},{10,11... | collective-permute-start | bytes 393224 | tf_op jit(solution)/shard_map/ppermute | solution.py:30
  44.2 1.9 %collective-permute-start.9 = (bf16[256,256]{1,0:T(8,128)(2,1)S(1)}, bf16[256,256]{1,0:T(8,128)(2,1)S(1)}, u32[]{:S(2)}, u32[]{:S(2)}) collective-permute-start(bf16[256,256]{1,0:T(8,128)(2,1)S(1)} %get-tuple-element.143), channel_id=1, source_target_pairs={{0,5},{1,4},{2,7},{3,6},{4,1},{5,0},{6,3},{7,2},{8,13},{9,12},{10,... | collective-permute-start | bytes 393224 | tf_op jit(solution)/shard_map/ppermute | solution.py:30
  46.1 4.3 %kernel_grad.2.given_ref = f32[32,256]{1,0:T(8,128)S(1)} custom-call(s32[1]{0:T(128)} %bitcast.core_ref, bf16[32,112,256]{2,1,0:T(8,128)(2,1)S(1)} %copy-done, bf16[32,64,256]{2,1,0:T(8,128)(2,1)S(1)} %collective-permute-done.near_ref.far_ref, bf16[16,64,256]{2,1,0:T(8,128)(2,1)S(1)} %collective-permute-done.2.far_ref, ...), custom_call_target="tpu_custom_call" | custom-call | flops 853278720 | bytes 3670016 | tf_op jit(solution)/shard_map/kernel_grad/pallas_call | solution.py:484
  50.4 0.0 collective-permute-done.7
  50.4 0.0 collective-permute-done.8
  50.4 1.6 %collective-permute-done.9 = bf16[256,256]{1,0:T(8,128)(2,1)S(1)} collective-permute-done((bf16[256,256]{1,0:T(8,128)(2,1)S(1)}, bf16[256,256]{1,0:T(8,128)(2,1)S(1)}, u32[]{:S(2)}, u32[]{:S(2)}) %collective-permute-start.9) | collective-permute-done | bytes 131104 | tf_op jit(solution)/shard_map/ppermute | solution.py:30
  52.0 0.1 fusion.1
  52.1 1.4 %collective-permute-start.18 = (bf16[16,64,256]{2,1,0:T(8,128)(2,1)S(1)}, bf16[16,64,256]{2,1,0:T(8,128)(2,1)S(1)}, u32[]{:S(2)}, u32[]{:S(2)}) collective-permute-start(bf16[16,64,256]{2,1,0:T(8,128)(2,1)S(1)} %get-tuple-element.120), channel_id=1, source_target_pairs={{0,30},{2,4},{4,2},{6,8},{8,6},{10,12},{12,10},{14,16},{16,14},{18... | collective-permute-start | bytes 1572872 | tf_op jit(solution)/shard_map/ppermute | solution.py:40
  53.5 0.0 collective-permute-done.10.far_ref
  53.5 0.1 collective-permute-start.11
  53.6 2.4 %collective-permute-start.12 = (bf16[64,256]{1,0:T(8,128)(2,1)S(1)}, bf16[64,256]{1,0:T(8,128)(2,1)S(1)}, u32[]{:S(2)}, u32[]{:S(2)}) collective-permute-start(bf16[64,256]{1,0:T(8,128)(2,1)S(1)} %get-tuple-element.111), channel_id=1, source_target_pairs={{0,16},{1,17},{2,18},{3,19},{4,20},{5,21},{6,22},{7,23},{8,24},{9,... | collective-permute-start | bytes 98312 | tf_op jit(solution)/shard_map/ppermute | solution.py:30
  56.0 2.0 %collective-permute-start.13 = (bf16[64,256]{1,0:T(8,128)(2,1)S(1)}, bf16[64,256]{1,0:T(8,128)(2,1)S(1)}, u32[]{:S(2)}, u32[]{:S(2)}) collective-permute-start(bf16[64,256]{1,0:T(8,128)(2,1)S(1)} %get-tuple-element.112), channel_id=1, source_target_pairs={{0,24},{1,25},{2,26},{3,27},{4,28},{5,29},{6,30},{7,31},{8,16},{9,... | collective-permute-start | bytes 98312 | tf_op jit(solution)/shard_map/ppermute | solution.py:30
  57.9 4.3 %kernel_grad.3 = f32[32,256]{1,0:T(8,128)S(1)} custom-call(s32[1]{0:T(128)} %bitcast.core_ref, bf16[32,112,256]{2,1,0:T(8,128)(2,1)S(1)} %copy-done, bf16[32,64,256]{2,1,0:T(8,128)(2,1)S(1)} %collective-permute-done.near_ref.far_ref, bf16[16,64,256]{2,1,0:T(8,128)(2,1)S(1)} %collective-permute-done.1.far_ref, ...), custom_call_target="tpu_custom_call" | custom-call | flops 853278720 | bytes 3670016 | tf_op jit(solution)/shard_map/kernel_grad/pallas_call | solution.py:484
  62.3 0.0 collective-permute-done.11
  62.3 0.9 %collective-permute-done.12 = bf16[64,256]{1,0:T(8,128)(2,1)S(1)} collective-permute-done((bf16[64,256]{1,0:T(8,128)(2,1)S(1)}, bf16[64,256]{1,0:T(8,128)(2,1)S(1)}, u32[]{:S(2)}, u32[]{:S(2)}) %collective-permute-start.12) | collective-permute-done | bytes 32800 | tf_op jit(solution)/shard_map/ppermute | solution.py:30
  63.2 1.1 %collective-permute-done.13 = bf16[64,256]{1,0:T(8,128)(2,1)S(1)} collective-permute-done((bf16[64,256]{1,0:T(8,128)(2,1)S(1)}, bf16[64,256]{1,0:T(8,128)(2,1)S(1)}, u32[]{:S(2)}, u32[]{:S(2)}) %collective-permute-start.13) | collective-permute-done | bytes 32800 | tf_op jit(solution)/shard_map/ppermute | solution.py:30
  64.3 0.3 collective-permute-start.14
  64.6 2.7 %collective-permute-start.15 = (bf16[96,256]{1,0:T(8,128)(2,1)S(1)}, bf16[96,256]{1,0:T(8,128)(2,1)S(1)}, u32[]{:S(2)}, u32[]{:S(2)}) collective-permute-start(bf16[96,256]{1,0:T(8,128)(2,1)S(1)} %pad_maximum_fusion.3), channel_id=1, source_target_pairs={{0,16},{1,17},{2,18},{3,19},{4,20},{5,21},{6,22},{7,23},{8,24},{9,... | collective-permute-start | bytes 147464 | tf_op jit(solution)/shard_map/ppermute | solution.py:30
  67.3 1.5 %collective-permute-start.16 = (bf16[96,256]{1,0:T(8,128)(2,1)S(1)}, bf16[96,256]{1,0:T(8,128)(2,1)S(1)}, u32[]{:S(2)}, u32[]{:S(2)}) collective-permute-start(bf16[96,256]{1,0:T(8,128)(2,1)S(1)} %pad_maximum_fusion.3), channel_id=1, source_target_pairs={{0,24},{1,25},{2,26},{3,27},{4,28},{5,29},{6,30},{7,31},{8,16},{9,... | collective-permute-start | bytes 147464 | tf_op jit(solution)/shard_map/ppermute | solution.py:30
  68.8 0.0 collective-permute-done.18.far_ref
  68.8 0.0 collective-permute-done.17.near_ref
  68.8 5.1 %backward.2.refs_0_ = bf16[32,112,256]{2,1,0:T(8,128)(2,1)} custom-call(s32[1]{0:T(128)} %bitcast.core_ref, f32[32,112,256]{2,1,0:T(8,128)S(1)} %get-tuple-element.94.grad_ref, bf16[32,64,256]{2,1,0:T(8,128)(2,1)S(1)} %collective-permute-done.17.near_ref, bf16[16,64,256]{2,1,0:T(8,128)(2,1)S(1)} %collective-permute-done.10.far_ref, ...), custom_call_target="tpu_custom_call" | custom-call | flops 853278720 | bytes 4587520 | tf_op jit(solution)/shard_map/backward/pallas_call | solution.py:530
  73.9 0.0 collective-permute-done.14
  73.9 0.0 collective-permute-done.15
  73.9 0.0 collective-permute-done.16
  74.0 0.6 collective-permute-start.19
  74.6 2.0 %collective-permute-start.20 = (bf16[288,256]{1,0:T(8,128)(2,1)S(1)}, bf16[288,256]{1,0:T(8,128)(2,1)S(1)}, u32[]{:S(2)}, u32[]{:S(2)}) collective-permute-start(bf16[288,256]{1,0:T(8,128)(2,1)S(1)} %pad_maximum_fusion.2), channel_id=1, source_target_pairs={{0,1},{1,0},{2,3},{3,2},{4,5},{5,4},{6,7},{7,6},{8,9},{9,8},{10,11... | collective-permute-start | bytes 442376 | tf_op jit(solution)/shard_map/ppermute | solution.py:30
  76.6 1.0 %collective-permute-start.21 = (bf16[288,256]{1,0:T(8,128)(2,1)S(1)}, bf16[288,256]{1,0:T(8,128)(2,1)S(1)}, u32[]{:S(2)}, u32[]{:S(2)}) collective-permute-start(bf16[288,256]{1,0:T(8,128)(2,1)S(1)} %pad_maximum_fusion.2), channel_id=1, source_target_pairs={{0,5},{1,4},{2,7},{3,6},{4,1},{5,0},{6,3},{7,2},{8,13},{9,12},{10,... | collective-permute-start | bytes 442376 | tf_op jit(solution)/shard_map/ppermute | solution.py:30
  77.6 5.1 %backward.3 = bf16[32,112,256]{2,1,0:T(8,128)(2,1)} custom-call(s32[1]{0:T(128)} %bitcast.core_ref, f32[32,112,256]{2,1,0:T(8,128)S(1)} %get-tuple-element.94.grad_ref, bf16[32,64,256]{2,1,0:T(8,128)(2,1)S(1)} %collective-permute-done.17.near_ref, bf16[16,64,256]{2,1,0:T(8,128)(2,1)S(1)} %collective-permute-done.18.far_ref, ...), custom_call_target="tpu_custom_call", output_to_operand_aliasing={{}: (6, {})} | custom-call | flops 853278720 | bytes 4587520 | tf_op jit(solution)/shard_map/backward/pallas_call | solution.py:530
  82.7 0.0 collective-permute-done.19
  82.7 0.8 collective-permute-done.20
  83.5 0.0 collective-permute-done.21
  83.7 0.1 collective-permute-start.22
  83.7 1.2 %copy.32 = bf16[32,112,256]{2,1,0:T(8,128)(2,1)} copy(bf16[32,112,256]{2,1,0:T(8,128)(2,1)S(1)} %get-tuple-element.153) | data formatting | bytes 3670016
  85.0 0.7 collective-permute-done.22.got_ref.tail_ref
  85.7 1.4 %finish.1 = (f32[256,1024]{1,0:T(8,128)}, f32[1024,256]{1,0:T(8,128)}, f32[31,256]{1,0:T(8,128)}) custom-call(s32[1]{0:T(128)} %bitcast.core_ref, bf16[1056,256]{1,0:T(8,128)(2,1)S(1)} %pad_maximum_fusion.1.own_ref, bf16[1056,256]{1,0:T(8,128)(2,1)S(1)} %collective-permute-done.22.got_ref.tail_ref, ...), custom_call_target="tpu_custom_call" | custom-call | tf_op jit(solution)/shard_map/finish/pallas_call | solution.py:566
  (28 shorter events, 0.4 us)
Async XLA Ops:
  0.6 8.2 %copy-start = (bf16[32,112,256]{2,1,0:T(8,128)(2,1)S(1)}, bf16[32,112,256]{2,1,0:T(8,128)(2,1)}, u32[]{:S(2)}) copy-start(bf16[32,112,256]{2,1,0:T(8,128)(2,1)} %fields_ref.5) | copy-start | bytes 5505028
  0.7 8.2 %copy-start.2 = (f32[31,256]{1,0:T(8,128)S(1)}, f32[31,256]{1,0:T(8,128)}, u32[]{:S(2)}) copy-start(f32[31,256]{1,0:T(8,128)} %kernel_ref.11) | copy-start | bytes 95236
  0.7 8.2 %copy-start.3 = (bf16[256,1024]{1,0:T(8,128)(2,1)S(1)}, bf16[256,1024]{1,0:T(8,128)(2,1)}, u32[]{:S(2)}) copy-start(bf16[256,1024]{1,0:T(8,128)(2,1)} %up_ref.5) | copy-start | bytes 1572868
  0.7 8.2 %copy-start.4 = (bf16[1024,256]{1,0:T(8,128)(2,1)S(1)}, bf16[1024,256]{1,0:T(8,128)(2,1)}, u32[]{:S(2)}) copy-start(bf16[1024,256]{1,0:T(8,128)(2,1)} %down_ref.5) | copy-start | bytes 1572868
  2.5 6.3 %collective-permute-start = (bf16[32,64,256]{2,1,0:T(8,128)(2,1)S(1)}, bf16[32,64,256]{2,1,0:T(8,128)(2,1)S(1)}, u32[]{:S(2)}, u32[]{:S(2)}) collective-permute-start(bf16[32,64,256]{2,1,0:T(8,128)(2,1)S(1)} %get-tuple-element.142), channel_id=1, source_target_pairs={{0,2},{1,3},{2,0},{3,1},{4,6},{5,7},{6,4},{7,5},{8,10},{9,11},{10,... | collective-permute-start | bytes 3145736 | tf_op jit(solution)/shard_map/ppermute | solution.py:30
  3.1 15.2 %copy-start.1 = (bf16[32,112,256]{2,1,0:T(8,128)(2,1)S(1)}, bf16[32,112,256]{2,1,0:T(8,128)(2,1)}, u32[]{:S(2)}) copy-start(bf16[32,112,256]{2,1,0:T(8,128)(2,1)} %cot_ref.9) | copy-start | bytes 5505028
  3.1 22.5 %collective-permute-start.2 = (bf16[16,64,256]{2,1,0:T(8,128)(2,1)S(1)}, bf16[16,64,256]{2,1,0:T(8,128)(2,1)S(1)}, u32[]{:S(2)}, u32[]{:S(2)}) collective-permute-start(bf16[16,64,256]{2,1,0:T(8,128)(2,1)S(1)} %slice.80), channel_id=1, source_target_pairs={{0,30},{2,4},{4,2},{6,8},{8,6},{10,12},{12,10},{14,16},{16,14},{18... | collective-permute-start | bytes 1572872 | tf_op jit(solution)/shard_map/ppermute | solution.py:40
  16.1 17.8 %collective-permute-start.1 = (bf16[16,64,256]{2,1,0:T(8,128)(2,1)S(1)}, bf16[16,64,256]{2,1,0:T(8,128)(2,1)S(1)}, u32[]{:S(2)}, u32[]{:S(2)}) collective-permute-start(bf16[16,64,256]{2,1,0:T(8,128)(2,1)S(1)} %slice.62), channel_id=1, source_target_pairs={{0,30},{2,4},{4,2},{6,8},{8,6},{10,12},{12,10},{14,16},{16,14},{18... | collective-permute-start | bytes 1572872 | tf_op jit(solution)/shard_map/ppermute | solution.py:40
  31.5 22.0 %collective-permute-start.10 = (bf16[16,64,256]{2,1,0:T(8,128)(2,1)S(1)}, bf16[16,64,256]{2,1,0:T(8,128)(2,1)S(1)}, u32[]{:S(2)}, u32[]{:S(2)}) collective-permute-start(bf16[16,64,256]{2,1,0:T(8,128)(2,1)S(1)} %get-tuple-element.105), channel_id=1, source_target_pairs={{0,30},{2,4},{4,2},{6,8},{8,6},{10,12},{12,10},{14,16},{16,14},{18... | collective-permute-start | bytes 1572872 | tf_op jit(solution)/shard_map/ppermute | solution.py:40
  40.2 1.4 %collective-permute-start.3 = (bf16[256,256]{1,0:T(8,128)(2,1)S(1)}, bf16[256,256]{1,0:T(8,128)(2,1)S(1)}, u32[]{:S(2)}, u32[]{:S(2)}) collective-permute-start(bf16[256,256]{1,0:T(8,128)(2,1)S(1)} %get-tuple-element.146), channel_id=1, source_target_pairs={{0,2},{1,3},{2,0},{3,1},{4,6},{5,7},{6,4},{7,5},{8,10},{9,11},{10,... | collective-permute-start | bytes 393224 | tf_op jit(solution)/shard_map/ppermute | solution.py:30
  40.3 1.5 %collective-permute-start.4 = (bf16[256,256]{1,0:T(8,128)(2,1)S(1)}, bf16[256,256]{1,0:T(8,128)(2,1)S(1)}, u32[]{:S(2)}, u32[]{:S(2)}) collective-permute-start(bf16[256,256]{1,0:T(8,128)(2,1)S(1)} %get-tuple-element.149), channel_id=1, source_target_pairs={{0,2},{1,3},{2,0},{3,1},{4,6},{5,7},{6,4},{7,5},{8,10},{9,11},{10,... | collective-permute-start | bytes 393224 | tf_op jit(solution)/shard_map/ppermute | solution.py:30
  40.8 1.3 %collective-permute-start.5 = (bf16[256,256]{1,0:T(8,128)(2,1)S(1)}, bf16[256,256]{1,0:T(8,128)(2,1)S(1)}, u32[]{:S(2)}, u32[]{:S(2)}) collective-permute-start(bf16[256,256]{1,0:T(8,128)(2,1)S(1)} %get-tuple-element.148), channel_id=1, source_target_pairs={{0,2},{1,3},{2,0},{3,1},{4,6},{5,7},{6,4},{7,5},{8,10},{9,11},{10,... | collective-permute-start | bytes 393224 | tf_op jit(solution)/shard_map/ppermute | solution.py:30
  40.9 1.5 %collective-permute-start.6 = (bf16[256,256]{1,0:T(8,128)(2,1)S(1)}, bf16[256,256]{1,0:T(8,128)(2,1)S(1)}, u32[]{:S(2)}, u32[]{:S(2)}) collective-permute-start(bf16[256,256]{1,0:T(8,128)(2,1)S(1)} %get-tuple-element.147), channel_id=1, source_target_pairs={{0,2},{1,3},{2,0},{3,1},{4,6},{5,7},{6,4},{7,5},{8,10},{9,11},{10,... | collective-permute-start | bytes 393224 | tf_op jit(solution)/shard_map/ppermute | solution.py:30
  41.6 27.2 %collective-permute-start.17 = (bf16[32,64,256]{2,1,0:T(8,128)(2,1)S(1)}, bf16[32,64,256]{2,1,0:T(8,128)(2,1)S(1)}, u32[]{:S(2)}, u32[]{:S(2)}) collective-permute-start(bf16[32,64,256]{2,1,0:T(8,128)(2,1)S(1)} %pad_maximum_fusion), channel_id=1, source_target_pairs={{0,2},{1,3},{2,0},{3,1},{4,6},{5,7},{6,4},{7,5},{8,10},{9,11},{10,... | collective-permute-start | bytes 3145736 | tf_op jit(solution)/shard_map/ppermute | solution.py:30
  42.5 7.9 %collective-permute-start.7 = (bf16[256,256]{1,0:T(8,128)(2,1)S(1)}, bf16[256,256]{1,0:T(8,128)(2,1)S(1)}, u32[]{:S(2)}, u32[]{:S(2)}) collective-permute-start(bf16[256,256]{1,0:T(8,128)(2,1)S(1)} %get-tuple-element.145), channel_id=1, source_target_pairs={{0,4},{1,5},{2,6},{3,7},{4,0},{5,1},{6,2},{7,3},{8,12},{9,13},{10,... | collective-permute-start | bytes 393224 | tf_op jit(solution)/shard_map/ppermute | solution.py:30
  42.6 7.8 %collective-permute-start.8 = (bf16[256,256]{1,0:T(8,128)(2,1)S(1)}, bf16[256,256]{1,0:T(8,128)(2,1)S(1)}, u32[]{:S(2)}, u32[]{:S(2)}) collective-permute-start(bf16[256,256]{1,0:T(8,128)(2,1)S(1)} %get-tuple-element.144), channel_id=1, source_target_pairs={{0,1},{1,0},{2,3},{3,2},{4,5},{5,4},{6,7},{7,6},{8,9},{9,8},{10,11... | collective-permute-start | bytes 393224 | tf_op jit(solution)/shard_map/ppermute | solution.py:30
  44.2 7.9 %collective-permute-start.9 = (bf16[256,256]{1,0:T(8,128)(2,1)S(1)}, bf16[256,256]{1,0:T(8,128)(2,1)S(1)}, u32[]{:S(2)}, u32[]{:S(2)}) collective-permute-start(bf16[256,256]{1,0:T(8,128)(2,1)S(1)} %get-tuple-element.143), channel_id=1, source_target_pairs={{0,5},{1,4},{2,7},{3,6},{4,1},{5,0},{6,3},{7,2},{8,13},{9,12},{10,... | collective-permute-start | bytes 393224 | tf_op jit(solution)/shard_map/ppermute | solution.py:30
  52.1 16.7 %collective-permute-start.18 = (bf16[16,64,256]{2,1,0:T(8,128)(2,1)S(1)}, bf16[16,64,256]{2,1,0:T(8,128)(2,1)S(1)}, u32[]{:S(2)}, u32[]{:S(2)}) collective-permute-start(bf16[16,64,256]{2,1,0:T(8,128)(2,1)S(1)} %get-tuple-element.120), channel_id=1, source_target_pairs={{0,30},{2,4},{4,2},{6,8},{8,6},{10,12},{12,10},{14,16},{16,14},{18... | collective-permute-start | bytes 1572872 | tf_op jit(solution)/shard_map/ppermute | solution.py:40
  53.5 8.8 %collective-permute-start.11 = (bf16[64,256]{1,0:T(8,128)(2,1)S(1)}, bf16[64,256]{1,0:T(8,128)(2,1)S(1)}, u32[]{:S(2)}, u32[]{:S(2)}) collective-permute-start(bf16[64,256]{1,0:T(8,128)(2,1)S(1)} %get-tuple-element.110), channel_id=1, source_target_pairs={{0,8},{1,9},{2,10},{3,11},{4,12},{5,13},{6,14},{7,15},{8,0},{9,1},... | collective-permute-start | bytes 98312 | tf_op jit(solution)/shard_map/ppermute | solution.py:30
  53.6 9.7 %collective-permute-start.12 = (bf16[64,256]{1,0:T(8,128)(2,1)S(1)}, bf16[64,256]{1,0:T(8,128)(2,1)S(1)}, u32[]{:S(2)}, u32[]{:S(2)}) collective-permute-start(bf16[64,256]{1,0:T(8,128)(2,1)S(1)} %get-tuple-element.111), channel_id=1, source_target_pairs={{0,16},{1,17},{2,18},{3,19},{4,20},{5,21},{6,22},{7,23},{8,24},{9,... | collective-permute-start | bytes 98312 | tf_op jit(solution)/shard_map/ppermute | solution.py:30
  56.0 8.3 %collective-permute-start.13 = (bf16[64,256]{1,0:T(8,128)(2,1)S(1)}, bf16[64,256]{1,0:T(8,128)(2,1)S(1)}, u32[]{:S(2)}, u32[]{:S(2)}) collective-permute-start(bf16[64,256]{1,0:T(8,128)(2,1)S(1)} %get-tuple-element.112), channel_id=1, source_target_pairs={{0,24},{1,25},{2,26},{3,27},{4,28},{5,29},{6,30},{7,31},{8,16},{9,... | collective-permute-start | bytes 98312 | tf_op jit(solution)/shard_map/ppermute | solution.py:30
  64.3 9.6 %collective-permute-start.14 = (bf16[96,256]{1,0:T(8,128)(2,1)S(1)}, bf16[96,256]{1,0:T(8,128)(2,1)S(1)}, u32[]{:S(2)}, u32[]{:S(2)}) collective-permute-start(bf16[96,256]{1,0:T(8,128)(2,1)S(1)} %pad_maximum_fusion.3), channel_id=1, source_target_pairs={{0,8},{1,9},{2,10},{3,11},{4,12},{5,13},{6,14},{7,15},{8,0},{9,1},... | collective-permute-start | bytes 147464 | tf_op jit(solution)/shard_map/ppermute | solution.py:30
  64.6 9.3 %collective-permute-start.15 = (bf16[96,256]{1,0:T(8,128)(2,1)S(1)}, bf16[96,256]{1,0:T(8,128)(2,1)S(1)}, u32[]{:S(2)}, u32[]{:S(2)}) collective-permute-start(bf16[96,256]{1,0:T(8,128)(2,1)S(1)} %pad_maximum_fusion.3), channel_id=1, source_target_pairs={{0,16},{1,17},{2,18},{3,19},{4,20},{5,21},{6,22},{7,23},{8,24},{9,... | collective-permute-start | bytes 147464 | tf_op jit(solution)/shard_map/ppermute | solution.py:30
  67.3 6.6 %collective-permute-start.16 = (bf16[96,256]{1,0:T(8,128)(2,1)S(1)}, bf16[96,256]{1,0:T(8,128)(2,1)S(1)}, u32[]{:S(2)}, u32[]{:S(2)}) collective-permute-start(bf16[96,256]{1,0:T(8,128)(2,1)S(1)} %pad_maximum_fusion.3), channel_id=1, source_target_pairs={{0,24},{1,25},{2,26},{3,27},{4,28},{5,29},{6,30},{7,31},{8,16},{9,... | collective-permute-start | bytes 147464 | tf_op jit(solution)/shard_map/ppermute | solution.py:30
  74.0 8.7 %collective-permute-start.19 = (bf16[288,256]{1,0:T(8,128)(2,1)S(1)}, bf16[288,256]{1,0:T(8,128)(2,1)S(1)}, u32[]{:S(2)}, u32[]{:S(2)}) collective-permute-start(bf16[288,256]{1,0:T(8,128)(2,1)S(1)} %pad_maximum_fusion.2), channel_id=1, source_target_pairs={{0,4},{1,5},{2,6},{3,7},{4,0},{5,1},{6,2},{7,3},{8,12},{9,13},{10,... | collective-permute-start | bytes 442376 | tf_op jit(solution)/shard_map/ppermute | solution.py:30
  74.6 8.9 %collective-permute-start.20 = (bf16[288,256]{1,0:T(8,128)(2,1)S(1)}, bf16[288,256]{1,0:T(8,128)(2,1)S(1)}, u32[]{:S(2)}, u32[]{:S(2)}) collective-permute-start(bf16[288,256]{1,0:T(8,128)(2,1)S(1)} %pad_maximum_fusion.2), channel_id=1, source_target_pairs={{0,1},{1,0},{2,3},{3,2},{4,5},{5,4},{6,7},{7,6},{8,9},{9,8},{10,11... | collective-permute-start | bytes 442376 | tf_op jit(solution)/shard_map/ppermute | solution.py:30
  76.6 7.0 %collective-permute-start.21 = (bf16[288,256]{1,0:T(8,128)(2,1)S(1)}, bf16[288,256]{1,0:T(8,128)(2,1)S(1)}, u32[]{:S(2)}, u32[]{:S(2)}) collective-permute-start(bf16[288,256]{1,0:T(8,128)(2,1)S(1)} %pad_maximum_fusion.2), channel_id=1, source_target_pairs={{0,5},{1,4},{2,7},{3,6},{4,1},{5,0},{6,3},{7,2},{8,13},{9,12},{10,... | collective-permute-start | bytes 442376 | tf_op jit(solution)/shard_map/ppermute | solution.py:30
  83.7 2.0 %collective-permute-start.22 = (bf16[1056,256]{1,0:T(8,128)(2,1)S(1)}, bf16[1056,256]{1,0:T(8,128)(2,1)S(1)}, u32[]{:S(2)}, u32[]{:S(2)}) collective-permute-start(bf16[1056,256]{1,0:T(8,128)(2,1)S(1)} %pad_maximum_fusion.1.own_ref), channel_id=1, source_target_pairs={{0,2},{1,3},{2,0},{3,1},{4,6},{5,7},{6,4},{7,5},{8,10},{9,11},{10,... | collective-permute-start | bytes 1622024 | tf_op jit(solution)/shard_map/ppermute | solution.py:30

commit v7 on v6

--- a/solution.py
+++ b/solution.py
@@ -9,7 +9,7 @@
 from jax.sharding import PartitionSpec as P
 
 KERNEL_SPACING = 4
-BLOCK = 4
+BLOCK = 8
 NEAR_BLOCK = 32
 FAR_BLOCK = 16
 AXES = ("lon", "lat")

time: 87.2 us -> 87.3 us (level)
  no operation moved by 1% of the time
where the time goes in v7:
time: 87.3 us; the launch traced here: 87.1 us
  Pallas kernels  47 us (54%)
  starting transfers between devices  29.5 us (34%)
  waiting for transfers between devices  5.85 us (7%)
  other arithmetic  2.21 us (3%)
  local copies, waits for them, and re-layouts  1.57 us (2%)
  between operations  0.99 us (1%)
    pallas_call x3, Pallas kernels, forward(): pl.pallas_call(functools.partial(forward_kernel, reach, not carried, last...  19.4 us
    ppermute x19, starting transfers between devices, xor_permute(): return lax.ppermute(value, AXES, pairs)  17.8 us
    ppermute x4, starting transfers between devices, off_chip(): return lax.ppermute(value, 'lon', pairs)  11.7 us
    pallas_call x2, Pallas kernels, backward(): pl.pallas_call(functools.partial(backward_kernel, start), grid=(count //...  10.3 us
    pallas_call x2, Pallas kernels, kernel_grad(): pl.pallas_call(functools.partial(kernel_grad_kernel, start), in_specs=[pl...  8.69 us
    pallas_call x1, Pallas kernels, inner(): pl.pallas_call(inner_kernel, in_specs=[pl.BlockSpec(memory_space=pltpu.SM...  7.21 us
    ppermute x19, waiting for transfers between devices, xor_permute(): return lax.ppermute(value, AXES, pairs)  5.84 us
    select_n x1, other arithmetic, per_device(): jnp.where(even, to_left, to_right)  1.84 us
  transfers between devices with their start and end apart: 23, of which 8 were waited for; matrix products, arithmetic and copies ran while one was open for 2% of the time, Pallas kernels for 52%

profile of v7, /device:TPU:0, one launch (start us, length us, event | category | flops | bytes accessed | tf_op | source)
XLA Modules:
  0.0 87.1 jit_solution(16434256703455164421)
XLA Ops:
  0.6 0.0 copy-start
  0.7 0.0 copy-start.2
  0.7 1.8 %broadcast_select_fusion = (bf16[32,64,256]{2,1,0:T(8,128)(2,1)S(1)}, bf16[32,64,256]{2,1,0:T(8,128)(2,1)S(1)}) fusion(pred[]{:T(512)S(6)} %eq.3, bf16[32,112,256]{2,1,0:T(8,128)(2,1)} %fields_ref.5), kind=kLoop, calls=%fused_computation.2 | loop fusion | flops 1048576 | bytes 4194305 | tf_op jit(solution)/shard_map/jit(_where)/select_n | solution.py:613
  2.5 0.5 collective-permute-start
  3.1 0.0 copy-start.1
  3.1 5.7 %collective-permute-start.2 = (bf16[16,64,256]{2,1,0:T(8,128)(2,1)S(1)}, bf16[16,64,256]{2,1,0:T(8,128)(2,1)S(1)}, u32[]{:S(2)}, u32[]{:S(2)}) collective-permute-start(bf16[16,64,256]{2,1,0:T(8,128)(2,1)S(1)} %slice.80), channel_id=1, source_target_pairs={{0,30},{2,4},{4,2},{6,8},{8,6},{10,12},{12,10},{14,16},{16,14},{18... | collective-permute-start | bytes 1572872 | tf_op jit(solution)/shard_map/ppermute | solution.py:40
  8.8 0.0 collective-permute-done.near_ref.far_ref
  8.8 0.0 copy-done.2
  8.8 7.2 %inner.1 = (f32[32,112,256]{2,1,0:T(8,128)S(1)}, bf16[1024,256]{1,0:T(8,128)(2,1)S(1)}, bf16[256,1024]{1,0:T(8,128)(2,1)S(1)}) custom-call(s32[1]{0:T(128)} %bitcast.core_ref, bf16[32,112,256]{2,1,0:T(8,128)(2,1)S(1)} %copy-done, bf16[32,64,256]{2,1,0:T(8,128)(2,1)S(1)} %collective-permute-done.near_ref.far_ref, f32[31,256]{1,0:T(8,128)S(1)} %copy-done.2, ...), custom_call_target="tpu_custom_call" | custom-call | flops 7395082240 | bytes 5505024 | tf_op jit(solution)/shard_map/inner/pallas_call | solution.py:249
  16.1 2.2 %collective-permute-start.1 = (bf16[16,64,256]{2,1,0:T(8,128)(2,1)S(1)}, bf16[16,64,256]{2,1,0:T(8,128)(2,1)S(1)}, u32[]{:S(2)}, u32[]{:S(2)}) collective-permute-start(bf16[16,64,256]{2,1,0:T(8,128)(2,1)S(1)} %slice.62), channel_id=1, source_target_pairs={{0,30},{2,4},{4,2},{6,8},{8,6},{10,12},{12,10},{14,16},{16,14},{18... | collective-permute-start | bytes 1572872 | tf_op jit(solution)/shard_map/ppermute | solution.py:40
  18.3 7.3 %forward.3 = (bf16[32,112,256]{2,1,0:T(8,128)(2,1)S(1)}, f32[32,112,256]{2,1,0:T(8,128)S(1)}, f32[4,256,256]{2,1,0:T(8,128)S(1)}, f32[256,1024]{1,0:T(8,128)S(1)}) custom-call(s32[1]{0:T(128)} %bitcast.core_ref, f32[32,112,256]{2,1,0:T(8,128)S(1)} %get-tuple-element.75.inner_ref, bf16[32,64,256]{2,1,0:T(8,128)(2,1)S(1)} %collective-permute-done.near_ref.far_ref, ...), custom_call_target="tpu_custom_call" | custom-call | flops 11274289152 | bytes 4718592 | tf_op jit(solution)/shard_map/forward/pallas_call | solution.py:407
  25.6 0.0 collective-permute-done.2.far_ref
  25.6 5.9 %forward.4 = (bf16[32,112,256]{2,1,0:T(8,128)(2,1)S(1)}, f32[32,112,256]{2,1,0:T(8,128)S(1)}, f32[4,256,256]{2,1,0:T(8,128)S(1)}, f32[256,1024]{1,0:T(8,128)S(1)...) custom-call(s32[1]{0:T(128)} %bitcast.core_ref, ...), custom_call_target="tpu_custom_call", output_to_operand_aliasing={{0}: (10, {}), {1}: (11, {}), {2}: (12, {}), {3}: (13, {})} | custom-call | flops 7516192768 | bytes 3145728 | tf_op jit(solution)/shard_map/forward/pallas_call | solution.py:407
  31.5 2.4 %collective-permute-start.10 = (bf16[16,64,256]{2,1,0:T(8,128)(2,1)S(1)}, bf16[16,64,256]{2,1,0:T(8,128)(2,1)S(1)}, u32[]{:S(2)}, u32[]{:S(2)}) collective-permute-start(bf16[16,64,256]{2,1,0:T(8,128)(2,1)S(1)} %get-tuple-element.105), channel_id=1, source_target_pairs={{0,30},{2,4},{4,2},{6,8},{8,6},{10,12},{12,10},{14,16},{16,14},{18... | collective-permute-start | bytes 1572872 | tf_op jit(solution)/shard_map/ppermute | solution.py:40
  33.9 0.0 collective-permute-done.1.far_ref
  33.9 6.3 %forward.5 = (bf16[32,112,256]{2,1,0:T(8,128)(2,1)S(1)}, f32[32,112,256]{2,1,0:T(8,128)S(1)}, f32[1024,256]{1,0:T(8,128)S(1)}, bf16[1024,256]{1,0:T(8,128)(2,1)S...) custom-call(s32[1]{0:T(128)} %bitcast.core_ref, ...), custom_call_target="tpu_custom_call", output_to_operand_aliasing={{0}: (10, {}), {1}: (11, {})} | custom-call | flops 7516192768 | bytes 3145728 | tf_op jit(solution)/shard_map/forward/pallas_call | solution.py:407
  40.2 0.1 collective-permute-start.3
  40.3 0.5 collective-permute-start.4
  40.8 0.1 collective-permute-start.5
  40.9 0.4 collective-permute-start.6
  41.3 0.1 pad_maximum_fusion
  41.4 0.2 collective-permute-done.3
  41.6 0.1 collective-permute-start.17
  41.8 0.0 collective-permute-done.4
  41.8 0.3 collective-permute-done.5
  42.1 0.2 collective-permute-done.6
  42.3 0.1 convert_add_fusion
  42.5 0.1 collective-permute-start.7
  42.6 1.6 %collective-permute-start.8 = (bf16[256,256]{1,0:T(8,128)(2,1)S(1)}, bf16[256,256]{1,0:T(8,128)(2,1)S(1)}, u32[]{:S(2)}, u32[]{:S(2)}) collective-permute-start(bf16[256,256]{1,0:T(8,128)(2,1)S(1)} %get-tuple-element.144), channel_id=1, source_target_pairs={{0,1},{1,0},{2,3},{3,2},{4,5},{5,4},{6,7},{7,6},{8,9},{9,8},{10,11... | collective-permute-start | bytes 393224 | tf_op jit(solution)/shard_map/ppermute | solution.py:30
  44.2 1.9 %collective-permute-start.9 = (bf16[256,256]{1,0:T(8,128)(2,1)S(1)}, bf16[256,256]{1,0:T(8,128)(2,1)S(1)}, u32[]{:S(2)}, u32[]{:S(2)}) collective-permute-start(bf16[256,256]{1,0:T(8,128)(2,1)S(1)} %get-tuple-element.143), channel_id=1, source_target_pairs={{0,5},{1,4},{2,7},{3,6},{4,1},{5,0},{6,3},{7,2},{8,13},{9,12},{10,... | collective-permute-start | bytes 393224 | tf_op jit(solution)/shard_map/ppermute | solution.py:30
  46.1 4.3 %kernel_grad.2.given_ref = f32[32,256]{1,0:T(8,128)S(1)} custom-call(s32[1]{0:T(128)} %bitcast.core_ref, bf16[32,112,256]{2,1,0:T(8,128)(2,1)S(1)} %copy-done, bf16[32,64,256]{2,1,0:T(8,128)(2,1)S(1)} %collective-permute-done.near_ref.far_ref, bf16[16,64,256]{2,1,0:T(8,128)(2,1)S(1)} %collective-permute-done.2.far_ref, ...), custom_call_target="tpu_custom_call" | custom-call | flops 853278720 | bytes 3670016 | tf_op jit(solution)/shard_map/kernel_grad/pallas_call | solution.py:484
  50.4 0.0 collective-permute-done.7
  50.4 0.0 collective-permute-done.8
  50.4 1.6 %collective-permute-done.9 = bf16[256,256]{1,0:T(8,128)(2,1)S(1)} collective-permute-done((bf16[256,256]{1,0:T(8,128)(2,1)S(1)}, bf16[256,256]{1,0:T(8,128)(2,1)S(1)}, u32[]{:S(2)}, u32[]{:S(2)}) %collective-permute-start.9) | collective-permute-done | bytes 131104 | tf_op jit(solution)/shard_map/ppermute | solution.py:30
  52.0 0.1 fusion.1
  52.1 1.4 %collective-permute-start.18 = (bf16[16,64,256]{2,1,0:T(8,128)(2,1)S(1)}, bf16[16,64,256]{2,1,0:T(8,128)(2,1)S(1)}, u32[]{:S(2)}, u32[]{:S(2)}) collective-permute-start(bf16[16,64,256]{2,1,0:T(8,128)(2,1)S(1)} %get-tuple-element.120), channel_id=1, source_target_pairs={{0,30},{2,4},{4,2},{6,8},{8,6},{10,12},{12,10},{14,16},{16,14},{18... | collective-permute-start | bytes 1572872 | tf_op jit(solution)/shard_map/ppermute | solution.py:40
  53.5 0.0 collective-permute-done.10.far_ref
  53.5 0.1 collective-permute-start.11
  53.6 2.4 %collective-permute-start.12 = (bf16[64,256]{1,0:T(8,128)(2,1)S(1)}, bf16[64,256]{1,0:T(8,128)(2,1)S(1)}, u32[]{:S(2)}, u32[]{:S(2)}) collective-permute-start(bf16[64,256]{1,0:T(8,128)(2,1)S(1)} %get-tuple-element.111), channel_id=1, source_target_pairs={{0,16},{1,17},{2,18},{3,19},{4,20},{5,21},{6,22},{7,23},{8,24},{9,... | collective-permute-start | bytes 98312 | tf_op jit(solution)/shard_map/ppermute | solution.py:30
  56.0 2.0 %collective-permute-start.13 = (bf16[64,256]{1,0:T(8,128)(2,1)S(1)}, bf16[64,256]{1,0:T(8,128)(2,1)S(1)}, u32[]{:S(2)}, u32[]{:S(2)}) collective-permute-start(bf16[64,256]{1,0:T(8,128)(2,1)S(1)} %get-tuple-element.112), channel_id=1, source_target_pairs={{0,24},{1,25},{2,26},{3,27},{4,28},{5,29},{6,30},{7,31},{8,16},{9,... | collective-permute-start | bytes 98312 | tf_op jit(solution)/shard_map/ppermute | solution.py:30
  57.9 4.3 %kernel_grad.3 = f32[32,256]{1,0:T(8,128)S(1)} custom-call(s32[1]{0:T(128)} %bitcast.core_ref, bf16[32,112,256]{2,1,0:T(8,128)(2,1)S(1)} %copy-done, bf16[32,64,256]{2,1,0:T(8,128)(2,1)S(1)} %collective-permute-done.near_ref.far_ref, bf16[16,64,256]{2,1,0:T(8,128)(2,1)S(1)} %collective-permute-done.1.far_ref, ...), custom_call_target="tpu_custom_call" | custom-call | flops 853278720 | bytes 3670016 | tf_op jit(solution)/shard_map/kernel_grad/pallas_call | solution.py:484
  62.3 0.0 collective-permute-done.11
  62.3 0.9 %collective-permute-done.12 = bf16[64,256]{1,0:T(8,128)(2,1)S(1)} collective-permute-done((bf16[64,256]{1,0:T(8,128)(2,1)S(1)}, bf16[64,256]{1,0:T(8,128)(2,1)S(1)}, u32[]{:S(2)}, u32[]{:S(2)}) %collective-permute-start.12) | collective-permute-done | bytes 32800 | tf_op jit(solution)/shard_map/ppermute | solution.py:30
  63.2 1.1 %collective-permute-done.13 = bf16[64,256]{1,0:T(8,128)(2,1)S(1)} collective-permute-done((bf16[64,256]{1,0:T(8,128)(2,1)S(1)}, bf16[64,256]{1,0:T(8,128)(2,1)S(1)}, u32[]{:S(2)}, u32[]{:S(2)}) %collective-permute-start.13) | collective-permute-done | bytes 32800 | tf_op jit(solution)/shard_map/ppermute | solution.py:30
  64.3 0.3 collective-permute-start.14
  64.6 2.7 %collective-permute-start.15 = (bf16[96,256]{1,0:T(8,128)(2,1)S(1)}, bf16[96,256]{1,0:T(8,128)(2,1)S(1)}, u32[]{:S(2)}, u32[]{:S(2)}) collective-permute-start(bf16[96,256]{1,0:T(8,128)(2,1)S(1)} %pad_maximum_fusion.3), channel_id=1, source_target_pairs={{0,16},{1,17},{2,18},{3,19},{4,20},{5,21},{6,22},{7,23},{8,24},{9,... | collective-permute-start | bytes 147464 | tf_op jit(solution)/shard_map/ppermute | solution.py:30
  67.3 1.5 %collective-permute-start.16 = (bf16[96,256]{1,0:T(8,128)(2,1)S(1)}, bf16[96,256]{1,0:T(8,128)(2,1)S(1)}, u32[]{:S(2)}, u32[]{:S(2)}) collective-permute-start(bf16[96,256]{1,0:T(8,128)(2,1)S(1)} %pad_maximum_fusion.3), channel_id=1, source_target_pairs={{0,24},{1,25},{2,26},{3,27},{4,28},{5,29},{6,30},{7,31},{8,16},{9,... | collective-permute-start | bytes 147464 | tf_op jit(solution)/shard_map/ppermute | solution.py:30
  68.8 0.0 collective-permute-done.18.far_ref
  68.8 0.0 collective-permute-done.17.near_ref
  68.8 5.1 %backward.2.refs_0_ = bf16[32,112,256]{2,1,0:T(8,128)(2,1)} custom-call(s32[1]{0:T(128)} %bitcast.core_ref, f32[32,112,256]{2,1,0:T(8,128)S(1)} %get-tuple-element.94.grad_ref, bf16[32,64,256]{2,1,0:T(8,128)(2,1)S(1)} %collective-permute-done.17.near_ref, bf16[16,64,256]{2,1,0:T(8,128)(2,1)S(1)} %collective-permute-done.10.far_ref, ...), custom_call_target="tpu_custom_call" | custom-call | flops 853278720 | bytes 4587520 | tf_op jit(solution)/shard_map/backward/pallas_call | solution.py:530
  73.9 0.0 collective-permute-done.14
  73.9 0.0 collective-permute-done.15
  73.9 0.0 collective-permute-done.16
  74.0 0.6 collective-permute-start.19
  74.6 2.0 %collective-permute-start.20 = (bf16[288,256]{1,0:T(8,128)(2,1)S(1)}, bf16[288,256]{1,0:T(8,128)(2,1)S(1)}, u32[]{:S(2)}, u32[]{:S(2)}) collective-permute-start(bf16[288,256]{1,0:T(8,128)(2,1)S(1)} %pad_maximum_fusion.2), channel_id=1, source_target_pairs={{0,1},{1,0},{2,3},{3,2},{4,5},{5,4},{6,7},{7,6},{8,9},{9,8},{10,11... | collective-permute-start | bytes 442376 | tf_op jit(solution)/shard_map/ppermute | solution.py:30
  76.6 1.0 %collective-permute-start.21 = (bf16[288,256]{1,0:T(8,128)(2,1)S(1)}, bf16[288,256]{1,0:T(8,128)(2,1)S(1)}, u32[]{:S(2)}, u32[]{:S(2)}) collective-permute-start(bf16[288,256]{1,0:T(8,128)(2,1)S(1)} %pad_maximum_fusion.2), channel_id=1, source_target_pairs={{0,5},{1,4},{2,7},{3,6},{4,1},{5,0},{6,3},{7,2},{8,13},{9,12},{10,... | collective-permute-start | bytes 442376 | tf_op jit(solution)/shard_map/ppermute | solution.py:30
  77.6 5.1 %backward.3 = bf16[32,112,256]{2,1,0:T(8,128)(2,1)} custom-call(s32[1]{0:T(128)} %bitcast.core_ref, f32[32,112,256]{2,1,0:T(8,128)S(1)} %get-tuple-element.94.grad_ref, bf16[32,64,256]{2,1,0:T(8,128)(2,1)S(1)} %collective-permute-done.17.near_ref, bf16[16,64,256]{2,1,0:T(8,128)(2,1)S(1)} %collective-permute-done.18.far_ref, ...), custom_call_target="tpu_custom_call", output_to_operand_aliasing={{}: (6, {})} | custom-call | flops 853278720 | bytes 4587520 | tf_op jit(solution)/shard_map/backward/pallas_call | solution.py:530
  82.8 0.0 collective-permute-done.19
  82.8 0.7 collective-permute-done.20
  83.6 0.0 collective-permute-done.21
  83.7 0.1 collective-permute-start.22
  83.8 1.2 %copy.32 = bf16[32,112,256]{2,1,0:T(8,128)(2,1)} copy(bf16[32,112,256]{2,1,0:T(8,128)(2,1)S(1)} %get-tuple-element.153) | data formatting | bytes 3670016
  85.0 0.7 collective-permute-done.22.got_ref.tail_ref
  85.7 1.4 %finish.1 = (f32[256,1024]{1,0:T(8,128)}, f32[1024,256]{1,0:T(8,128)}, f32[31,256]{1,0:T(8,128)}) custom-call(s32[1]{0:T(128)} %bitcast.core_ref, bf16[1056,256]{1,0:T(8,128)(2,1)S(1)} %pad_maximum_fusion.1.own_ref, bf16[1056,256]{1,0:T(8,128)(2,1)S(1)} %collective-permute-done.22.got_ref.tail_ref, ...), custom_call_target="tpu_custom_call" | custom-call | tf_op jit(solution)/shard_map/finish/pallas_call | solution.py:566
  (28 shorter events, 0.4 us)
Async XLA Ops:
  0.6 8.2 %copy-start = (bf16[32,112,256]{2,1,0:T(8,128)(2,1)S(1)}, bf16[32,112,256]{2,1,0:T(8,128)(2,1)}, u32[]{:S(2)}) copy-start(bf16[32,112,256]{2,1,0:T(8,128)(2,1)} %fields_ref.5) | copy-start | bytes 5505028
  0.7 8.2 %copy-start.2 = (f32[31,256]{1,0:T(8,128)S(1)}, f32[31,256]{1,0:T(8,128)}, u32[]{:S(2)}) copy-start(f32[31,256]{1,0:T(8,128)} %kernel_ref.11) | copy-start | bytes 95236
  0.7 8.2 %copy-start.3 = (bf16[256,1024]{1,0:T(8,128)(2,1)S(1)}, bf16[256,1024]{1,0:T(8,128)(2,1)}, u32[]{:S(2)}) copy-start(bf16[256,1024]{1,0:T(8,128)(2,1)} %up_ref.5) | copy-start | bytes 1572868
  0.7 8.2 %copy-start.4 = (bf16[1024,256]{1,0:T(8,128)(2,1)S(1)}, bf16[1024,256]{1,0:T(8,128)(2,1)}, u32[]{:S(2)}) copy-start(bf16[1024,256]{1,0:T(8,128)(2,1)} %down_ref.5) | copy-start | bytes 1572868
  2.5 6.3 %collective-permute-start = (bf16[32,64,256]{2,1,0:T(8,128)(2,1)S(1)}, bf16[32,64,256]{2,1,0:T(8,128)(2,1)S(1)}, u32[]{:S(2)}, u32[]{:S(2)}) collective-permute-start(bf16[32,64,256]{2,1,0:T(8,128)(2,1)S(1)} %get-tuple-element.142), channel_id=1, source_target_pairs={{0,2},{1,3},{2,0},{3,1},{4,6},{5,7},{6,4},{7,5},{8,10},{9,11},{10,... | collective-permute-start | bytes 3145736 | tf_op jit(solution)/shard_map/ppermute | solution.py:30
  3.1 15.2 %copy-start.1 = (bf16[32,112,256]{2,1,0:T(8,128)(2,1)S(1)}, bf16[32,112,256]{2,1,0:T(8,128)(2,1)}, u32[]{:S(2)}) copy-start(bf16[32,112,256]{2,1,0:T(8,128)(2,1)} %cot_ref.9) | copy-start | bytes 5505028
  3.1 22.5 %collective-permute-start.2 = (bf16[16,64,256]{2,1,0:T(8,128)(2,1)S(1)}, bf16[16,64,256]{2,1,0:T(8,128)(2,1)S(1)}, u32[]{:S(2)}, u32[]{:S(2)}) collective-permute-start(bf16[16,64,256]{2,1,0:T(8,128)(2,1)S(1)} %slice.80), channel_id=1, source_target_pairs={{0,30},{2,4},{4,2},{6,8},{8,6},{10,12},{12,10},{14,16},{16,14},{18... | collective-permute-start | bytes 1572872 | tf_op jit(solution)/shard_map/ppermute | solution.py:40
  16.1 17.8 %collective-permute-start.1 = (bf16[16,64,256]{2,1,0:T(8,128)(2,1)S(1)}, bf16[16,64,256]{2,1,0:T(8,128)(2,1)S(1)}, u32[]{:S(2)}, u32[]{:S(2)}) collective-permute-start(bf16[16,64,256]{2,1,0:T(8,128)(2,1)S(1)} %slice.62), channel_id=1, source_target_pairs={{0,30},{2,4},{4,2},{6,8},{8,6},{10,12},{12,10},{14,16},{16,14},{18... | collective-permute-start | bytes 1572872 | tf_op jit(solution)/shard_map/ppermute | solution.py:40
  31.5 22.0 %collective-permute-start.10 = (bf16[16,64,256]{2,1,0:T(8,128)(2,1)S(1)}, bf16[16,64,256]{2,1,0:T(8,128)(2,1)S(1)}, u32[]{:S(2)}, u32[]{:S(2)}) collective-permute-start(bf16[16,64,256]{2,1,0:T(8,128)(2,1)S(1)} %get-tuple-element.105), channel_id=1, source_target_pairs={{0,30},{2,4},{4,2},{6,8},{8,6},{10,12},{12,10},{14,16},{16,14},{18... | collective-permute-start | bytes 1572872 | tf_op jit(solution)/shard_map/ppermute | solution.py:40
  40.2 1.4 %collective-permute-start.3 = (bf16[256,256]{1,0:T(8,128)(2,1)S(1)}, bf16[256,256]{1,0:T(8,128)(2,1)S(1)}, u32[]{:S(2)}, u32[]{:S(2)}) collective-permute-start(bf16[256,256]{1,0:T(8,128)(2,1)S(1)} %get-tuple-element.146), channel_id=1, source_target_pairs={{0,2},{1,3},{2,0},{3,1},{4,6},{5,7},{6,4},{7,5},{8,10},{9,11},{10,... | collective-permute-start | bytes 393224 | tf_op jit(solution)/shard_map/ppermute | solution.py:30
  40.3 1.5 %collective-permute-start.4 = (bf16[256,256]{1,0:T(8,128)(2,1)S(1)}, bf16[256,256]{1,0:T(8,128)(2,1)S(1)}, u32[]{:S(2)}, u32[]{:S(2)}) collective-permute-start(bf16[256,256]{1,0:T(8,128)(2,1)S(1)} %get-tuple-element.149), channel_id=1, source_target_pairs={{0,2},{1,3},{2,0},{3,1},{4,6},{5,7},{6,4},{7,5},{8,10},{9,11},{10,... | collective-permute-start | bytes 393224 | tf_op jit(solution)/shard_map/ppermute | solution.py:30
  40.8 1.3 %collective-permute-start.5 = (bf16[256,256]{1,0:T(8,128)(2,1)S(1)}, bf16[256,256]{1,0:T(8,128)(2,1)S(1)}, u32[]{:S(2)}, u32[]{:S(2)}) collective-permute-start(bf16[256,256]{1,0:T(8,128)(2,1)S(1)} %get-tuple-element.148), channel_id=1, source_target_pairs={{0,2},{1,3},{2,0},{3,1},{4,6},{5,7},{6,4},{7,5},{8,10},{9,11},{10,... | collective-permute-start | bytes 393224 | tf_op jit(solution)/shard_map/ppermute | solution.py:30
  40.9 1.5 %collective-permute-start.6 = (bf16[256,256]{1,0:T(8,128)(2,1)S(1)}, bf16[256,256]{1,0:T(8,128)(2,1)S(1)}, u32[]{:S(2)}, u32[]{:S(2)}) collective-permute-start(bf16[256,256]{1,0:T(8,128)(2,1)S(1)} %get-tuple-element.147), channel_id=1, source_target_pairs={{0,2},{1,3},{2,0},{3,1},{4,6},{5,7},{6,4},{7,5},{8,10},{9,11},{10,... | collective-permute-start | bytes 393224 | tf_op jit(solution)/shard_map/ppermute | solution.py:30
  41.6 27.2 %collective-permute-start.17 = (bf16[32,64,256]{2,1,0:T(8,128)(2,1)S(1)}, bf16[32,64,256]{2,1,0:T(8,128)(2,1)S(1)}, u32[]{:S(2)}, u32[]{:S(2)}) collective-permute-start(bf16[32,64,256]{2,1,0:T(8,128)(2,1)S(1)} %pad_maximum_fusion), channel_id=1, source_target_pairs={{0,2},{1,3},{2,0},{3,1},{4,6},{5,7},{6,4},{7,5},{8,10},{9,11},{10,... | collective-permute-start | bytes 3145736 | tf_op jit(solution)/shard_map/ppermute | solution.py:30
  42.5 7.9 %collective-permute-start.7 = (bf16[256,256]{1,0:T(8,128)(2,1)S(1)}, bf16[256,256]{1,0:T(8,128)(2,1)S(1)}, u32[]{:S(2)}, u32[]{:S(2)}) collective-permute-start(bf16[256,256]{1,0:T(8,128)(2,1)S(1)} %get-tuple-element.145), channel_id=1, source_target_pairs={{0,4},{1,5},{2,6},{3,7},{4,0},{5,1},{6,2},{7,3},{8,12},{9,13},{10,... | collective-permute-start | bytes 393224 | tf_op jit(solution)/shard_map/ppermute | solution.py:30
  42.6 7.8 %collective-permute-start.8 = (bf16[256,256]{1,0:T(8,128)(2,1)S(1)}, bf16[256,256]{1,0:T(8,128)(2,1)S(1)}, u32[]{:S(2)}, u32[]{:S(2)}) collective-permute-start(bf16[256,256]{1,0:T(8,128)(2,1)S(1)} %get-tuple-element.144), channel_id=1, source_target_pairs={{0,1},{1,0},{2,3},{3,2},{4,5},{5,4},{6,7},{7,6},{8,9},{9,8},{10,11... | collective-permute-start | bytes 393224 | tf_op jit(solution)/shard_map/ppermute | solution.py:30
  44.2 7.9 %collective-permute-start.9 = (bf16[256,256]{1,0:T(8,128)(2,1)S(1)}, bf16[256,256]{1,0:T(8,128)(2,1)S(1)}, u32[]{:S(2)}, u32[]{:S(2)}) collective-permute-start(bf16[256,256]{1,0:T(8,128)(2,1)S(1)} %get-tuple-element.143), channel_id=1, source_target_pairs={{0,5},{1,4},{2,7},{3,6},{4,1},{5,0},{6,3},{7,2},{8,13},{9,12},{10,... | collective-permute-start | bytes 393224 | tf_op jit(solution)/shard_map/ppermute | solution.py:30
  52.1 16.7 %collective-permute-start.18 = (bf16[16,64,256]{2,1,0:T(8,128)(2,1)S(1)}, bf16[16,64,256]{2,1,0:T(8,128)(2,1)S(1)}, u32[]{:S(2)}, u32[]{:S(2)}) collective-permute-start(bf16[16,64,256]{2,1,0:T(8,128)(2,1)S(1)} %get-tuple-element.120), channel_id=1, source_target_pairs={{0,30},{2,4},{4,2},{6,8},{8,6},{10,12},{12,10},{14,16},{16,14},{18... | collective-permute-start | bytes 1572872 | tf_op jit(solution)/shard_map/ppermute | solution.py:40
  53.5 8.8 %collective-permute-start.11 = (bf16[64,256]{1,0:T(8,128)(2,1)S(1)}, bf16[64,256]{1,0:T(8,128)(2,1)S(1)}, u32[]{:S(2)}, u32[]{:S(2)}) collective-permute-start(bf16[64,256]{1,0:T(8,128)(2,1)S(1)} %get-tuple-element.110), channel_id=1, source_target_pairs={{0,8},{1,9},{2,10},{3,11},{4,12},{5,13},{6,14},{7,15},{8,0},{9,1},... | collective-permute-start | bytes 98312 | tf_op jit(solution)/shard_map/ppermute | solution.py:30
  53.6 9.7 %collective-permute-start.12 = (bf16[64,256]{1,0:T(8,128)(2,1)S(1)}, bf16[64,256]{1,0:T(8,128)(2,1)S(1)}, u32[]{:S(2)}, u32[]{:S(2)}) collective-permute-start(bf16[64,256]{1,0:T(8,128)(2,1)S(1)} %get-tuple-element.111), channel_id=1, source_target_pairs={{0,16},{1,17},{2,18},{3,19},{4,20},{5,21},{6,22},{7,23},{8,24},{9,... | collective-permute-start | bytes 98312 | tf_op jit(solution)/shard_map/ppermute | solution.py:30
  56.0 8.3 %collective-permute-start.13 = (bf16[64,256]{1,0:T(8,128)(2,1)S(1)}, bf16[64,256]{1,0:T(8,128)(2,1)S(1)}, u32[]{:S(2)}, u32[]{:S(2)}) collective-permute-start(bf16[64,256]{1,0:T(8,128)(2,1)S(1)} %get-tuple-element.112), channel_id=1, source_target_pairs={{0,24},{1,25},{2,26},{3,27},{4,28},{5,29},{6,30},{7,31},{8,16},{9,... | collective-permute-start | bytes 98312 | tf_op jit(solution)/shard_map/ppermute | solution.py:30
  64.3 9.6 %collective-permute-start.14 = (bf16[96,256]{1,0:T(8,128)(2,1)S(1)}, bf16[96,256]{1,0:T(8,128)(2,1)S(1)}, u32[]{:S(2)}, u32[]{:S(2)}) collective-permute-start(bf16[96,256]{1,0:T(8,128)(2,1)S(1)} %pad_maximum_fusion.3), channel_id=1, source_target_pairs={{0,8},{1,9},{2,10},{3,11},{4,12},{5,13},{6,14},{7,15},{8,0},{9,1},... | collective-permute-start | bytes 147464 | tf_op jit(solution)/shard_map/ppermute | solution.py:30
  64.6 9.3 %collective-permute-start.15 = (bf16[96,256]{1,0:T(8,128)(2,1)S(1)}, bf16[96,256]{1,0:T(8,128)(2,1)S(1)}, u32[]{:S(2)}, u32[]{:S(2)}) collective-permute-start(bf16[96,256]{1,0:T(8,128)(2,1)S(1)} %pad_maximum_fusion.3), channel_id=1, source_target_pairs={{0,16},{1,17},{2,18},{3,19},{4,20},{5,21},{6,22},{7,23},{8,24},{9,... | collective-permute-start | bytes 147464 | tf_op jit(solution)/shard_map/ppermute | solution.py:30
  67.3 6.6 %collective-permute-start.16 = (bf16[96,256]{1,0:T(8,128)(2,1)S(1)}, bf16[96,256]{1,0:T(8,128)(2,1)S(1)}, u32[]{:S(2)}, u32[]{:S(2)}) collective-permute-start(bf16[96,256]{1,0:T(8,128)(2,1)S(1)} %pad_maximum_fusion.3), channel_id=1, source_target_pairs={{0,24},{1,25},{2,26},{3,27},{4,28},{5,29},{6,30},{7,31},{8,16},{9,... | collective-permute-start | bytes 147464 | tf_op jit(solution)/shard_map/ppermute | solution.py:30
  74.0 8.8 %collective-permute-start.19 = (bf16[288,256]{1,0:T(8,128)(2,1)S(1)}, bf16[288,256]{1,0:T(8,128)(2,1)S(1)}, u32[]{:S(2)}, u32[]{:S(2)}) collective-permute-start(bf16[288,256]{1,0:T(8,128)(2,1)S(1)} %pad_maximum_fusion.2), channel_id=1, source_target_pairs={{0,4},{1,5},{2,6},{3,7},{4,0},{5,1},{6,2},{7,3},{8,12},{9,13},{10,... | collective-permute-start | bytes 442376 | tf_op jit(solution)/shard_map/ppermute | solution.py:30
  74.6 8.9 %collective-permute-start.20 = (bf16[288,256]{1,0:T(8,128)(2,1)S(1)}, bf16[288,256]{1,0:T(8,128)(2,1)S(1)}, u32[]{:S(2)}, u32[]{:S(2)}) collective-permute-start(bf16[288,256]{1,0:T(8,128)(2,1)S(1)} %pad_maximum_fusion.2), channel_id=1, source_target_pairs={{0,1},{1,0},{2,3},{3,2},{4,5},{5,4},{6,7},{7,6},{8,9},{9,8},{10,11... | collective-permute-start | bytes 442376 | tf_op jit(solution)/shard_map/ppermute | solution.py:30
  76.6 7.0 %collective-permute-start.21 = (bf16[288,256]{1,0:T(8,128)(2,1)S(1)}, bf16[288,256]{1,0:T(8,128)(2,1)S(1)}, u32[]{:S(2)}, u32[]{:S(2)}) collective-permute-start(bf16[288,256]{1,0:T(8,128)(2,1)S(1)} %pad_maximum_fusion.2), channel_id=1, source_target_pairs={{0,5},{1,4},{2,7},{3,6},{4,1},{5,0},{6,3},{7,2},{8,13},{9,12},{10,... | collective-permute-start | bytes 442376 | tf_op jit(solution)/shard_map/ppermute | solution.py:30
  83.7 2.0 %collective-permute-start.22 = (bf16[1056,256]{1,0:T(8,128)(2,1)S(1)}, bf16[1056,256]{1,0:T(8,128)(2,1)S(1)}, u32[]{:S(2)}, u32[]{:S(2)}) collective-permute-start(bf16[1056,256]{1,0:T(8,128)(2,1)S(1)} %pad_maximum_fusion.1.own_ref), channel_id=1, source_target_pairs={{0,2},{1,3},{2,0},{3,1},{4,6},{5,7},{6,4},{7,5},{8,10},{9,11},{10,... | collective-permute-start | bytes 1622024 | tf_op jit(solution)/shard_map/ppermute | solution.py:30
